TPU v7x, 128 devices: a whole 4x4x4 slice. The times are simulated.
128 devices in a mesh: src: 16 (over y_hi, z, core), tgt: 8 (over y_lo, x).
Axes of the slice: x: 4, y: 4 (y_hi: 2, y_lo: 2; y = y_hi * 2 + y_lo), z: 4, core: 2. Of those that a mesh axis runs over, the one named last changes fastest.
Arguments:
- sources: float32 [64, 128, 16384], P(None, None, ('src', 'tgt')), may hold values from -6 to 6
- source_interp: float32 [128, 32, 16384], P(None, None, ('src', 'tgt')), may hold values from -0.5 to 0.5
- target_interp: float32 [128, 32, 16384], P(None, None, ('src', 'tgt')), may hold values from -1 to 1
- transfer: float32 [9, 32, 64, 16384], P(None, None, None, ('src', 'tgt')), may hold values from -0.75 to 0.75
Outputs:
- targets: float32 [64, 128, 16384], P(None, None, ('src', 'tgt'))
All inputs are finite; a program needn't handle non-finite values.
Results may differ from a plain program's by a relative error of at most 0.00017.
Values sent between devices are 32-bit elements; how exact they have to be, the bound alone decides.
No kernel may reach another device: no remote copies, remote signals or barrier semaphores. Data moves between devices by JAX's collectives and lax.ppermute only.
A program may use at most 128 MiB of HBM per device.

v0:
```python
import jax.numpy as jnp
from jax import lax

N_SRC = 16
N_TGT = 8
LOCAL_LEVELS = 2


def flip_axis(values, axis, half):
    shape = values.shape
    length = shape[axis]
    split = shape[:axis] + (length // (2 * half), 2, half) + shape[axis + 1 :]
    return jnp.flip(values.reshape(split), axis + 1).reshape(shape)


def mixing(weight, coeffs):
    return jnp.einsum("kjg,jrg->krg", weight, coeffs, precision=lax.Precision.HIGHEST)


def reference(sources, source_interp, target_interp, transfer):
    rank = source_interp.shape[1]
    blocks_dev = sources.shape[2] // (N_SRC * N_TGT)
    local_bits = blocks_dev.bit_length() - 1
    src_bits = N_SRC.bit_length() - 1
    tgt_bits = N_TGT.bit_length() - 1
    order = [m for m in range(LOCAL_LEVELS)]
    order = order + [local_bits + tgt_bits + j for j in range(src_bits)]
    order = order + [local_bits + j for j in range(tgt_bits)]
    coeffs = jnp.einsum("bkg,rbg->krg", source_interp, sources, precision=lax.Precision.HIGHEST)
    for position, bit_pos in enumerate(order):
        weight = transfer[position]
        partner = flip_axis(coeffs, 2, 1 << bit_pos)
        coeffs = mixing(weight[:, :rank], coeffs) + mixing(weight[:, rank:], partner)
    return jnp.einsum("bkg,krg->rbg", target_interp, coeffs, precision=lax.Precision.HIGHEST)


def solution(mesh):
    return reference
```

profile of v0, /device:TPU:0, one launch (start us, length us, event | category | flops | bytes accessed | tf_op | source)
XLA Modules:
  0.0 312.0 jit_solution(8411340043974905667)
XLA Ops:
  0.0 7.4 %fusion.90 = (f32[1,32,64,128]{3,2,1,0:T(8,128)S(1)}, f32[1,32,64,128]{3,2,1,0:T(8,128)}, f32[1,32,64,128]{3,2,1,0:T(8,128)}, f32[1,32,64,128]{3,2,1,0:T(8,128)}...) fusion(f32[9,32,64,128]{3,2,1,0:T(8,128)} %param.2), kind=kLoop, calls=%fused_computation.60 | loop fusion | bytes 18874368 | tf_op jit(solution)/slice | solution.py:31
  7.4 3.1 copy.40
  10.4 5.3 %copy.12 = f32[64,128,128]{1,0,2:T(8,128)} copy(f32[64,128,128]{2,1,0:T(8,128)} %param) | data formatting | bytes 8388608 | tf_op args[0]
  15.8 3.6 %copy.13 = f32[128,32,128]{0,1,2:T(8,128)} copy(f32[128,32,128]{2,1,0:T(8,128)} %param.1) | data formatting | bytes 4194304 | tf_op args[1]
  19.4 10.8 %fusion.92 = f32[128,64,32]{1,2,0:T(8,128)} fusion(f32[64,128,128]{1,0,2:T(8,128)} %copy.12, f32[128,32,128]{0,1,2:T(8,128)} %copy.13), kind=kOutput, calls=%fused_computation.62 | convolution fusion | flops 402653184 | bytes 7340032 | tf_op jit(solution)/bkg,rbg->krg/dot_general | solution.py:29
  30.2 3.1 rev.36
  33.3 4.0 %fusion.28 = f32[128,64,32]{1,2,0:T(8,128)S(1)} fusion(f32[32,64,128]{1,0,2:T(8,128)} %bitcast.131, f32[32,64,128]{1,0,2:T(8,128)S(1)} %bitcast.112), kind=kOutput, calls=%fused_computation.29 | convolution fusion | flops 100663296 | bytes 3145728 | tf_op jit(solution)/kjg,jrg->krg/dot_general | solution.py:17
  37.3 3.6 %fusion.50 = f32[128,64,32]{1,2,0:T(8,128)} fusion(f32[128,64,32]{1,2,0:T(8,128)S(1)} %fusion.28, f32[32,64,128]{1,0,2:T(8,128)S(1)} %bitcast.113, f32[128,64,32]{1,2,0:T(8,128)S(1)} %copy-done.2), kind=kOutput, calls=%fused_computation.51 | convolution fusion | flops 100925440 | bytes 4194304 | tf_op jit(solution)/kjg,jrg->krg/dot_general | solution.py:17
  40.9 3.2 %rev.37 = f32[32,64,32,2,2]{1,0,4,3,2:T(8,128)} reverse(f32[32,64,32,2,2]{1,0,4,3,2:T(8,128)} %bitcast.128), dimensions={3} | reverse | bytes 2097152 | tf_op jit(solution)/jit(_flip)/rev | solution.py:13
  44.2 1.8 copy.41
  46.0 4.2 %fusion.24 = f32[128,64,32]{1,2,0:T(8,128)S(1)} fusion(f32[32,64,128]{1,0,2:T(8,128)} %bitcast.130, f32[32,64,128]{1,0,2:T(8,128)S(1)} %bitcast.126), kind=kOutput, calls=%fused_computation.25 | convolution fusion | flops 100663296 | bytes 3145728 | tf_op jit(solution)/kjg,jrg->krg/dot_general | solution.py:17
  50.3 3.6 %fusion.55 = f32[128,64,32]{1,2,0:T(8,128)} fusion(f32[128,64,32]{1,2,0:T(8,128)S(1)} %fusion.24, f32[32,64,128]{1,0,2:T(8,128)S(1)} %bitcast.127, f32[128,64,32]{1,2,0:T(8,128)S(1)} %copy-done.1), kind=kOutput, calls=%fused_computation.52 | convolution fusion | flops 100925440 | bytes 4194304 | tf_op jit(solution)/kjg,jrg->krg/dot_general | solution.py:17
  53.8 2.7 copy.17
  56.5 0.1 collective-permute-start
  56.6 3.1 copy.42
  59.7 5.0 %fusion.22 = f32[128,64,32]{1,2,0:T(8,128)} fusion(f32[32,64,128]{1,0,2:T(8,128)S(1)} %bitcast.114, f32[128,64,32]{1,2,0:T(8,128)} %fusion.55), kind=kOutput, calls=%fused_computation.23 | convolution fusion | flops 100663296 | bytes 3145728 | tf_op jit(solution)/kjg,jrg->krg/dot_general | solution.py:17
  64.7 4.0 %copy.18 = f32[32,64,1,1,128]{1,0,4,3,2:T(8,128)} copy(f32[32,64,1,1,128]{4,1,3,2,0:T(8,128)} %collective-permute-done) | data formatting | bytes 2097152 | tf_op jit(solution)/reshape | solution.py:13
  68.7 5.8 %fusion.60 = f32[128,64,32]{1,2,0:T(8,128)} fusion(f32[128,64,32]{1,2,0:T(8,128)} %fusion.22, f32[32,64,128]{1,0,2:T(8,128)S(1)} %bitcast.115, f32[32,64,1,1,128]{1,0,4,3,2:T(8,128)} %copy.18), kind=kOutput, calls=%fused_computation.53 | convolution fusion | flops 100925440 | bytes 4194304 | tf_op jit(solution)/kjg,jrg->krg/dot_general | solution.py:17
  74.5 2.7 copy.20
  77.1 2.5 collective-permute-start.1
  79.6 3.1 copy.43
  82.7 5.0 %fusion.18 = f32[128,64,32]{1,2,0:T(8,128)} fusion(f32[32,64,128]{1,0,2:T(8,128)S(1)} %bitcast.116, f32[128,64,32]{1,2,0:T(8,128)} %fusion.60), kind=kOutput, calls=%fused_computation.19 | convolution fusion | flops 100663296 | bytes 3145728 | tf_op jit(solution)/kjg,jrg->krg/dot_general | solution.py:17
  87.7 15.9 %collective-permute-done.1 = f32[32,64,1,1,128]{4,1,3,2,0:T(8,128)} collective-permute-done((f32[32,64,1,1,128]{4,1,3,2,0:T(8,128)S(1)}, f32[32,64,1,1,128]{4,1,3,2,0:T(8,128)}, u32[]{:S(2)}, u32[]{:S(2)}) %collective-permute-start.1) | collective-permute-done | bytes 1048608 | tf_op jit(solution)/reshape | solution.py:13
  103.6 4.1 %copy.21 = f32[32,64,1,1,128]{1,0,4,3,2:T(8,128)} copy(f32[32,64,1,1,128]{4,1,3,2,0:T(8,128)} %collective-permute-done.1) | data formatting | bytes 2097152 | tf_op jit(solution)/reshape | solution.py:13
  107.6 5.8 %fusion.65 = f32[128,64,32]{1,2,0:T(8,128)} fusion(f32[128,64,32]{1,2,0:T(8,128)} %fusion.18, f32[32,64,128]{1,0,2:T(8,128)S(1)} %bitcast.117, f32[32,64,1,1,128]{1,0,4,3,2:T(8,128)} %copy.21), kind=kOutput, calls=%fused_computation.54 | convolution fusion | flops 100925440 | bytes 4194304 | tf_op jit(solution)/kjg,jrg->krg/dot_general | solution.py:17
  113.4 2.7 copy.23
  116.0 4.0 %collective-permute-start.2 = (f32[32,64,1,1,128]{4,1,3,2,0:T(8,128)S(1)}, f32[32,64,1,1,128]{4,1,3,2,0:T(8,128)}, u32[]{:S(2)}, u32[]{:S(2)}) collective-permute-start(f32[32,64,1,1,128]{4,1,3,2,0:T(8,128)S(1)} %copy.23), channel_id=3, source_target_pairs={{0,32},{1,33},{2,34},{3,35},{4,36},{5,37},{6,38},{7,39},{8,40},{9,... | collective-permute-start | bytes 3145736 | tf_op jit(solution)/reshape | solution.py:13
  120.0 3.1 copy.44
  123.1 5.0 %fusion.14 = f32[128,64,32]{1,2,0:T(8,128)} fusion(f32[32,64,128]{1,0,2:T(8,128)S(1)} %bitcast.118, f32[128,64,32]{1,2,0:T(8,128)} %fusion.65), kind=kOutput, calls=%fused_computation.15 | convolution fusion | flops 100663296 | bytes 3145728 | tf_op jit(solution)/kjg,jrg->krg/dot_general | solution.py:17
  128.0 15.1 %collective-permute-done.2 = f32[32,64,1,1,128]{4,1,3,2,0:T(8,128)} collective-permute-done((f32[32,64,1,1,128]{4,1,3,2,0:T(8,128)S(1)}, f32[32,64,1,1,128]{4,1,3,2,0:T(8,128)}, u32[]{:S(2)}, u32[]{:S(2)}) %collective-permute-start.2) | collective-permute-done | bytes 1048608 | tf_op jit(solution)/reshape | solution.py:13
  143.1 4.0 %copy.24 = f32[32,64,1,1,128]{1,0,4,3,2:T(8,128)} copy(f32[32,64,1,1,128]{4,1,3,2,0:T(8,128)} %collective-permute-done.2) | data formatting | bytes 2097152 | tf_op jit(solution)/reshape | solution.py:13
  147.2 5.8 %fusion.70 = f32[128,64,32]{1,2,0:T(8,128)} fusion(f32[128,64,32]{1,2,0:T(8,128)} %fusion.14, f32[32,64,128]{1,0,2:T(8,128)S(1)} %bitcast.119, f32[32,64,1,1,128]{1,0,4,3,2:T(8,128)} %copy.24), kind=kOutput, calls=%fused_computation.55 | convolution fusion | flops 100925440 | bytes 4194304 | tf_op jit(solution)/kjg,jrg->krg/dot_general | solution.py:17
  153.0 2.7 copy.26
  155.6 3.5 %collective-permute-start.3 = (f32[32,64,1,1,128]{4,1,3,2,0:T(8,128)S(1)}, f32[32,64,1,1,128]{4,1,3,2,0:T(8,128)}, u32[]{:S(2)}, u32[]{:S(2)}) collective-permute-start(f32[32,64,1,1,128]{4,1,3,2,0:T(8,128)S(1)} %copy.26), channel_id=4, source_target_pairs={{0,64},{1,65},{2,66},{3,67},{4,68},{5,69},{6,70},{7,71},{8,72},{9,... | collective-permute-start | bytes 3145736 | tf_op jit(solution)/reshape | solution.py:13
  159.1 3.1 copy.45
  162.2 5.0 %fusion.10 = f32[128,64,32]{1,2,0:T(8,128)} fusion(f32[32,64,128]{1,0,2:T(8,128)S(1)} %bitcast.120, f32[128,64,32]{1,2,0:T(8,128)} %fusion.70), kind=kOutput, calls=%fused_computation.11 | convolution fusion | flops 100663296 | bytes 3145728 | tf_op jit(solution)/kjg,jrg->krg/dot_general | solution.py:17
  167.1 14.6 %collective-permute-done.3 = f32[32,64,1,1,128]{4,1,3,2,0:T(8,128)} collective-permute-done((f32[32,64,1,1,128]{4,1,3,2,0:T(8,128)S(1)}, f32[32,64,1,1,128]{4,1,3,2,0:T(8,128)}, u32[]{:S(2)}, u32[]{:S(2)}) %collective-permute-start.3) | collective-permute-done | bytes 1048608 | tf_op jit(solution)/reshape | solution.py:13
  181.7 4.1 %copy.27 = f32[32,64,1,1,128]{1,0,4,3,2:T(8,128)} copy(f32[32,64,1,1,128]{4,1,3,2,0:T(8,128)} %collective-permute-done.3) | data formatting | bytes 2097152 | tf_op jit(solution)/reshape | solution.py:13
  185.8 5.8 %fusion.75 = f32[128,64,32]{1,2,0:T(8,128)} fusion(f32[128,64,32]{1,2,0:T(8,128)} %fusion.10, f32[32,64,128]{1,0,2:T(8,128)S(1)} %bitcast.121, f32[32,64,1,1,128]{1,0,4,3,2:T(8,128)} %copy.27), kind=kOutput, calls=%fused_computation.56 | convolution fusion | flops 100925440 | bytes 4194304 | tf_op jit(solution)/kjg,jrg->krg/dot_general | solution.py:17
  191.6 2.7 copy.29
  194.2 2.0 collective-permute-start.4
  196.2 3.1 copy.46
  199.3 5.0 %fusion.6 = f32[128,64,32]{1,2,0:T(8,128)} fusion(f32[32,64,128]{1,0,2:T(8,128)S(1)} %bitcast.122, f32[128,64,32]{1,2,0:T(8,128)} %fusion.75), kind=kOutput, calls=%fused_computation.7 | convolution fusion | flops 100663296 | bytes 3145728 | tf_op jit(solution)/kjg,jrg->krg/dot_general | solution.py:17
  204.2 13.9 %collective-permute-done.4 = f32[32,64,1,1,128]{4,1,3,2,0:T(8,128)} collective-permute-done((f32[32,64,1,1,128]{4,1,3,2,0:T(8,128)S(1)}, f32[32,64,1,1,128]{4,1,3,2,0:T(8,128)}, u32[]{:S(2)}, u32[]{:S(2)}) %collective-permute-start.4) | collective-permute-done | bytes 1048608 | tf_op jit(solution)/reshape | solution.py:13
  218.1 4.0 %copy.30 = f32[32,64,1,1,128]{1,0,4,3,2:T(8,128)} copy(f32[32,64,1,1,128]{4,1,3,2,0:T(8,128)} %collective-permute-done.4) | data formatting | bytes 2097152 | tf_op jit(solution)/reshape | solution.py:13
  222.1 5.8 %fusion.80 = f32[128,64,32]{1,2,0:T(8,128)} fusion(f32[128,64,32]{1,2,0:T(8,128)} %fusion.6, f32[32,64,128]{1,0,2:T(8,128)S(1)} %bitcast.123, f32[32,64,1,1,128]{1,0,4,3,2:T(8,128)} %copy.30), kind=kOutput, calls=%fused_computation.57 | convolution fusion | flops 100925440 | bytes 4194304 | tf_op jit(solution)/kjg,jrg->krg/dot_general | solution.py:17
  227.9 2.7 copy.32
  230.6 3.3 %collective-permute-start.5 = (f32[32,64,1,1,128]{4,1,3,2,0:T(8,128)S(1)}, f32[32,64,1,1,128]{4,1,3,2,0:T(8,128)}, u32[]{:S(2)}, u32[]{:S(2)}) collective-permute-start(f32[32,64,1,1,128]{4,1,3,2,0:T(8,128)S(1)} %copy.32), channel_id=6, source_target_pairs={{0,2},{1,3},{2,0},{3,1},{4,6},{5,7},{6,4},{7,5},{8,10},{9,11},{10,... | collective-permute-start | bytes 3145736 | tf_op jit(solution)/reshape | solution.py:13
  233.9 3.1 copy.47
  236.9 5.0 %fusion.2 = f32[128,64,32]{1,2,0:T(8,128)} fusion(f32[32,64,128]{1,0,2:T(8,128)S(1)} %bitcast.124, f32[128,64,32]{1,2,0:T(8,128)} %fusion.80), kind=kOutput, calls=%fused_computation.3 | convolution fusion | flops 100663296 | bytes 3145728 | tf_op jit(solution)/kjg,jrg->krg/dot_general | solution.py:17
  241.9 12.9 %collective-permute-done.5 = f32[32,64,1,1,128]{4,1,3,2,0:T(8,128)} collective-permute-done((f32[32,64,1,1,128]{4,1,3,2,0:T(8,128)S(1)}, f32[32,64,1,1,128]{4,1,3,2,0:T(8,128)}, u32[]{:S(2)}, u32[]{:S(2)}) %collective-permute-start.5) | collective-permute-done | bytes 1048608 | tf_op jit(solution)/reshape | solution.py:13
  254.8 4.1 %copy.33 = f32[32,64,1,1,128]{1,0,4,3,2:T(8,128)} copy(f32[32,64,1,1,128]{4,1,3,2,0:T(8,128)} %collective-permute-done.5) | data formatting | bytes 2097152 | tf_op jit(solution)/reshape | solution.py:13
  258.9 5.8 %fusion.85 = f32[128,64,32]{1,2,0:T(8,128)} fusion(f32[128,64,32]{1,2,0:T(8,128)} %fusion.2, f32[32,64,128]{1,0,2:T(8,128)S(1)} %bitcast.125, f32[32,64,1,1,128]{1,0,4,3,2:T(8,128)} %copy.33), kind=kOutput, calls=%fused_computation.58 | convolution fusion | flops 100925440 | bytes 4194304 | tf_op jit(solution)/kjg,jrg->krg/dot_general | solution.py:17
  264.6 3.8 %copy.34 = f32[32,64,1,1,128]{4,1,3,2,0:T(8,128)} copy(f32[32,64,1,1,128]{1,0,4,3,2:T(8,128)} %bitcast.105) | data formatting | bytes 2097152 | tf_op jit(solution)/reshape | solution.py:13
  268.4 1.6 collective-permute-start.6
  270.1 2.9 copy.39
  272.9 2.9 copy.37
  275.8 3.7 %copy.35 = f32[128,32,128]{0,1,2:T(8,128)} copy(f32[128,32,128]{2,1,0:T(8,128)} %param.3) | data formatting | bytes 4194304 | tf_op args[2]
  279.5 5.9 %fusion.33 = f32[128,64,32]{1,2,0:T(8,128)} fusion(f32[32,32,128]{0,1,2:T(8,128)} %copy.37, f32[128,64,32]{1,2,0:T(8,128)S(1)} %copy-done), kind=kOutput, calls=%fused_computation.34 | convolution fusion | flops 100663296 | bytes 2621440 | tf_op jit(solution)/kjg,jrg->krg/dot_general | solution.py:17
  285.4 4.7 %collective-permute-done.6 = f32[32,64,1,1,128]{4,1,3,2,0:T(8,128)S(1)} collective-permute-done((f32[32,64,1,1,128]{4,1,3,2,0:T(8,128)}, f32[32,64,1,1,128]{4,1,3,2,0:T(8,128)S(1)}, u32[]{:S(2)}, u32[]{:S(2)}) %collective-permute-start.6) | collective-permute-done | bytes 1048608 | tf_op jit(solution)/reshape | solution.py:13
  290.1 2.8 copy.38
  292.9 5.2 %fusion.93 = f32[128,64,32]{1,2,0:T(8,128)S(1)} fusion(f32[32,64,128]{1,0,2:T(8,128)} %copy.38, f32[32,32,128]{0,1,2:T(8,128)S(1)} %copy-done.3), kind=kOutput, calls=%fused_computation.63 | convolution fusion | flops 100663296 | bytes 2621440 | tf_op jit(solution)/kjg,jrg->krg/dot_general | solution.py:17
  298.1 8.2 %convolution_bitcast_fusion = f32[64,128,128]{1,0,2:T(8,128)} fusion(f32[128,32,128]{0,1,2:T(8,128)S(1)} %copy-done.5, f32[128,64,32]{1,2,0:T(8,128)S(1)} %copy-done.4, f32[128,64,32]{1,2,0:T(8,128)S(1)} %fusion.93), kind=kOutput, calls=%fused_computation | convolution fusion | flops 402915328 | bytes 8388608 | tf_op jit(solution)/bkg,krg->rbg/dot_general | solution.py:34
  306.4 5.4 %copy.36 = f32[64,128,128]{2,1,0:T(8,128)} copy(f32[64,128,128]{1,0,2:T(8,128)} %convolution_bitcast_fusion) | data formatting | bytes 8388608 | tf_op jit(solution)/bkg,krg->rbg/transpose | solution.py:34
  (16 shorter events, 0.1 us)
Async XLA Ops:
  33.3 4.0 %copy-start.2 = (f32[128,64,32]{1,2,0:T(8,128)S(1)}, f32[128,64,32]{1,2,0:T(8,128)}, u32[]{:S(2)}) copy-start(f32[128,64,32]{1,2,0:T(8,128)} %fusion.92) | copy-start | bytes 3145732
  46.0 4.3 %copy-start.1 = (f32[128,64,32]{1,2,0:T(8,128)S(1)}, f32[128,64,32]{1,2,0:T(8,128)}, u32[]{:S(2)}) copy-start(f32[128,64,32]{1,2,0:T(8,128)} %fusion.50) | copy-start | bytes 3145732
  56.5 8.1 %collective-permute-start = (f32[32,64,1,1,128]{4,1,3,2,0:T(8,128)S(1)}, f32[32,64,1,1,128]{4,1,3,2,0:T(8,128)}, u32[]{:S(2)}, u32[]{:S(2)}) collective-permute-start(f32[32,64,1,1,128]{4,1,3,2,0:T(8,128)S(1)} %copy.17), channel_id=1, source_target_pairs={{0,8},{1,9},{2,10},{3,11},{4,12},{5,13},{6,14},{7,15},{8,0},{9,1},... | collective-permute-start | bytes 3145736 | tf_op jit(solution)/reshape | solution.py:13
  77.1 26.4 %collective-permute-start.1 = (f32[32,64,1,1,128]{4,1,3,2,0:T(8,128)S(1)}, f32[32,64,1,1,128]{4,1,3,2,0:T(8,128)}, u32[]{:S(2)}, u32[]{:S(2)}) collective-permute-start(f32[32,64,1,1,128]{4,1,3,2,0:T(8,128)S(1)} %copy.20), channel_id=2, source_target_pairs={{0,16},{1,17},{2,18},{3,19},{4,20},{5,21},{6,22},{7,23},{8,24},{9,... | collective-permute-start | bytes 3145736 | tf_op jit(solution)/reshape | solution.py:13
  116.0 27.1 %collective-permute-start.2 = (f32[32,64,1,1,128]{4,1,3,2,0:T(8,128)S(1)}, f32[32,64,1,1,128]{4,1,3,2,0:T(8,128)}, u32[]{:S(2)}, u32[]{:S(2)}) collective-permute-start(f32[32,64,1,1,128]{4,1,3,2,0:T(8,128)S(1)} %copy.23), channel_id=3, source_target_pairs={{0,32},{1,33},{2,34},{3,35},{4,36},{5,37},{6,38},{7,39},{8,40},{9,... | collective-permute-start | bytes 3145736 | tf_op jit(solution)/reshape | solution.py:13
  155.6 26.1 %collective-permute-start.3 = (f32[32,64,1,1,128]{4,1,3,2,0:T(8,128)S(1)}, f32[32,64,1,1,128]{4,1,3,2,0:T(8,128)}, u32[]{:S(2)}, u32[]{:S(2)}) collective-permute-start(f32[32,64,1,1,128]{4,1,3,2,0:T(8,128)S(1)} %copy.26), channel_id=4, source_target_pairs={{0,64},{1,65},{2,66},{3,67},{4,68},{5,69},{6,70},{7,71},{8,72},{9,... | collective-permute-start | bytes 3145736 | tf_op jit(solution)/reshape | solution.py:13
  194.2 23.9 %collective-permute-start.4 = (f32[32,64,1,1,128]{4,1,3,2,0:T(8,128)S(1)}, f32[32,64,1,1,128]{4,1,3,2,0:T(8,128)}, u32[]{:S(2)}, u32[]{:S(2)}) collective-permute-start(f32[32,64,1,1,128]{4,1,3,2,0:T(8,128)S(1)} %copy.29), channel_id=5, source_target_pairs={{0,1},{1,0},{2,3},{3,2},{4,5},{5,4},{6,7},{7,6},{8,9},{9,8},{10,11... | collective-permute-start | bytes 3145736 | tf_op jit(solution)/reshape | solution.py:13
  230.6 24.2 %collective-permute-start.5 = (f32[32,64,1,1,128]{4,1,3,2,0:T(8,128)S(1)}, f32[32,64,1,1,128]{4,1,3,2,0:T(8,128)}, u32[]{:S(2)}, u32[]{:S(2)}) collective-permute-start(f32[32,64,1,1,128]{4,1,3,2,0:T(8,128)S(1)} %copy.32), channel_id=6, source_target_pairs={{0,2},{1,3},{2,0},{3,1},{4,6},{5,7},{6,4},{7,5},{8,10},{9,11},{10,... | collective-permute-start | bytes 3145736 | tf_op jit(solution)/reshape | solution.py:13
  264.6 5.3 %copy-start.6 = (f32[32,64,128]{2,1,0:T(8,128)S(1)}, f32[32,64,128]{2,1,0:T(8,128)}, u32[]{:S(2)}) copy-start(f32[32,64,128]{2,1,0:T(8,128)} %get-tuple-element.11) | copy-start | bytes 3145732
  268.4 21.7 %collective-permute-start.6 = (f32[32,64,1,1,128]{4,1,3,2,0:T(8,128)}, f32[32,64,1,1,128]{4,1,3,2,0:T(8,128)S(1)}, u32[]{:S(2)}, u32[]{:S(2)}) collective-permute-start(f32[32,64,1,1,128]{4,1,3,2,0:T(8,128)} %copy.34), channel_id=7, source_target_pairs={{0,4},{1,5},{2,6},{3,7},{4,0},{5,1},{6,2},{7,3},{8,12},{9,13},{10,... | collective-permute-start | bytes 3145736 | tf_op jit(solution)/reshape | solution.py:13
  275.8 3.7 %copy-start = (f32[128,64,32]{1,2,0:T(8,128)S(1)}, f32[128,64,32]{1,2,0:T(8,128)}, u32[]{:S(2)}) copy-start(f32[128,64,32]{1,2,0:T(8,128)} %fusion.85) | copy-start | bytes 3145732
  285.4 7.5 %copy-start.3 = (f32[32,32,128]{0,1,2:T(8,128)S(1)}, f32[32,32,128]{0,1,2:T(8,128)}, u32[]{:S(2)}) copy-start(f32[32,32,128]{0,1,2:T(8,128)} %copy.39) | copy-start | bytes 1572868
  292.9 5.2 %copy-start.4 = (f32[128,64,32]{1,2,0:T(8,128)S(1)}, f32[128,64,32]{1,2,0:T(8,128)}, u32[]{:S(2)}) copy-start(f32[128,64,32]{1,2,0:T(8,128)} %fusion.33) | copy-start | bytes 3145732
  292.9 5.2 %copy-start.5 = (f32[128,32,128]{0,1,2:T(8,128)S(1)}, f32[128,32,128]{0,1,2:T(8,128)}, u32[]{:S(2)}) copy-start(f32[128,32,128]{0,1,2:T(8,128)} %copy.35) | copy-start | bytes 6291460
where the time goes:
time: 316 us; the launch traced here: 312 us
  matrix products  110 us (35%)
  local copies, waits for them, and re-layouts  108 us (34%)
  waiting for transfers between devices  77 us (24%)
  starting transfers between devices  16.8 us (5%)
    dot_general x18, matrix products, mixing(): jnp.einsum('kjg,jrg->krg', weight, coeffs, precision=lax.Precision.HIGHEST)  91.1 us
    reshape x7, waiting for transfers between devices, flip_axis(): return jnp.flip(values.reshape(split), axis + 1).reshape(shape)  77 us
    reshape x14, local copies, waits for them, and re-layouts, flip_axis(): return jnp.flip(values.reshape(split), axis + 1).reshape(shape)  46.8 us
    unnamed x25, local copies, waits for them, and re-layouts  35.8 us
    reshape x7, starting transfers between devices, flip_axis(): return jnp.flip(values.reshape(split), axis + 1).reshape(shape)  16.8 us
    dot_general x1, matrix products, reference(): jnp.einsum('bkg,rbg->krg', source_interp, sources, precision=lax.Precisio...  10.8 us
    dot_general x1, matrix products, reference(): jnp.einsum('bkg,krg->rbg', target_interp, coeffs, precision=lax.Precision...  8.24 us
    slice x1, local copies, waits for them, and re-layouts, reference(): weight = transfer[position]  7.38 us
  transfers between devices with their start and end apart: 7, of which 6 were waited for; matrix products, arithmetic and copies ran while one was open for 20% of the time, Pallas kernels for 0%

commit v1 on v0

v1 whole, which is shorter than its diff:
```python
import jax
import jax.numpy as jnp
from jax import lax
from jax.experimental import pallas as pl
from jax.experimental.pallas import tpu as pltpu
from jax.sharding import PartitionSpec as P

R, B, K, NB = 64, 128, 32, 128
HALF = NB // 2
CHUNKS = (16, 16, 16, 16)
MIB = 1 << 20
F32, BF16 = jnp.float32, jnp.bfloat16
VMEM = pl.BlockSpec(memory_space=pltpu.VMEM)


def in_vmem(*arrays):
    return [pltpu.with_memory_space_constraint(x, pltpu.VMEM) for x in arrays]


def in_hbm(*arrays):
    return [pltpu.with_memory_space_constraint(x, pltpu.HBM) for x in arrays]


def split(x):
    high = x.astype(BF16)
    return high, (x - high.astype(F32)).astype(BF16)


def low_lanes(shape):
    return lax.broadcasted_iota(jnp.int32, shape, len(shape) - 1) < HALF


def prepare_transfer(block, out_ref, k0):
    turned = [jnp.concatenate([block[i], block[i + 8]], 0).T for i in range(8)]
    mask = low_lanes((8, 8, NB))
    for g0 in range(0, NB, 8):
        v = jnp.swapaxes(jnp.stack([t[g0 : g0 + 8] for t in turned]), 0, 1)
        w = pltpu.roll(v, HALF, 2)
        vh = v.astype(BF16).astype(F32)
        wh = w.astype(BF16).astype(F32)
        first = jnp.where(mask, vh, w - wh)
        second = jnp.where(mask, wh, v - vh)
        gh, gl = divmod(g0, HALF)
        rows = jnp.concatenate([first, second], 1).astype(BF16)
        out_ref[gl : gl + 8, gh * K + k0 : gh * K + k0 + 16, :] = rows


def mix(weight, own, partner, mask):
    high, low = split(jnp.concatenate([own, partner], 0))
    both = jnp.concatenate([weight, weight], 1)
    s = jnp.dot(both, jnp.concatenate([high, high, low, low], 0), preferred_element_type=F32)
    return jnp.where(mask, s[:K], s[K:])


def source_kernel(src_ref, si_ref, t_ref, *refs):
    n = len(CHUNKS)
    outs, (s_ref, a_ref, m_ref, t0_ref, t1_ref, c_ref, d_ref) = refs[:n], refs[n:]
    step = pl.program_id(0)

    turned = [src_ref[i].T for i in range(8)]
    r0 = pl.multiple_of(step * 8, 8)
    for g0 in range(0, NB, 8):
        v = jnp.swapaxes(jnp.stack([t[g0 : g0 + 8] for t in turned]), 0, 1)
        s_ref[g0 : g0 + 8, pl.ds(r0, 8), :] = v
    b0 = pl.multiple_of(step * 16, 8)
    for i in range(2):
        a_ref[:, pl.ds(pl.multiple_of(b0 + 8 * i, 8), 8), :] = jnp.swapaxes(si_ref[8 * i : 8 * i + 8], 0, 1)

    for s in range(4):
        @pl.when(step == s)
        def _():
            prepare_transfer(t_ref[0], t0_ref if s < 2 else t1_ref, 16 * (s % 2))

    @pl.when(step == 7)
    def _():
        @pl.loop(0, K // 8)
        def _(i):
            k0 = pl.multiple_of(i * 8, 8)
            turned = [a_ref[k0 + j].T for j in range(8)]
            for g0 in range(0, NB, 8):
                v = jnp.swapaxes(jnp.stack([t[g0 : g0 + 8] for t in turned]), 0, 1)
                m_ref[g0 : g0 + 8, pl.ds(k0, 8), :] = v

        mask = low_lanes((K, NB))

        @pl.loop(0, 4)
        def _(i):
            for j in range(16):
                gl = i * 16 + j
                mh, ml = split(jnp.concatenate([m_ref[gl], m_ref[gl + HALF]], 0))
                sh, sl = split(jnp.concatenate([s_ref[gl], s_ref[gl + HALF]], 0))
                dims = (((1,), (1,)), ((), ()))
                s = lax.dot_general(jnp.concatenate([mh, ml], 1), jnp.concatenate([sh, sh], 1), dims, preferred_element_type=F32)
                s = s + lax.dot_general(mh, sl, dims, preferred_element_type=F32)
                c_ref[gl] = jnp.where(mask, s[:K], s[K:])

        @pl.loop(0, 4)
        def _(i):
            for j in range(16):
                d_ref[i * 16 + j] = mix(t0_ref[i * 16 + j], c_ref[i * 16 + j], c_ref[i * 16 + (j ^ 1)], mask)

        first = 0
        for out, size in zip(outs, CHUNKS):
            for j in range(size):
                gl = first + j
                out[j] = mix(t1_ref[gl], d_ref[gl], d_ref[gl ^ 2], mask)
            first += size


def source_stage(sources, source_interp, transfer):
    return pl.pallas_call(
        source_kernel,
        name="source_stage",
        grid=(8,),
        in_specs=[
            pl.BlockSpec((8, B, NB), lambda i: (i, 0, 0)),
            pl.BlockSpec((16, K, NB), lambda i: (i, 0, 0)),
            pl.BlockSpec((1, 16, 2 * K, NB), lambda i: (jnp.minimum(i // 2, 1), jnp.where(i < 4, i % 2, 1), 0, 0)),
        ],
        out_specs=[VMEM] * len(CHUNKS),
        out_shape=[pltpu.VMEM((size, K, NB), F32) for size in CHUNKS],
        scratch_shapes=[
            pltpu.VMEM((NB, R, B), F32),
            pltpu.VMEM((K, B, NB), F32),
            pltpu.VMEM((NB, K, B), F32),
            pltpu.VMEM((HALF, 2 * K, NB), BF16),
            pltpu.VMEM((HALF, 2 * K, NB), BF16),
            pltpu.VMEM((HALF, K, NB), F32),
            pltpu.VMEM((HALF, K, NB), F32),
        ],
        compiler_params=pltpu.CompilerParams(vmem_limit_bytes=20 * MIB),
    )(*in_hbm(sources, source_interp, transfer))


def transfer_stage(transfer, level):
    def kernel(t_ref, o_ref):
        for i in range(2):
            prepare_transfer(t_ref.at[level, pl.ds(16 * i, 16)], o_ref, 16 * i)

    return pl.pallas_call(
        kernel,
        name=f"transfer_{level}",
        in_specs=[VMEM],
        out_specs=VMEM,
        out_shape=pltpu.VMEM((HALF, 2 * K, NB), BF16),
        compiler_params=pltpu.CompilerParams(vmem_limit_bytes=4 * MIB),
        cost_estimate=pl.CostEstimate(flops=10**6, bytes_accessed=4 * MIB, transcendentals=0),
    )(*in_vmem(transfer))


def target_matrix_kernel(ti_ref, o_ref, a_ref):
    for b0 in range(0, B, 8):
        a_ref[:, b0 : b0 + 8, :] = jnp.swapaxes(ti_ref[b0 : b0 + 8], 0, 1)

    @pl.loop(0, K // 8)
    def _(i):
        k0 = pl.multiple_of(i * 8, 8)
        turned = [a_ref[k0 + j].T for j in range(8)]
        for g0 in range(0, NB, 8):
            v = jnp.swapaxes(jnp.stack([t[g0 : g0 + 8] for t in turned]), 0, 1)
            o_ref[g0 : g0 + 8, pl.ds(k0, 8), :] = v


def target_matrix_stage(target_interp):
    return pl.pallas_call(
        target_matrix_kernel,
        name="target_matrix",
        in_specs=[VMEM],
        out_specs=VMEM,
        out_shape=pltpu.VMEM((NB, K, B), F32),
        scratch_shapes=[pltpu.VMEM((K, B, NB), F32)],
        compiler_params=pltpu.CompilerParams(vmem_limit_bytes=6 * MIB),
        cost_estimate=pl.CostEstimate(flops=10**6, bytes_accessed=8 * MIB, transcendentals=0),
    )(*in_vmem(target_interp))


def level_stage(weights, own, partner, first, level):
    size = own.shape[0]

    def kernel(t_ref, c_ref, p_ref, o_ref):
        mask = low_lanes((K, NB))
        for j in range(size):
            o_ref[j] = mix(t_ref[first + j], c_ref[j], p_ref[j], mask)

    return pl.pallas_call(
        kernel,
        name=f"level_{level}_{first}",
        in_specs=[VMEM] * 3,
        out_specs=VMEM,
        out_shape=pltpu.VMEM((size, K, NB), F32),
        compiler_params=pltpu.CompilerParams(vmem_limit_bytes=2 * MIB),
        cost_estimate=pl.CostEstimate(flops=size * 2 * 64 * 256 * 128, bytes_accessed=size * 64 * 1024, transcendentals=0),
    )(*in_vmem(weights, own, partner))


def last_stage(weights, own, partner, matrix, first):
    size = own.shape[0]

    def kernel(t_ref, c_ref, p_ref, m_ref, o_ref):
        mask = low_lanes((K, NB))
        for j0 in range(0, size, 8):
            values = [[], []]
            for j in range(j0, j0 + 8):
                gl = first + j
                c = mix(t_ref[gl], c_ref[j], p_ref[j], mask)
                high, low = split(c)
                left = jnp.concatenate([high, low, high, low], 0).T
                for gh in range(2):
                    th, tl = split(m_ref[gh * HALF + gl])
                    right = jnp.concatenate([th, th, tl, tl], 0)
                    values[gh].append(jnp.dot(left[gh * R : gh * R + R], right, preferred_element_type=F32))
            for gh in range(2):
                o_ref[:, gh, j0 : j0 + 8, :] = jnp.swapaxes(jnp.stack(values[gh]), 0, 1)

    return pl.pallas_call(
        kernel,
        name=f"last_{first}",
        in_specs=[VMEM] * 4,
        out_specs=VMEM,
        out_shape=pltpu.VMEM((R, 2, size, B), F32),
        compiler_params=pltpu.CompilerParams(vmem_limit_bytes=4 * MIB),
        cost_estimate=pl.CostEstimate(flops=size * 4 * 64 * 256 * 128, bytes_accessed=size * 128 * 1024, transcendentals=0),
    )(*in_vmem(weights, own, partner, matrix))


def output_stage(parts):
    def kernel(*refs):
        *ins, o_ref = refs
        r0 = pl.program_id(0) * 8
        for i in range(8):
            rows = [ref[r0 + i, gh] for gh in range(2) for ref in ins]
            o_ref[i] = jnp.concatenate(rows, 0).T

    return pl.pallas_call(
        kernel,
        name="output",
        grid=(8,),
        in_specs=[VMEM] * len(parts),
        out_specs=pl.BlockSpec((8, B, NB), lambda i: (i, 0, 0)),
        out_shape=jax.ShapeDtypeStruct((R, B, NB), F32),
        compiler_params=pltpu.CompilerParams(vmem_limit_bytes=4 * MIB),
    )(*in_vmem(*parts))


def device_program(exchange, sources, source_interp, target_interp, transfer):
    chunks = source_stage(sources, source_interp, transfer)
    firsts = [sum(CHUNKS[:i]) for i in range(len(CHUNKS))]
    for level in range(2, 8):
        weights = transfer_stage(transfer, level)
        partners = [exchange(c, level) for c in chunks]
        chunks = [level_stage(weights, c, p, first, level) for c, p, first in zip(chunks, partners, firsts)]
    weights = transfer_stage(transfer, 8)
    matrix = target_matrix_stage(target_interp)
    partners = [exchange(c, 8) for c in chunks]
    parts = [last_stage(weights, c, p, matrix, first) for c, p, first in zip(chunks, partners, firsts)]
    return output_stage(parts)


def solution(mesh):
    n_src, n_tgt = mesh.shape["src"], mesh.shape["tgt"]

    def exchange(c, level):
        if level < 6:
            axis, size, bit = "src", n_src, level - 2
        else:
            axis, size, bit = "tgt", n_tgt, level - 6
        return lax.ppermute(c, axis, [(i, i ^ (1 << bit)) for i in range(size)])

    def program(*args):
        return device_program(exchange, *args)

    blocks = ("src", "tgt")
    return jax.shard_map(
        program,
        mesh=mesh,
        in_specs=(P(None, None, blocks), P(None, None, blocks), P(None, None, blocks), P(None, None, None, blocks)),
        out_specs=P(None, None, blocks),
        check_vma=False,
    )
```

time: 316 us -> 143 us (0.45); the launches traced: 312 us -> 143 us
  matrix products: 110 us -> 0 us
  local copies, waits for them, and re-layouts: 108 us -> 0.01 us
  Pallas kernels: 0 us -> 46.2 us
  starting transfers between devices: 16.8 us -> 56.1 us
  waiting for transfers between devices: 77 us -> 40.4 us
    dot_general x20 -> x0, matrix products: 110 us -> none  [the longest x18 91.1 us: mixing(): jnp.einsum('kjg,jrg->krg', weight, coeffs, precision=lax.Precision.HIGHEST)]
    reshape x7 -> x0, waiting for transfers between devices: 77 us -> none  [flip_axis(): return jnp.flip(values.reshape(split), axis + 1).reshape(shape)]
    ppermute x0 -> x28, starting transfers between devices: none -> 56.1 us  [exchange(): return lax.ppermute(c, axis, [(i, i ^ 1 << bit) for i in range(size)])]
    reshape x14 -> x0, local copies, waits for them, and re-layouts: 46.8 us -> none  [flip_axis(): return jnp.flip(values.reshape(split), axis + 1).reshape(shape)]
    pallas_call x0 -> x38, Pallas kernels: none -> 46.2 us  [the longest x1 14.6 us: source_stage(): pl.pallas_call(source_kernel, name='source_stage', grid=(8,), in_specs=[p...]
    ppermute x0 -> x28, waiting for transfers between devices: none -> 40.4 us  [exchange(): return lax.ppermute(c, axis, [(i, i ^ 1 << bit) for i in range(size)])]
    unnamed x25 -> x4, local copies, waits for them, and re-layouts: 35.8 us -> 0.01 us
    reshape x7 -> x0, starting transfers between devices: 16.8 us -> none  [flip_axis(): return jnp.flip(values.reshape(split), axis + 1).reshape(shape)]
  transfers between devices with their start and end apart: 7 -> 28, of which waited for: 6 -> 17; matrix products, arithmetic and copies ran while one was open for 20% -> 0% of each run, Pallas kernels for 0% -> 17%
where the time goes in v1:
time: 143 us
  starting transfers between devices  56.1 us (39%)
  Pallas kernels  46.2 us (32%)
  waiting for transfers between devices  40.4 us (28%)
    ppermute x28, starting transfers between devices, exchange(): return lax.ppermute(c, axis, [(i, i ^ 1 << bit) for i in range(size)])  56.1 us
    ppermute x28, waiting for transfers between devices, exchange(): return lax.ppermute(c, axis, [(i, i ^ 1 << bit) for i in range(size)])  40.4 us
    pallas_call x1, Pallas kernels, source_stage(): pl.pallas_call(source_kernel, name='source_stage', grid=(8,), in_specs=[p...  14.6 us
    pallas_call x4, Pallas kernels, last_stage(): pl.pallas_call(kernel, name=f'last_{first}', in_specs=[VMEM] * 4, out_spe...  13.9 us
    pallas_call x24, Pallas kernels, level_stage(): pl.pallas_call(kernel, name=f'level_{level}_{first}', in_specs=[VMEM] * 3...  7.07 us
    pallas_call x7, Pallas kernels, transfer_stage(): pl.pallas_call(kernel, name=f'transfer_{level}', in_specs=[VMEM], out_spe...  5.07 us
    pallas_call x1, Pallas kernels, output_stage(): pl.pallas_call(kernel, name='output', grid=(8,), in_specs=[VMEM] * len(pa...  4.21 us
  transfers between devices with their start and end apart: 28, of which 17 were waited for; matrix products, arithmetic and copies ran while one was open for 0% of the time, Pallas kernels for 17%

profile of v1, /device:TPU:0, one launch (start us, length us, event | category | flops | bytes accessed | tf_op | source)
XLA Modules:
  0.0 143.0 jit_solution(16835487781977545509)
XLA Ops:
  0.0 14.6 %source_stage.1 = (f32[16,32,128]{2,1,0:T(8,128)S(1)}, f32[16,32,128]{2,1,0:T(8,128)S(1)}, f32[16,32,128]{2,1,0:T(8,128)S(1)}, f32[16,32,128]{2,1,0:T(8,128)S(1)}) custom-call(f32[64,128,128]{2,1,0:T(8,128)} %src_ref.1, f32[128,32,128]{2,1,0:T(8,128)} %si_ref.1, f32[9,32,64,128]{3,2,1,0:T(8,128)} %t_ref.15), custom_call_target="tpu_custom_call" | custom-call | tf_op jit(solution)/shard_map/source_stage/pallas_call | solution.py:111
  14.7 0.5 collective-permute-start.14
  15.3 0.4 collective-permute-start
  15.7 0.7 transfer_2.1.t_ref
  16.4 0.3 level_2_48.1.c_ref
  16.7 2.1 %collective-permute-start.22 = (f32[16,32,128]{2,1,0:T(8,128)S(1)}, f32[16,32,128]{2,1,0:T(8,128)S(1)}, u32[]{:S(2)}, u32[]{:S(2)}) collective-permute-start(f32[16,32,128]{2,1,0:T(8,128)S(1)} %level_2_48.1.c_ref), channel_id=1, source_target_pairs={{0,16},{8,24},{16,0},{24,8},{32,48},{40,56},{48,32},{56,40},{64,80... | collective-permute-start | bytes 786440 | tf_op jit(solution)/shard_map/ppermute | solution.py:267
  19.5 2.1 %collective-permute-start.8 = (f32[16,32,128]{2,1,0:T(8,128)S(1)}, f32[16,32,128]{2,1,0:T(8,128)S(1)}, u32[]{:S(2)}, u32[]{:S(2)}) collective-permute-start(f32[16,32,128]{2,1,0:T(8,128)S(1)} %level_2_16.1.c_ref), channel_id=1, source_target_pairs={{0,16},{8,24},{16,0},{24,8},{32,48},{40,56},{48,32},{56,40},{64,80... | collective-permute-start | bytes 786440 | tf_op jit(solution)/shard_map/ppermute | solution.py:267
  22.0 0.7 transfer_3.1.t_ref
  22.8 3.2 %collective-permute-done.22.p_ref = f32[16,32,128]{2,1,0:T(8,128)S(1)} collective-permute-done((f32[16,32,128]{2,1,0:T(8,128)S(1)}, f32[16,32,128]{2,1,0:T(8,128)S(1)}, u32[]{:S(2)}, u32[]{:S(2)}) %collective-permute-start.22) | collective-permute-done | bytes 262176 | tf_op jit(solution)/shard_map/ppermute | solution.py:267
  26.2 4.1 %collective-permute-start.23 = (f32[16,32,128]{2,1,0:T(8,128)S(1)}, f32[16,32,128]{2,1,0:T(8,128)S(1)}, u32[]{:S(2)}, u32[]{:S(2)}) collective-permute-start(f32[16,32,128]{2,1,0:T(8,128)S(1)} %level_3_48.1.c_ref), channel_id=1, source_target_pairs={{0,32},{8,40},{16,48},{24,56},{32,0},{40,8},{48,16},{56,24},{64,96... | collective-permute-start | bytes 786440 | tf_op jit(solution)/shard_map/ppermute | solution.py:267
  30.3 1.2 collective-permute-done.15.p_ref
  31.9 4.1 %collective-permute-start.16 = (f32[16,32,128]{2,1,0:T(8,128)S(1)}, f32[16,32,128]{2,1,0:T(8,128)S(1)}, u32[]{:S(2)}, u32[]{:S(2)}) collective-permute-start(f32[16,32,128]{2,1,0:T(8,128)S(1)} %level_3_32.1.c_ref), channel_id=1, source_target_pairs={{0,32},{8,40},{16,48},{24,56},{32,0},{40,8},{48,16},{56,24},{64,96... | collective-permute-start | bytes 786440 | tf_op jit(solution)/shard_map/ppermute | solution.py:267
  35.9 1.2 collective-permute-done.8.p_ref
  37.5 4.1 %collective-permute-start.9 = (f32[16,32,128]{2,1,0:T(8,128)S(1)}, f32[16,32,128]{2,1,0:T(8,128)S(1)}, u32[]{:S(2)}, u32[]{:S(2)}) collective-permute-start(f32[16,32,128]{2,1,0:T(8,128)S(1)} %level_3_16.1.c_ref), channel_id=1, source_target_pairs={{0,32},{8,40},{16,48},{24,56},{32,0},{40,8},{48,16},{56,24},{64,96... | collective-permute-start | bytes 786440 | tf_op jit(solution)/shard_map/ppermute | solution.py:267
  41.5 1.2 collective-permute-done.1.p_ref
  43.1 4.1 %collective-permute-start.2 = (f32[16,32,128]{2,1,0:T(8,128)S(1)}, f32[16,32,128]{2,1,0:T(8,128)S(1)}, u32[]{:S(2)}, u32[]{:S(2)}) collective-permute-start(f32[16,32,128]{2,1,0:T(8,128)S(1)} %level_3_0.1.c_ref), channel_id=1, source_target_pairs={{0,32},{8,40},{16,48},{24,56},{32,0},{40,8},{48,16},{56,24},{64,96... | collective-permute-start | bytes 786440 | tf_op jit(solution)/shard_map/ppermute | solution.py:267
  47.2 0.7 transfer_4.1.t_ref
  47.9 4.1 %collective-permute-done.23.p_ref = f32[16,32,128]{2,1,0:T(8,128)S(1)} collective-permute-done((f32[16,32,128]{2,1,0:T(8,128)S(1)}, f32[16,32,128]{2,1,0:T(8,128)S(1)}, u32[]{:S(2)}, u32[]{:S(2)}) %collective-permute-start.23) | collective-permute-done | bytes 262176 | tf_op jit(solution)/shard_map/ppermute | solution.py:267
  52.3 3.5 %collective-permute-start.24 = (f32[16,32,128]{2,1,0:T(8,128)S(1)}, f32[16,32,128]{2,1,0:T(8,128)S(1)}, u32[]{:S(2)}, u32[]{:S(2)}) collective-permute-start(f32[16,32,128]{2,1,0:T(8,128)S(1)} %level_4_48.1.c_ref), channel_id=1, source_target_pairs={{0,64},{8,72},{16,80},{24,88},{32,96},{40,104},{48,112},{56,120},{... | collective-permute-start | bytes 786440 | tf_op jit(solution)/shard_map/ppermute | solution.py:267
  55.8 1.9 %collective-permute-done.16.p_ref = f32[16,32,128]{2,1,0:T(8,128)S(1)} collective-permute-done((f32[16,32,128]{2,1,0:T(8,128)S(1)}, f32[16,32,128]{2,1,0:T(8,128)S(1)}, u32[]{:S(2)}, u32[]{:S(2)}) %collective-permute-start.16) | collective-permute-done | bytes 262176 | tf_op jit(solution)/shard_map/ppermute | solution.py:267
  57.6 0.3 level_4_32.1.c_ref
  57.9 3.3 %collective-permute-start.17 = (f32[16,32,128]{2,1,0:T(8,128)S(1)}, f32[16,32,128]{2,1,0:T(8,128)S(1)}, u32[]{:S(2)}, u32[]{:S(2)}) collective-permute-start(f32[16,32,128]{2,1,0:T(8,128)S(1)} %level_4_32.1.c_ref), channel_id=1, source_target_pairs={{0,64},{8,72},{16,80},{24,88},{32,96},{40,104},{48,112},{56,120},{... | collective-permute-start | bytes 786440 | tf_op jit(solution)/shard_map/ppermute | solution.py:267
  61.2 2.0 %collective-permute-done.9.p_ref = f32[16,32,128]{2,1,0:T(8,128)S(1)} collective-permute-done((f32[16,32,128]{2,1,0:T(8,128)S(1)}, f32[16,32,128]{2,1,0:T(8,128)S(1)}, u32[]{:S(2)}, u32[]{:S(2)}) %collective-permute-start.9) | collective-permute-done | bytes 262176 | tf_op jit(solution)/shard_map/ppermute | solution.py:267
  63.2 0.3 level_4_16.1.c_ref
  63.5 3.3 %collective-permute-start.10 = (f32[16,32,128]{2,1,0:T(8,128)S(1)}, f32[16,32,128]{2,1,0:T(8,128)S(1)}, u32[]{:S(2)}, u32[]{:S(2)}) collective-permute-start(f32[16,32,128]{2,1,0:T(8,128)S(1)} %level_4_16.1.c_ref), channel_id=1, source_target_pairs={{0,64},{8,72},{16,80},{24,88},{32,96},{40,104},{48,112},{56,120},{... | collective-permute-start | bytes 786440 | tf_op jit(solution)/shard_map/ppermute | solution.py:267
  66.8 1.2 collective-permute-done.2.p_ref
  68.0 0.3 level_4_0.1.c_ref
  68.3 3.3 %collective-permute-start.3 = (f32[16,32,128]{2,1,0:T(8,128)S(1)}, f32[16,32,128]{2,1,0:T(8,128)S(1)}, u32[]{:S(2)}, u32[]{:S(2)}) collective-permute-start(f32[16,32,128]{2,1,0:T(8,128)S(1)} %level_4_0.1.c_ref), channel_id=1, source_target_pairs={{0,64},{8,72},{16,80},{24,88},{32,96},{40,104},{48,112},{56,120},{... | collective-permute-start | bytes 786440 | tf_op jit(solution)/shard_map/ppermute | solution.py:267
  71.6 0.7 transfer_5.1.t_ref
  72.3 0.3 level_5_48.1.c_ref
  72.6 1.6 %collective-permute-start.25 = (f32[16,32,128]{2,1,0:T(8,128)S(1)}, f32[16,32,128]{2,1,0:T(8,128)S(1)}, u32[]{:S(2)}, u32[]{:S(2)}) collective-permute-start(f32[16,32,128]{2,1,0:T(8,128)S(1)} %level_5_48.1.c_ref), channel_id=1, source_target_pairs={{0,1},{1,0},{2,3},{3,2},{4,5},{5,4},{6,7},{7,6},{8,9},{9,8},{10,11... | collective-permute-start | bytes 786440 | tf_op jit(solution)/shard_map/ppermute | solution.py:267
  74.2 0.3 level_5_32.1.c_ref
  74.5 0.6 collective-permute-start.18
  75.1 0.3 level_5_16.1.c_ref
  75.4 1.6 %collective-permute-start.11 = (f32[16,32,128]{2,1,0:T(8,128)S(1)}, f32[16,32,128]{2,1,0:T(8,128)S(1)}, u32[]{:S(2)}, u32[]{:S(2)}) collective-permute-start(f32[16,32,128]{2,1,0:T(8,128)S(1)} %level_5_16.1.c_ref), channel_id=1, source_target_pairs={{0,1},{1,0},{2,3},{3,2},{4,5},{5,4},{6,7},{7,6},{8,9},{9,8},{10,11... | collective-permute-start | bytes 786440 | tf_op jit(solution)/shard_map/ppermute | solution.py:267
  77.0 0.5 collective-permute-done.3.p_ref
  77.8 1.6 %collective-permute-start.4 = (f32[16,32,128]{2,1,0:T(8,128)S(1)}, f32[16,32,128]{2,1,0:T(8,128)S(1)}, u32[]{:S(2)}, u32[]{:S(2)}) collective-permute-start(f32[16,32,128]{2,1,0:T(8,128)S(1)} %level_5_0.1.c_ref), channel_id=1, source_target_pairs={{0,1},{1,0},{2,3},{3,2},{4,5},{5,4},{6,7},{7,6},{8,9},{9,8},{10,11... | collective-permute-start | bytes 786440 | tf_op jit(solution)/shard_map/ppermute | solution.py:267
  79.4 0.7 transfer_6.1.t_ref
  80.1 1.8 %collective-permute-done.25.p_ref = f32[16,32,128]{2,1,0:T(8,128)S(1)} collective-permute-done((f32[16,32,128]{2,1,0:T(8,128)S(1)}, f32[16,32,128]{2,1,0:T(8,128)S(1)}, u32[]{:S(2)}, u32[]{:S(2)}) %collective-permute-start.25) | collective-permute-done | bytes 262176 | tf_op jit(solution)/shard_map/ppermute | solution.py:267
  82.2 3.1 %collective-permute-start.26 = (f32[16,32,128]{2,1,0:T(8,128)S(1)}, f32[16,32,128]{2,1,0:T(8,128)S(1)}, u32[]{:S(2)}, u32[]{:S(2)}) collective-permute-start(f32[16,32,128]{2,1,0:T(8,128)S(1)} %level_6_48.1.c_ref), channel_id=1, source_target_pairs={{0,2},{1,3},{2,0},{3,1},{4,6},{5,7},{6,4},{7,5},{8,10},{9,11},{10,... | collective-permute-start | bytes 786440 | tf_op jit(solution)/shard_map/ppermute | solution.py:267
  85.4 2.2 %collective-permute-done.18.p_ref = f32[16,32,128]{2,1,0:T(8,128)S(1)} collective-permute-done((f32[16,32,128]{2,1,0:T(8,128)S(1)}, f32[16,32,128]{2,1,0:T(8,128)S(1)}, u32[]{:S(2)}, u32[]{:S(2)}) %collective-permute-start.18) | collective-permute-done | bytes 262176 | tf_op jit(solution)/shard_map/ppermute | solution.py:267
  87.9 3.1 %collective-permute-start.19 = (f32[16,32,128]{2,1,0:T(8,128)S(1)}, f32[16,32,128]{2,1,0:T(8,128)S(1)}, u32[]{:S(2)}, u32[]{:S(2)}) collective-permute-start(f32[16,32,128]{2,1,0:T(8,128)S(1)} %level_6_32.1.c_ref), channel_id=1, source_target_pairs={{0,2},{1,3},{2,0},{3,1},{4,6},{5,7},{6,4},{7,5},{8,10},{9,11},{10,... | collective-permute-start | bytes 786440 | tf_op jit(solution)/shard_map/ppermute | solution.py:267
  91.0 2.2 %collective-permute-done.11.p_ref = f32[16,32,128]{2,1,0:T(8,128)S(1)} collective-permute-done((f32[16,32,128]{2,1,0:T(8,128)S(1)}, f32[16,32,128]{2,1,0:T(8,128)S(1)}, u32[]{:S(2)}, u32[]{:S(2)}) %collective-permute-start.11) | collective-permute-done | bytes 262176 | tf_op jit(solution)/shard_map/ppermute | solution.py:267
  93.5 3.1 %collective-permute-start.12 = (f32[16,32,128]{2,1,0:T(8,128)S(1)}, f32[16,32,128]{2,1,0:T(8,128)S(1)}, u32[]{:S(2)}, u32[]{:S(2)}) collective-permute-start(f32[16,32,128]{2,1,0:T(8,128)S(1)} %level_6_16.1.c_ref), channel_id=1, source_target_pairs={{0,2},{1,3},{2,0},{3,1},{4,6},{5,7},{6,4},{7,5},{8,10},{9,11},{10,... | collective-permute-start | bytes 786440 | tf_op jit(solution)/shard_map/ppermute | solution.py:267
  96.6 2.2 %collective-permute-done.4.p_ref = f32[16,32,128]{2,1,0:T(8,128)S(1)} collective-permute-done((f32[16,32,128]{2,1,0:T(8,128)S(1)}, f32[16,32,128]{2,1,0:T(8,128)S(1)}, u32[]{:S(2)}, u32[]{:S(2)}) %collective-permute-start.4) | collective-permute-done | bytes 262176 | tf_op jit(solution)/shard_map/ppermute | solution.py:267
  99.1 3.1 %collective-permute-start.5 = (f32[16,32,128]{2,1,0:T(8,128)S(1)}, f32[16,32,128]{2,1,0:T(8,128)S(1)}, u32[]{:S(2)}, u32[]{:S(2)}) collective-permute-start(f32[16,32,128]{2,1,0:T(8,128)S(1)} %level_6_0.1.c_ref), channel_id=1, source_target_pairs={{0,2},{1,3},{2,0},{3,1},{4,6},{5,7},{6,4},{7,5},{8,10},{9,11},{10,... | collective-permute-start | bytes 786440 | tf_op jit(solution)/shard_map/ppermute | solution.py:267
  102.2 0.7 transfer_7.1.t_ref
  102.9 3.7 %collective-permute-done.26.p_ref = f32[16,32,128]{2,1,0:T(8,128)S(1)} collective-permute-done((f32[16,32,128]{2,1,0:T(8,128)S(1)}, f32[16,32,128]{2,1,0:T(8,128)S(1)}, u32[]{:S(2)}, u32[]{:S(2)}) %collective-permute-start.26) | collective-permute-done | bytes 262176 | tf_op jit(solution)/shard_map/ppermute | solution.py:267
  106.9 0.8 collective-permute-start.27
  107.7 4.6 %collective-permute-done.19.p_ref = f32[16,32,128]{2,1,0:T(8,128)S(1)} collective-permute-done((f32[16,32,128]{2,1,0:T(8,128)S(1)}, f32[16,32,128]{2,1,0:T(8,128)S(1)}, u32[]{:S(2)}, u32[]{:S(2)}) %collective-permute-start.19) | collective-permute-done | bytes 262176 | tf_op jit(solution)/shard_map/ppermute | solution.py:267
  112.2 0.3 level_7_32.1.c_ref
  112.5 0.8 collective-permute-start.20
  113.3 4.6 %collective-permute-done.12.p_ref = f32[16,32,128]{2,1,0:T(8,128)S(1)} collective-permute-done((f32[16,32,128]{2,1,0:T(8,128)S(1)}, f32[16,32,128]{2,1,0:T(8,128)S(1)}, u32[]{:S(2)}, u32[]{:S(2)}) %collective-permute-start.12) | collective-permute-done | bytes 262176 | tf_op jit(solution)/shard_map/ppermute | solution.py:267
  117.8 0.3 level_7_16.1.c_ref
  118.2 0.8 collective-permute-start.13
  118.9 2.5 %collective-permute-done.5.p_ref = f32[16,32,128]{2,1,0:T(8,128)S(1)} collective-permute-done((f32[16,32,128]{2,1,0:T(8,128)S(1)}, f32[16,32,128]{2,1,0:T(8,128)S(1)}, u32[]{:S(2)}, u32[]{:S(2)}) %collective-permute-start.5) | collective-permute-done | bytes 262176 | tf_op jit(solution)/shard_map/ppermute | solution.py:267
  121.7 1.0 collective-permute-start.6
  122.7 0.7 transfer_8.1.t_ref
  123.4 1.4 %target_matrix.1.m_ref = f32[128,32,128]{2,1,0:T(8,128)S(1)} custom-call(f32[128,32,128]{2,1,0:T(8,128)S(1)} %copy-done.1), custom_call_target="tpu_custom_call" | custom-call | flops 1000000 | bytes 8388608 | tf_op jit(solution)/shard_map/target_matrix/pallas_call | solution.py:165
  124.9 3.5 %last_48.1.refs_3_ = f32[64,2,16,128]{3,2,1,0:T(8,128)S(1)} custom-call(bf16[64,64,128]{2,1,0:T(8,128)(2,1)S(1)} %transfer_8.1.t_ref, f32[16,32,128]{2,1,0:T(8,128)S(1)} %level_7_48.1.c_ref, f32[16,32,128]{2,1,0:T(8,128)S(1)} %collective-permute-done.27.p_ref, f32[128,32,128]{2,1,0:T(8,128)S(1)} %target_matrix.1.m_ref), custom_call_target="tpu_custom_call" | custom-call | flops 134217728 | bytes 2097152 | tf_op jit(solution)/shard_map/last_48/pallas_call | solution.py:215
  128.4 3.5 %last_32.1.refs_2_ = f32[64,2,16,128]{3,2,1,0:T(8,128)S(1)} custom-call(bf16[64,64,128]{2,1,0:T(8,128)(2,1)S(1)} %transfer_8.1.t_ref, f32[16,32,128]{2,1,0:T(8,128)S(1)} %level_7_32.1.c_ref, f32[16,32,128]{2,1,0:T(8,128)S(1)} %collective-permute-done.20.p_ref, f32[128,32,128]{2,1,0:T(8,128)S(1)} %target_matrix.1.m_ref), custom_call_target="tpu_custom_call" | custom-call | flops 134217728 | bytes 2097152 | tf_op jit(solution)/shard_map/last_32/pallas_call | solution.py:215
  131.9 3.5 %last_16.1.refs_1_ = f32[64,2,16,128]{3,2,1,0:T(8,128)S(1)} custom-call(bf16[64,64,128]{2,1,0:T(8,128)(2,1)S(1)} %transfer_8.1.t_ref, f32[16,32,128]{2,1,0:T(8,128)S(1)} %level_7_16.1.c_ref, f32[16,32,128]{2,1,0:T(8,128)S(1)} %collective-permute-done.13.p_ref, f32[128,32,128]{2,1,0:T(8,128)S(1)} %target_matrix.1.m_ref), custom_call_target="tpu_custom_call" | custom-call | flops 134217728 | bytes 2097152 | tf_op jit(solution)/shard_map/last_16/pallas_call | solution.py:215
  135.4 3.5 %last_0.1.refs_0_ = f32[64,2,16,128]{3,2,1,0:T(8,128)S(1)} custom-call(bf16[64,64,128]{2,1,0:T(8,128)(2,1)S(1)} %transfer_8.1.t_ref, f32[16,32,128]{2,1,0:T(8,128)S(1)} %level_7_0.1.c_ref, f32[16,32,128]{2,1,0:T(8,128)S(1)} %collective-permute-done.6.p_ref, f32[128,32,128]{2,1,0:T(8,128)S(1)} %target_matrix.1.m_ref), custom_call_target="tpu_custom_call" | custom-call | flops 134217728 | bytes 2097152 | tf_op jit(solution)/shard_map/last_0/pallas_call | solution.py:215
  138.8 4.2 %output.1 = f32[64,128,128]{2,1,0:T(8,128)} custom-call(f32[64,2,16,128]{3,2,1,0:T(8,128)S(1)} %last_0.1.refs_0_, f32[64,2,16,128]{3,2,1,0:T(8,128)S(1)} %last_16.1.refs_1_, f32[64,2,16,128]{3,2,1,0:T(8,128)S(1)} %last_32.1.refs_2_, f32[64,2,16,128]{3,2,1,0:T(8,128)S(1)} %last_48.1.refs_3_), custom_call_target="tpu_custom_call" | custom-call | tf_op jit(solution)/shard_map/output/pallas_call | solution.py:234
  (34 shorter events, 4.8 us)
Async XLA Ops:
  0.0 15.7 %copy-start = (f32[9,32,64,128]{3,2,1,0:T(8,128)S(1)}, f32[9,32,64,128]{3,2,1,0:T(8,128)}, u32[]{:S(2)}) copy-start(f32[9,32,64,128]{3,2,1,0:T(8,128)} %t_ref.15) | copy-start | bytes 28311556
  14.6 1.8 %collective-permute-start.21 = (f32[16,32,128]{2,1,0:T(8,128)S(1)}, f32[16,32,128]{2,1,0:T(8,128)S(1)}, u32[]{:S(2)}, u32[]{:S(2)}) collective-permute-start(f32[16,32,128]{2,1,0:T(8,128)S(1)} %get-tuple-element.12.c_ref), channel_id=1, source_target_pairs={{0,8},{8,0},{16,24},{24,16},{32,40},{40,32},{48,56},{56,48},{64,72... | collective-permute-start | bytes 786440 | tf_op jit(solution)/shard_map/ppermute | solution.py:267
  14.7 4.1 %collective-permute-start.14 = (f32[16,32,128]{2,1,0:T(8,128)S(1)}, f32[16,32,128]{2,1,0:T(8,128)S(1)}, u32[]{:S(2)}, u32[]{:S(2)}) collective-permute-start(f32[16,32,128]{2,1,0:T(8,128)S(1)} %get-tuple-element.11.c_ref), channel_id=1, source_target_pairs={{0,8},{8,0},{16,24},{24,16},{32,40},{40,32},{48,56},{56,48},{64,72... | collective-permute-start | bytes 786440 | tf_op jit(solution)/shard_map/ppermute | solution.py:267
  15.2 4.1 %collective-permute-start.7 = (f32[16,32,128]{2,1,0:T(8,128)S(1)}, f32[16,32,128]{2,1,0:T(8,128)S(1)}, u32[]{:S(2)}, u32[]{:S(2)}) collective-permute-start(f32[16,32,128]{2,1,0:T(8,128)S(1)} %get-tuple-element.10.c_ref), channel_id=1, source_target_pairs={{0,8},{8,0},{16,24},{24,16},{32,40},{40,32},{48,56},{56,48},{64,72... | collective-permute-start | bytes 786440 | tf_op jit(solution)/shard_map/ppermute | solution.py:267
  15.3 6.3 %collective-permute-start = (f32[16,32,128]{2,1,0:T(8,128)S(1)}, f32[16,32,128]{2,1,0:T(8,128)S(1)}, u32[]{:S(2)}, u32[]{:S(2)}) collective-permute-start(f32[16,32,128]{2,1,0:T(8,128)S(1)} %get-tuple-element.9.c_ref), channel_id=1, source_target_pairs={{0,8},{8,0},{16,24},{24,16},{32,40},{40,32},{48,56},{56,48},{64,72... | collective-permute-start | bytes 786440 | tf_op jit(solution)/shard_map/ppermute | solution.py:267
  16.7 9.2 %collective-permute-start.22 = (f32[16,32,128]{2,1,0:T(8,128)S(1)}, f32[16,32,128]{2,1,0:T(8,128)S(1)}, u32[]{:S(2)}, u32[]{:S(2)}) collective-permute-start(f32[16,32,128]{2,1,0:T(8,128)S(1)} %level_2_48.1.c_ref), channel_id=1, source_target_pairs={{0,16},{8,24},{16,0},{24,8},{32,48},{40,56},{48,32},{56,40},{64,80... | collective-permute-start | bytes 786440 | tf_op jit(solution)/shard_map/ppermute | solution.py:267
  19.1 12.4 %collective-permute-start.15 = (f32[16,32,128]{2,1,0:T(8,128)S(1)}, f32[16,32,128]{2,1,0:T(8,128)S(1)}, u32[]{:S(2)}, u32[]{:S(2)}) collective-permute-start(f32[16,32,128]{2,1,0:T(8,128)S(1)} %level_2_32.1.c_ref), channel_id=1, source_target_pairs={{0,16},{8,24},{16,0},{24,8},{32,48},{40,56},{48,32},{56,40},{64,80... | collective-permute-start | bytes 786440 | tf_op jit(solution)/shard_map/ppermute | solution.py:267
  19.5 17.6 %collective-permute-start.8 = (f32[16,32,128]{2,1,0:T(8,128)S(1)}, f32[16,32,128]{2,1,0:T(8,128)S(1)}, u32[]{:S(2)}, u32[]{:S(2)}) collective-permute-start(f32[16,32,128]{2,1,0:T(8,128)S(1)} %level_2_16.1.c_ref), channel_id=1, source_target_pairs={{0,16},{8,24},{16,0},{24,8},{32,48},{40,56},{48,32},{56,40},{64,80... | collective-permute-start | bytes 786440 | tf_op jit(solution)/shard_map/ppermute | solution.py:267
  21.9 20.9 %collective-permute-start.1 = (f32[16,32,128]{2,1,0:T(8,128)S(1)}, f32[16,32,128]{2,1,0:T(8,128)S(1)}, u32[]{:S(2)}, u32[]{:S(2)}) collective-permute-start(f32[16,32,128]{2,1,0:T(8,128)S(1)} %level_2_0.1.c_ref), channel_id=1, source_target_pairs={{0,16},{8,24},{16,0},{24,8},{32,48},{40,56},{48,32},{56,40},{64,80... | collective-permute-start | bytes 786440 | tf_op jit(solution)/shard_map/ppermute | solution.py:267
  26.2 25.8 %collective-permute-start.23 = (f32[16,32,128]{2,1,0:T(8,128)S(1)}, f32[16,32,128]{2,1,0:T(8,128)S(1)}, u32[]{:S(2)}, u32[]{:S(2)}) collective-permute-start(f32[16,32,128]{2,1,0:T(8,128)S(1)} %level_3_48.1.c_ref), channel_id=1, source_target_pairs={{0,32},{8,40},{16,48},{24,56},{32,0},{40,8},{48,16},{56,24},{64,96... | collective-permute-start | bytes 786440 | tf_op jit(solution)/shard_map/ppermute | solution.py:267
  31.9 25.8 %collective-permute-start.16 = (f32[16,32,128]{2,1,0:T(8,128)S(1)}, f32[16,32,128]{2,1,0:T(8,128)S(1)}, u32[]{:S(2)}, u32[]{:S(2)}) collective-permute-start(f32[16,32,128]{2,1,0:T(8,128)S(1)} %level_3_32.1.c_ref), channel_id=1, source_target_pairs={{0,32},{8,40},{16,48},{24,56},{32,0},{40,8},{48,16},{56,24},{64,96... | collective-permute-start | bytes 786440 | tf_op jit(solution)/shard_map/ppermute | solution.py:267
  37.5 25.8 %collective-permute-start.9 = (f32[16,32,128]{2,1,0:T(8,128)S(1)}, f32[16,32,128]{2,1,0:T(8,128)S(1)}, u32[]{:S(2)}, u32[]{:S(2)}) collective-permute-start(f32[16,32,128]{2,1,0:T(8,128)S(1)} %level_3_16.1.c_ref), channel_id=1, source_target_pairs={{0,32},{8,40},{16,48},{24,56},{32,0},{40,8},{48,16},{56,24},{64,96... | collective-permute-start | bytes 786440 | tf_op jit(solution)/shard_map/ppermute | solution.py:267
  43.1 24.9 %collective-permute-start.2 = (f32[16,32,128]{2,1,0:T(8,128)S(1)}, f32[16,32,128]{2,1,0:T(8,128)S(1)}, u32[]{:S(2)}, u32[]{:S(2)}) collective-permute-start(f32[16,32,128]{2,1,0:T(8,128)S(1)} %level_3_0.1.c_ref), channel_id=1, source_target_pairs={{0,32},{8,40},{16,48},{24,56},{32,0},{40,8},{48,16},{56,24},{64,96... | collective-permute-start | bytes 786440 | tf_op jit(solution)/shard_map/ppermute | solution.py:267
  52.3 20.0 %collective-permute-start.24 = (f32[16,32,128]{2,1,0:T(8,128)S(1)}, f32[16,32,128]{2,1,0:T(8,128)S(1)}, u32[]{:S(2)}, u32[]{:S(2)}) collective-permute-start(f32[16,32,128]{2,1,0:T(8,128)S(1)} %level_4_48.1.c_ref), channel_id=1, source_target_pairs={{0,64},{8,72},{16,80},{24,88},{32,96},{40,104},{48,112},{56,120},{... | collective-permute-start | bytes 786440 | tf_op jit(solution)/shard_map/ppermute | solution.py:267
  57.9 16.3 %collective-permute-start.17 = (f32[16,32,128]{2,1,0:T(8,128)S(1)}, f32[16,32,128]{2,1,0:T(8,128)S(1)}, u32[]{:S(2)}, u32[]{:S(2)}) collective-permute-start(f32[16,32,128]{2,1,0:T(8,128)S(1)} %level_4_32.1.c_ref), channel_id=1, source_target_pairs={{0,64},{8,72},{16,80},{24,88},{32,96},{40,104},{48,112},{56,120},{... | collective-permute-start | bytes 786440 | tf_op jit(solution)/shard_map/ppermute | solution.py:267
  63.5 11.6 %collective-permute-start.10 = (f32[16,32,128]{2,1,0:T(8,128)S(1)}, f32[16,32,128]{2,1,0:T(8,128)S(1)}, u32[]{:S(2)}, u32[]{:S(2)}) collective-permute-start(f32[16,32,128]{2,1,0:T(8,128)S(1)} %level_4_16.1.c_ref), channel_id=1, source_target_pairs={{0,64},{8,72},{16,80},{24,88},{32,96},{40,104},{48,112},{56,120},{... | collective-permute-start | bytes 786440 | tf_op jit(solution)/shard_map/ppermute | solution.py:267
  68.3 9.2 %collective-permute-start.3 = (f32[16,32,128]{2,1,0:T(8,128)S(1)}, f32[16,32,128]{2,1,0:T(8,128)S(1)}, u32[]{:S(2)}, u32[]{:S(2)}) collective-permute-start(f32[16,32,128]{2,1,0:T(8,128)S(1)} %level_4_0.1.c_ref), channel_id=1, source_target_pairs={{0,64},{8,72},{16,80},{24,88},{32,96},{40,104},{48,112},{56,120},{... | collective-permute-start | bytes 786440 | tf_op jit(solution)/shard_map/ppermute | solution.py:267
  72.6 9.3 %collective-permute-start.25 = (f32[16,32,128]{2,1,0:T(8,128)S(1)}, f32[16,32,128]{2,1,0:T(8,128)S(1)}, u32[]{:S(2)}, u32[]{:S(2)}) collective-permute-start(f32[16,32,128]{2,1,0:T(8,128)S(1)} %level_5_48.1.c_ref), channel_id=1, source_target_pairs={{0,1},{1,0},{2,3},{3,2},{4,5},{5,4},{6,7},{7,6},{8,9},{9,8},{10,11... | collective-permute-start | bytes 786440 | tf_op jit(solution)/shard_map/ppermute | solution.py:267
  74.5 13.1 %collective-permute-start.18 = (f32[16,32,128]{2,1,0:T(8,128)S(1)}, f32[16,32,128]{2,1,0:T(8,128)S(1)}, u32[]{:S(2)}, u32[]{:S(2)}) collective-permute-start(f32[16,32,128]{2,1,0:T(8,128)S(1)} %level_5_32.1.c_ref), channel_id=1, source_target_pairs={{0,1},{1,0},{2,3},{3,2},{4,5},{5,4},{6,7},{7,6},{8,9},{9,8},{10,11... | collective-permute-start | bytes 786440 | tf_op jit(solution)/shard_map/ppermute | solution.py:267
  75.4 17.8 %collective-permute-start.11 = (f32[16,32,128]{2,1,0:T(8,128)S(1)}, f32[16,32,128]{2,1,0:T(8,128)S(1)}, u32[]{:S(2)}, u32[]{:S(2)}) collective-permute-start(f32[16,32,128]{2,1,0:T(8,128)S(1)} %level_5_16.1.c_ref), channel_id=1, source_target_pairs={{0,1},{1,0},{2,3},{3,2},{4,5},{5,4},{6,7},{7,6},{8,9},{9,8},{10,11... | collective-permute-start | bytes 786440 | tf_op jit(solution)/shard_map/ppermute | solution.py:267
  77.8 21.0 %collective-permute-start.4 = (f32[16,32,128]{2,1,0:T(8,128)S(1)}, f32[16,32,128]{2,1,0:T(8,128)S(1)}, u32[]{:S(2)}, u32[]{:S(2)}) collective-permute-start(f32[16,32,128]{2,1,0:T(8,128)S(1)} %level_5_0.1.c_ref), channel_id=1, source_target_pairs={{0,1},{1,0},{2,3},{3,2},{4,5},{5,4},{6,7},{7,6},{8,9},{9,8},{10,11... | collective-permute-start | bytes 786440 | tf_op jit(solution)/shard_map/ppermute | solution.py:267
  82.2 24.4 %collective-permute-start.26 = (f32[16,32,128]{2,1,0:T(8,128)S(1)}, f32[16,32,128]{2,1,0:T(8,128)S(1)}, u32[]{:S(2)}, u32[]{:S(2)}) collective-permute-start(f32[16,32,128]{2,1,0:T(8,128)S(1)} %level_6_48.1.c_ref), channel_id=1, source_target_pairs={{0,2},{1,3},{2,0},{3,1},{4,6},{5,7},{6,4},{7,5},{8,10},{9,11},{10,... | collective-permute-start | bytes 786440 | tf_op jit(solution)/shard_map/ppermute | solution.py:267
  87.9 24.4 %collective-permute-start.19 = (f32[16,32,128]{2,1,0:T(8,128)S(1)}, f32[16,32,128]{2,1,0:T(8,128)S(1)}, u32[]{:S(2)}, u32[]{:S(2)}) collective-permute-start(f32[16,32,128]{2,1,0:T(8,128)S(1)} %level_6_32.1.c_ref), channel_id=1, source_target_pairs={{0,2},{1,3},{2,0},{3,1},{4,6},{5,7},{6,4},{7,5},{8,10},{9,11},{10,... | collective-permute-start | bytes 786440 | tf_op jit(solution)/shard_map/ppermute | solution.py:267
  93.5 24.4 %collective-permute-start.12 = (f32[16,32,128]{2,1,0:T(8,128)S(1)}, f32[16,32,128]{2,1,0:T(8,128)S(1)}, u32[]{:S(2)}, u32[]{:S(2)}) collective-permute-start(f32[16,32,128]{2,1,0:T(8,128)S(1)} %level_6_16.1.c_ref), channel_id=1, source_target_pairs={{0,2},{1,3},{2,0},{3,1},{4,6},{5,7},{6,4},{7,5},{8,10},{9,11},{10,... | collective-permute-start | bytes 786440 | tf_op jit(solution)/shard_map/ppermute | solution.py:267
  99.1 22.3 %collective-permute-start.5 = (f32[16,32,128]{2,1,0:T(8,128)S(1)}, f32[16,32,128]{2,1,0:T(8,128)S(1)}, u32[]{:S(2)}, u32[]{:S(2)}) collective-permute-start(f32[16,32,128]{2,1,0:T(8,128)S(1)} %level_6_0.1.c_ref), channel_id=1, source_target_pairs={{0,2},{1,3},{2,0},{3,1},{4,6},{5,7},{6,4},{7,5},{8,10},{9,11},{10,... | collective-permute-start | bytes 786440 | tf_op jit(solution)/shard_map/ppermute | solution.py:267
  106.9 18.0 %collective-permute-start.27 = (f32[16,32,128]{2,1,0:T(8,128)S(1)}, f32[16,32,128]{2,1,0:T(8,128)S(1)}, u32[]{:S(2)}, u32[]{:S(2)}) collective-permute-start(f32[16,32,128]{2,1,0:T(8,128)S(1)} %level_7_48.1.c_ref), channel_id=1, source_target_pairs={{0,4},{1,5},{2,6},{3,7},{4,0},{5,1},{6,2},{7,3},{8,12},{9,13},{10,... | collective-permute-start | bytes 786440 | tf_op jit(solution)/shard_map/ppermute | solution.py:267
  112.5 15.8 %collective-permute-start.20 = (f32[16,32,128]{2,1,0:T(8,128)S(1)}, f32[16,32,128]{2,1,0:T(8,128)S(1)}, u32[]{:S(2)}, u32[]{:S(2)}) collective-permute-start(f32[16,32,128]{2,1,0:T(8,128)S(1)} %level_7_32.1.c_ref), channel_id=1, source_target_pairs={{0,4},{1,5},{2,6},{3,7},{4,0},{5,1},{6,2},{7,3},{8,12},{9,13},{10,... | collective-permute-start | bytes 786440 | tf_op jit(solution)/shard_map/ppermute | solution.py:267
  118.2 13.7 %collective-permute-start.13 = (f32[16,32,128]{2,1,0:T(8,128)S(1)}, f32[16,32,128]{2,1,0:T(8,128)S(1)}, u32[]{:S(2)}, u32[]{:S(2)}) collective-permute-start(f32[16,32,128]{2,1,0:T(8,128)S(1)} %level_7_16.1.c_ref), channel_id=1, source_target_pairs={{0,4},{1,5},{2,6},{3,7},{4,0},{5,1},{6,2},{7,3},{8,12},{9,13},{10,... | collective-permute-start | bytes 786440 | tf_op jit(solution)/shard_map/ppermute | solution.py:267
  121.7 1.7 %copy-start.1 = (f32[128,32,128]{2,1,0:T(8,128)S(1)}, f32[128,32,128]{2,1,0:T(8,128)}, u32[]{:S(2)}) copy-start(f32[128,32,128]{2,1,0:T(8,128)} %ti_ref.1) | copy-start | bytes 6291460
  121.7 13.6 %collective-permute-start.6 = (f32[16,32,128]{2,1,0:T(8,128)S(1)}, f32[16,32,128]{2,1,0:T(8,128)S(1)}, u32[]{:S(2)}, u32[]{:S(2)}) collective-permute-start(f32[16,32,128]{2,1,0:T(8,128)S(1)} %level_7_0.1.c_ref), channel_id=1, source_target_pairs={{0,4},{1,5},{2,6},{3,7},{4,0},{5,1},{6,2},{7,3},{8,12},{9,13},{10,... | collective-permute-start | bytes 786440 | tf_op jit(solution)/shard_map/ppermute | solution.py:267

commit v2 on v1

v2 whole, which is shorter than its diff:
```python
import jax
import jax.numpy as jnp
from jax import lax
from jax.experimental import pallas as pl
from jax.experimental.pallas import tpu as pltpu
from jax.sharding import PartitionSpec as P

R, B, K, NB = 64, 128, 32, 128
HALF = NB // 2
CHUNKS = (16, 16, 16, 16)
MIB = 1 << 20
F32, BF16 = jnp.float32, jnp.bfloat16
VMEM = pl.BlockSpec(memory_space=pltpu.VMEM)
ANY = pl.BlockSpec(memory_space=pl.ANY)
NEAR_ZERO = pl.CostEstimate(flops=1, bytes_accessed=1, transcendentals=0)
STEP = (0, 1, -2, 0, 1, -3, -4, -5, -6, -7, -8, -9, 0, 2, 1, 3, 0, 2, 1, 3, 0, 2, 1, 3, 0, 2, 1, 3, 0, 2, 1, 3, 0, 2, 1, 3, 2, 3, 2, 3)
ORDER = [("step", i) if i >= 0 else ("prepare", -i) for i in STEP]


def in_vmem(*arrays):
    return [pltpu.with_memory_space_constraint(x, pltpu.VMEM) for x in arrays]


def in_hbm(*arrays):
    return [pltpu.with_memory_space_constraint(x, pltpu.HBM) for x in arrays]


def split(x):
    high = x.astype(BF16)
    return high, (x - high.astype(F32)).astype(BF16)


def low_lanes(shape):
    return lax.broadcasted_iota(jnp.int32, shape, len(shape) - 1) < HALF


def prepare_transfer(block, out_ref, k0):
    turned = [jnp.concatenate([block[i], block[i + 8]], 0).T for i in range(8)]
    mask = low_lanes((8, 8, NB))
    for g0 in range(0, NB, 8):
        v = jnp.swapaxes(jnp.stack([t[g0 : g0 + 8] for t in turned]), 0, 1)
        w = pltpu.roll(v, HALF, 2)
        vh = v.astype(BF16).astype(F32)
        wh = w.astype(BF16).astype(F32)
        first = jnp.where(mask, vh, w - wh)
        second = jnp.where(mask, wh, v - vh)
        gh, gl = divmod(g0, HALF)
        rows = jnp.concatenate([first, second], 1).astype(BF16)
        out_ref[gl : gl + 8, gh * K + k0 : gh * K + k0 + 16, :] = rows


def mix(weight, own, partner, mask):
    high, low = split(jnp.concatenate([own, partner], 0))
    both = jnp.concatenate([weight, weight], 1)
    s = jnp.dot(both, jnp.concatenate([high, high, low, low], 0), preferred_element_type=F32)
    return jnp.where(mask, s[:K], s[K:])


def source_prepare(sources, source_interp, transfer):
    def kernel(src_hbm, si_hbm, t_hbm, s_ref, m_ref, t0_ref, t1_ref, src, si, t, a_ref, src_sem, si_sem, t_sem):
        si_copy = [pltpu.make_async_copy(si_hbm.at[pl.ds(32 * i, 32)], si.at[pl.ds(32 * i, 32)], si_sem.at[i]) for i in range(4)]
        t_copy = [pltpu.make_async_copy(t_hbm.at[i], t.at[i], t_sem.at[i]) for i in range(2)]

        def src_copy(i):
            rows = pl.ds(pl.multiple_of(8 * i, 8), 8)
            return pltpu.make_async_copy(src_hbm.at[rows], src.at[rows], src_sem.at[i])

        for copy in si_copy + [src_copy(i) for i in range(8)] + t_copy:
            copy.start()
        for i in range(4):
            si_copy[i].wait()
            for b0 in range(32 * i, 32 * i + 32, 8):
                a_ref[:, b0 : b0 + 8, :] = jnp.swapaxes(si[b0 : b0 + 8], 0, 1)

        def turn(block, out_ref, first):
            turned = [block(j).T for j in range(8)]
            for g0 in range(0, NB, 8):
                out_ref[g0 : g0 + 8, pl.ds(first, 8), :] = jnp.swapaxes(jnp.stack([x[g0 : g0 + 8] for x in turned]), 0, 1)

        @pl.loop(0, K // 8)
        def _(i):
            k0 = pl.multiple_of(i * 8, 8)
            turn(lambda j: a_ref[k0 + j], m_ref, k0)

        @pl.loop(0, 8)
        def _(i):
            src_copy(i).wait()
            r0 = pl.multiple_of(i * 8, 8)
            turn(lambda j: src[r0 + j], s_ref, r0)

        for i, out_ref in enumerate((t0_ref, t1_ref)):
            t_copy[i].wait()
            for half in range(2):
                prepare_transfer(t.at[i, pl.ds(16 * half, 16)], out_ref, 16 * half)

    hbm = pl.BlockSpec(memory_space=pltpu.HBM)
    return pl.pallas_call(
        kernel,
        name="source_prepare",
        in_specs=[hbm] * 3,
        out_specs=[VMEM] * 4,
        out_shape=[pltpu.VMEM((NB, R, B), F32), pltpu.VMEM((NB, K, B), F32)] + [pltpu.VMEM((HALF, 2 * K, NB), BF16)] * 2,
        scratch_shapes=[
            pltpu.VMEM((R, B, NB), F32),
            pltpu.VMEM((B, K, NB), F32),
            pltpu.VMEM((2, K, 2 * K, NB), F32),
            pltpu.VMEM((K, B, NB), F32),
            pltpu.SemaphoreType.DMA((8,)),
            pltpu.SemaphoreType.DMA((4,)),
            pltpu.SemaphoreType.DMA((2,)),
        ],
        compiler_params=pltpu.CompilerParams(vmem_limit_bytes=14 * MIB),
    )(*in_hbm(sources, source_interp, transfer))


def source_stage(prepared, first, size, after):
    def kernel(s_ref, m_ref, t0_ref, t1_ref, _, o_ref, c_ref, d_ref):
        mask = low_lanes((K, NB))
        dims = (((1,), (1,)), ((), ()))
        for j in range(size):
            gl = first + j
            mh, ml = split(jnp.concatenate([m_ref[gl], m_ref[gl + HALF]], 0))
            sh, sl = split(jnp.concatenate([s_ref[gl], s_ref[gl + HALF]], 0))
            s = lax.dot_general(jnp.concatenate([mh, ml], 1), jnp.concatenate([sh, sh], 1), dims, preferred_element_type=F32)
            s = s + lax.dot_general(mh, sl, dims, preferred_element_type=F32)
            c_ref[j] = jnp.where(mask, s[:K], s[K:])
        for j in range(size):
            d_ref[j] = mix(t0_ref[first + j], c_ref[j], c_ref[j ^ 1], mask)
        for j in range(size):
            o_ref[j] = mix(t1_ref[first + j], d_ref[j], d_ref[j ^ 2], mask)

    return pl.pallas_call(
        kernel,
        name=f"source_{first}",
        in_specs=[VMEM] * 4 + [ANY],
        out_specs=VMEM,
        out_shape=pltpu.VMEM((size, K, NB), F32),
        scratch_shapes=[pltpu.VMEM((size, K, NB), F32)] * 2,
        compiler_params=pltpu.CompilerParams(vmem_limit_bytes=4 * MIB),
        cost_estimate=NEAR_ZERO,
    )(*in_vmem(*prepared, after))


def transfer_stage(transfer, level, after):
    def kernel(t_ref, _, o_ref):
        for i in range(2):
            prepare_transfer(t_ref.at[level, pl.ds(16 * i, 16)], o_ref, 16 * i)

    return pl.pallas_call(
        kernel,
        name=f"transfer_{level}",
        in_specs=[VMEM, ANY],
        out_specs=VMEM,
        out_shape=pltpu.VMEM((HALF, 2 * K, NB), BF16),
        compiler_params=pltpu.CompilerParams(vmem_limit_bytes=4 * MIB),
        cost_estimate=NEAR_ZERO,
    )(*in_vmem(transfer, after))


def target_matrix_kernel(ti_ref, _, o_ref, a_ref):
    for b0 in range(0, B, 8):
        a_ref[:, b0 : b0 + 8, :] = jnp.swapaxes(ti_ref[b0 : b0 + 8], 0, 1)

    @pl.loop(0, K // 8)
    def _(i):
        k0 = pl.multiple_of(i * 8, 8)
        turned = [a_ref[k0 + j].T for j in range(8)]
        for g0 in range(0, NB, 8):
            v = jnp.swapaxes(jnp.stack([t[g0 : g0 + 8] for t in turned]), 0, 1)
            o_ref[g0 : g0 + 8, pl.ds(k0, 8), :] = v


def target_matrix_stage(target_interp, after):
    return pl.pallas_call(
        target_matrix_kernel,
        name="target_matrix",
        in_specs=[VMEM, ANY],
        out_specs=VMEM,
        out_shape=pltpu.VMEM((NB, K, B), F32),
        scratch_shapes=[pltpu.VMEM((K, B, NB), F32)],
        compiler_params=pltpu.CompilerParams(vmem_limit_bytes=6 * MIB),
        cost_estimate=NEAR_ZERO,
    )(*in_vmem(target_interp, after))


def level_stage(weights, own, partner, first, level, after):
    size = own.shape[0]

    def kernel(t_ref, c_ref, p_ref, _, o_ref):
        mask = low_lanes((K, NB))
        for j in range(size):
            o_ref[j] = mix(t_ref[first + j], c_ref[j], p_ref[j], mask)

    return pl.pallas_call(
        kernel,
        name=f"level_{level}_{first}",
        in_specs=[VMEM] * 3 + [ANY],
        out_specs=VMEM,
        out_shape=pltpu.VMEM((size, K, NB), F32),
        compiler_params=pltpu.CompilerParams(vmem_limit_bytes=2 * MIB),
        cost_estimate=NEAR_ZERO,
    )(*in_vmem(weights, own, partner, after))


def last_stage(weights, own, partner, matrix, first, after):
    size = own.shape[0]

    def kernel(t_ref, c_ref, p_ref, m_ref, _, o_ref, d_ref, v_ref):
        mask = low_lanes((K, NB))
        for j in range(size):
            d_ref[j] = mix(t_ref[first + j], c_ref[j], p_ref[j], mask)
        for j in range(size):
            gl = first + j
            high, low = split(d_ref[j])
            left = jnp.concatenate([high, low, high, low], 0).T
            for gh in range(2):
                th, tl = split(m_ref[gh * HALF + gl])
                right = jnp.concatenate([th, th, tl, tl], 0)
                v_ref[gh, j] = jnp.dot(left[gh * R : gh * R + R], right, preferred_element_type=F32)
        for gh in range(2):
            for j0 in range(0, size, 8):
                for r0 in range(0, R, 8):
                    o_ref[r0 : r0 + 8, gh, j0 : j0 + 8, :] = jnp.swapaxes(v_ref[gh, j0 : j0 + 8, r0 : r0 + 8, :], 0, 1)

    return pl.pallas_call(
        kernel,
        name=f"last_{first}",
        in_specs=[VMEM] * 4 + [ANY],
        out_specs=VMEM,
        out_shape=pltpu.VMEM((R, 2, size, B), F32),
        scratch_shapes=[pltpu.VMEM((size, K, NB), F32), pltpu.VMEM((2, size, R, B), F32)],
        compiler_params=pltpu.CompilerParams(vmem_limit_bytes=4 * MIB),
        cost_estimate=NEAR_ZERO,
    )(*in_vmem(weights, own, partner, matrix, after))


def output_stage(parts):
    def kernel(*refs):
        ins, (o_hbm, o_ref, sem) = refs[:-3], refs[-3:]

        def copy(i):
            rows = pl.ds(pl.multiple_of(8 * i, 8), 8)
            return pltpu.make_async_copy(o_ref.at[rows], o_hbm.at[rows], sem.at[i])

        @pl.loop(0, 8)
        def _(i):
            for j in range(8):
                r = i * 8 + j
                o_ref[r] = jnp.concatenate([ref[r, gh] for gh in range(2) for ref in ins], 0).T
            copy(i).start()

        @pl.loop(0, 8)
        def _(i):
            copy(i).wait()

    return pl.pallas_call(
        kernel,
        name="output",
        in_specs=[VMEM] * len(parts),
        out_specs=pl.BlockSpec(memory_space=pltpu.HBM),
        out_shape=pltpu.HBM((R, B, NB), F32),
        scratch_shapes=[pltpu.VMEM((R, B, NB), F32), pltpu.SemaphoreType.DMA((8,))],
        compiler_params=pltpu.CompilerParams(vmem_limit_bytes=6 * MIB),
    )(*in_vmem(*parts))


def device_program(exchange, sources, source_interp, target_interp, transfer):
    prepared = source_prepare(sources, source_interp, transfer)
    count = len(CHUNKS)
    firsts = [sum(CHUNKS[:i]) for i in range(count)]
    weights, parts = {}, {}
    level, own, partner = [1] * count, [None] * count, [None] * count
    after = prepared[2]
    for kind, index in ORDER:
        if kind == "prepare":
            if index == 9:
                after = weights[9] = target_matrix_stage(target_interp, after)
            else:
                after = weights[index] = transfer_stage(transfer, index, after)
            continue
        first, size, n = firsts[index], CHUNKS[index], level[index]
        if n == 8:
            after = parts[index] = last_stage(weights[8], own[index], partner[index], weights[9], first, after)
            continue
        if n == 1:
            after = source_stage(prepared, first, size, after)
        else:
            after = level_stage(weights[n], own[index], partner[index], first, n, after)
        own[index], level[index] = after, n + 1
        partner[index] = exchange(after, n + 1)
    return output_stage([parts[i] for i in range(count)])


def solution(mesh):
    n_src, n_tgt = mesh.shape["src"], mesh.shape["tgt"]

    def exchange(c, level):
        if level < 6:
            axis, size, bit = "src", n_src, level - 2
        else:
            axis, size, bit = "tgt", n_tgt, level - 6
        return lax.ppermute(c, axis, [(i, i ^ (1 << bit)) for i in range(size)])

    def program(*args):
        return device_program(exchange, *args)

    blocks = ("src", "tgt")
    return jax.shard_map(
        program,
        mesh=mesh,
        in_specs=(P(None, None, blocks), P(None, None, blocks), P(None, None, blocks), P(None, None, None, blocks)),
        out_specs=P(None, None, blocks),
        check_vma=False,
    )
```

time: 143 us -> 109 us (0.76)
  Pallas kernels: 46.2 us -> 31.5 us
  starting transfers between devices: 56.1 us -> 44.2 us
  waiting for transfers between devices: 40.4 us -> 30.6 us
  local copies, waits for them, and re-layouts: 0.01 us -> 1.65 us
    pallas_call x13 -> x17, Pallas kernels: 37.7 us -> 22.9 us  [the longest x1 7.69 us: source_prepare(): pl.pallas_call(kernel, name='source_prepare', in_specs=[hbm] * 3, out_spe...]
    ppermute x28, starting transfers between devices: 56.1 us -> 44.2 us  [exchange(): return lax.ppermute(c, axis, [(i, i ^ 1 << bit) for i in range(size)])]
    ppermute x28, waiting for transfers between devices: 40.4 us -> 30.6 us  [exchange(): return lax.ppermute(c, axis, [(i, i ^ 1 << bit) for i in range(size)])]
    unnamed x4 -> x8, local copies, waits for them, and re-layouts: 0.01 us -> 1.65 us
  transfers between devices with their start and end apart: 28 -> 28, of which waited for: 17 -> 14; matrix products, arithmetic and copies ran while one was open for 0% -> 0% of each run, Pallas kernels for 17% -> 18%
where the time goes in v2:
time: 109 us
  starting transfers between devices  44.2 us (41%)
  Pallas kernels  31.5 us (29%)
  waiting for transfers between devices  30.6 us (28%)
  local copies, waits for them, and re-layouts  1.65 us (2%)
    ppermute x28, starting transfers between devices, exchange(): return lax.ppermute(c, axis, [(i, i ^ 1 << bit) for i in range(size)])  44.2 us
    ppermute x28, waiting for transfers between devices, exchange(): return lax.ppermute(c, axis, [(i, i ^ 1 << bit) for i in range(size)])  30.6 us
    pallas_call x1, Pallas kernels, source_prepare(): pl.pallas_call(kernel, name='source_prepare', in_specs=[hbm] * 3, out_spe...  7.69 us
    pallas_call x24, Pallas kernels, level_stage(): pl.pallas_call(kernel, name=f'level_{level}_{first}', in_specs=[VMEM] * 3...  7.09 us
    pallas_call x7, Pallas kernels, transfer_stage(): pl.pallas_call(kernel, name=f'transfer_{level}', in_specs=[VMEM, ANY], ou...  5.08 us
    pallas_call x4, Pallas kernels, source_stage(): pl.pallas_call(kernel, name=f'source_{first}', in_specs=[VMEM] * 4 + [ANY...  4.81 us
    pallas_call x4, Pallas kernels, last_stage(): pl.pallas_call(kernel, name=f'last_{first}', in_specs=[VMEM] * 4 + [ANY],...  2.87 us
    pallas_call x1, Pallas kernels, output_stage(): pl.pallas_call(kernel, name='output', in_specs=[VMEM] * len(parts), out_s...  2.49 us
  transfers between devices with their start and end apart: 28, of which 14 were waited for; matrix products, arithmetic and copies ran while one was open for 0% of the time, Pallas kernels for 18%

profile of v2, /device:TPU:0, one launch (start us, length us, event | category | flops | bytes accessed | tf_op | source)
XLA Modules:
  0.0 108.6 jit_solution(661217160205255156)
XLA Ops:
  0.0 7.7 %source_prepare.1 = (f32[128,64,128]{2,1,0:T(8,128)S(1)}, f32[128,32,128]{2,1,0:T(8,128)S(1)}, bf16[64,64,128]{2,1,0:T(8,128)(2,1)S(1)}, bf16[64,64,128]{2,1,0:T(8,128)(2,1)S(1)}) custom-call(f32[64,128,128]{2,1,0:T(8,128)} %src_hbm.1, f32[128,32,128]{2,1,0:T(8,128)} %si_hbm.1, f32[9,32,64,128]{3,2,1,0:T(8,128)} %t_ref.13), custom_call_target="tpu_custom_call" | custom-call | tf_op jit(solution)/shard_map/source_prepare/pallas_call | solution.py:97
  7.7 1.2 %source_0.1._.c_ref = f32[16,32,128]{2,1,0:T(8,128)S(1)} custom-call(f32[128,64,128]{2,1,0:T(8,128)S(1)} %get-tuple-element.9.s_ref, f32[128,32,128]{2,1,0:T(8,128)S(1)} %get-tuple-element.10.m_ref, bf16[64,64,128]{2,1,0:T(8,128)(2,1)S(1)} %get-tuple-element.11.t0_ref._, bf16[64,64,128]{2,1,0:T(8,128)(2,1)S(1)} %get-tuple-element.12.t1_ref, ...), custom_call_target="tpu_custom_call" | custom-call | flops 1 | bytes 1 | tf_op jit(solution)/shard_map/source_0/pallas_call | solution.py:132
  9.0 1.2 %source_16.1._.c_ref = f32[16,32,128]{2,1,0:T(8,128)S(1)} custom-call(f32[128,64,128]{2,1,0:T(8,128)S(1)} %get-tuple-element.9.s_ref, f32[128,32,128]{2,1,0:T(8,128)S(1)} %get-tuple-element.10.m_ref, bf16[64,64,128]{2,1,0:T(8,128)(2,1)S(1)} %get-tuple-element.11.t0_ref._, bf16[64,64,128]{2,1,0:T(8,128)(2,1)S(1)} %get-tuple-element.12.t1_ref, ...), custom_call_target="tpu_custom_call" | custom-call | flops 1 | bytes 1 | tf_op jit(solution)/shard_map/source_16/pallas_call | solution.py:132
  10.3 0.6 collective-permute-start
  10.8 0.3 slice-done.1
  11.2 0.4 slice-done.2
  11.6 0.7 transfer_2.1.t_ref._
  12.4 0.3 level_2_0.1._.c_ref
  12.7 2.1 %collective-permute-start.2 = (f32[16,32,128]{2,1,0:T(8,128)S(1)}, f32[16,32,128]{2,1,0:T(8,128)S(1)}, u32[]{:S(2)}, u32[]{:S(2)}) collective-permute-start(f32[16,32,128]{2,1,0:T(8,128)S(1)} %level_2_0.1._.c_ref), channel_id=1, source_target_pairs={{0,16},{8,24},{16,0},{24,8},{32,48},{40,56},{48,32},{56,40},{64,80... | collective-permute-start | bytes 786440 | tf_op jit(solution)/shard_map/ppermute | solution.py:302
  14.7 0.3 level_2_16.1._.c_ref
  15.2 0.7 transfer_3.1._.t_ref
  15.9 0.7 transfer_4.1._.t_ref
  16.6 0.7 transfer_5.1._.t_ref
  17.4 0.7 transfer_6.1._.t_ref
  18.1 0.7 transfer_7.1._.t_ref
  18.8 0.7 transfer_8.1._.t_ref
  19.6 0.8 copy-done
  20.4 1.4 %target_matrix.1._.m_ref = f32[128,32,128]{2,1,0:T(8,128)S(1)} custom-call(f32[128,32,128]{2,1,0:T(8,128)S(1)} %copy-done, bf16[64,64,128]{2,1,0:T(8,128)(2,1)S(1)} %transfer_8.1._.t_ref), custom_call_target="tpu_custom_call" | custom-call | flops 1 | bytes 1 | tf_op jit(solution)/shard_map/target_matrix/pallas_call | solution.py:174
  22.2 4.3 %collective-permute-start.3 = (f32[16,32,128]{2,1,0:T(8,128)S(1)}, f32[16,32,128]{2,1,0:T(8,128)S(1)}, u32[]{:S(2)}, u32[]{:S(2)}) collective-permute-start(f32[16,32,128]{2,1,0:T(8,128)S(1)} %level_3_0.1._.c_ref), channel_id=1, source_target_pairs={{0,32},{8,40},{16,48},{24,56},{32,0},{40,8},{48,16},{56,24},{64,96... | collective-permute-start | bytes 786440 | tf_op jit(solution)/shard_map/ppermute | solution.py:302
  26.5 1.2 %source_32.1._.c_ref = f32[16,32,128]{2,1,0:T(8,128)S(1)} custom-call(f32[128,64,128]{2,1,0:T(8,128)S(1)} %get-tuple-element.9.s_ref, f32[128,32,128]{2,1,0:T(8,128)S(1)} %get-tuple-element.10.m_ref, bf16[64,64,128]{2,1,0:T(8,128)(2,1)S(1)} %get-tuple-element.11.t0_ref._, bf16[64,64,128]{2,1,0:T(8,128)(2,1)S(1)} %get-tuple-element.12.t1_ref, ...), custom_call_target="tpu_custom_call" | custom-call | flops 1 | bytes 1 | tf_op jit(solution)/shard_map/source_32/pallas_call | solution.py:132
  28.1 3.8 %collective-permute-start.7 = (f32[16,32,128]{2,1,0:T(8,128)S(1)}, f32[16,32,128]{2,1,0:T(8,128)S(1)}, u32[]{:S(2)}, u32[]{:S(2)}) collective-permute-start(f32[16,32,128]{2,1,0:T(8,128)S(1)} %level_3_16.1._.c_ref), channel_id=1, source_target_pairs={{0,32},{8,40},{16,48},{24,56},{32,0},{40,8},{48,16},{56,24},{64,96... | collective-permute-start | bytes 786440 | tf_op jit(solution)/shard_map/ppermute | solution.py:302
  31.9 1.2 %source_48.1._.c_ref = f32[16,32,128]{2,1,0:T(8,128)S(1)} custom-call(f32[128,64,128]{2,1,0:T(8,128)S(1)} %get-tuple-element.9.s_ref, f32[128,32,128]{2,1,0:T(8,128)S(1)} %get-tuple-element.10.m_ref, bf16[64,64,128]{2,1,0:T(8,128)(2,1)S(1)} %get-tuple-element.11.t0_ref._, bf16[64,64,128]{2,1,0:T(8,128)(2,1)S(1)} %get-tuple-element.12.t1_ref, ...), custom_call_target="tpu_custom_call" | custom-call | flops 1 | bytes 1 | tf_op jit(solution)/shard_map/source_48/pallas_call | solution.py:132
  33.2 3.5 %collective-permute-done.3.p_ref = f32[16,32,128]{2,1,0:T(8,128)S(1)} collective-permute-done((f32[16,32,128]{2,1,0:T(8,128)S(1)}, f32[16,32,128]{2,1,0:T(8,128)S(1)}, u32[]{:S(2)}, u32[]{:S(2)}) %collective-permute-start.3) | collective-permute-done | bytes 262176 | tf_op jit(solution)/shard_map/ppermute | solution.py:302
  37.0 3.3 %collective-permute-start.5 = (f32[16,32,128]{2,1,0:T(8,128)S(1)}, f32[16,32,128]{2,1,0:T(8,128)S(1)}, u32[]{:S(2)}, u32[]{:S(2)}) collective-permute-start(f32[16,32,128]{2,1,0:T(8,128)S(1)} %level_4_0.1._.c_ref), channel_id=1, source_target_pairs={{0,64},{8,72},{16,80},{24,88},{32,96},{40,104},{48,112},{56,120},{... | collective-permute-start | bytes 786440 | tf_op jit(solution)/shard_map/ppermute | solution.py:302
  40.7 1.6 %collective-permute-done.7.p_ref = f32[16,32,128]{2,1,0:T(8,128)S(1)} collective-permute-done((f32[16,32,128]{2,1,0:T(8,128)S(1)}, f32[16,32,128]{2,1,0:T(8,128)S(1)}, u32[]{:S(2)}, u32[]{:S(2)}) %collective-permute-start.7) | collective-permute-done | bytes 262176 | tf_op jit(solution)/shard_map/ppermute | solution.py:302
  42.3 0.3 level_4_16.1._.c_ref
  42.6 3.3 %collective-permute-start.11 = (f32[16,32,128]{2,1,0:T(8,128)S(1)}, f32[16,32,128]{2,1,0:T(8,128)S(1)}, u32[]{:S(2)}, u32[]{:S(2)}) collective-permute-start(f32[16,32,128]{2,1,0:T(8,128)S(1)} %level_4_16.1._.c_ref), channel_id=1, source_target_pairs={{0,64},{8,72},{16,80},{24,88},{32,96},{40,104},{48,112},{56,120},{... | collective-permute-start | bytes 786440 | tf_op jit(solution)/shard_map/ppermute | solution.py:302
  46.3 0.3 level_5_0.1._.c_ref
  46.6 1.6 %collective-permute-start.9 = (f32[16,32,128]{2,1,0:T(8,128)S(1)}, f32[16,32,128]{2,1,0:T(8,128)S(1)}, u32[]{:S(2)}, u32[]{:S(2)}) collective-permute-start(f32[16,32,128]{2,1,0:T(8,128)S(1)} %level_5_0.1._.c_ref), channel_id=1, source_target_pairs={{0,1},{1,0},{2,3},{3,2},{4,5},{5,4},{6,7},{7,6},{8,9},{9,8},{10,11... | collective-permute-start | bytes 786440 | tf_op jit(solution)/shard_map/ppermute | solution.py:302
  48.5 0.9 collective-permute-start.16
  49.4 1.2 %collective-permute-done.11.p_ref = f32[16,32,128]{2,1,0:T(8,128)S(1)} collective-permute-done((f32[16,32,128]{2,1,0:T(8,128)S(1)}, f32[16,32,128]{2,1,0:T(8,128)S(1)}, u32[]{:S(2)}, u32[]{:S(2)}) %collective-permute-start.11) | collective-permute-done | bytes 262176 | tf_op jit(solution)/shard_map/ppermute | solution.py:302
  50.9 1.6 %collective-permute-start.15 = (f32[16,32,128]{2,1,0:T(8,128)S(1)}, f32[16,32,128]{2,1,0:T(8,128)S(1)}, u32[]{:S(2)}, u32[]{:S(2)}) collective-permute-start(f32[16,32,128]{2,1,0:T(8,128)S(1)} %level_5_16.1._.c_ref), channel_id=1, source_target_pairs={{0,1},{1,0},{2,3},{3,2},{4,5},{5,4},{6,7},{7,6},{8,9},{9,8},{10,11... | collective-permute-start | bytes 786440 | tf_op jit(solution)/shard_map/ppermute | solution.py:302
  52.5 3.1 %collective-permute-done.10.p_ref = f32[16,32,128]{2,1,0:T(8,128)S(1)} collective-permute-done((f32[16,32,128]{2,1,0:T(8,128)S(1)}, f32[16,32,128]{2,1,0:T(8,128)S(1)}, u32[]{:S(2)}, u32[]{:S(2)}) %collective-permute-start.10) | collective-permute-done | bytes 262176 | tf_op jit(solution)/shard_map/ppermute | solution.py:302
  56.0 0.3 level_6_0.1._.c_ref
  56.3 3.1 %collective-permute-start.13 = (f32[16,32,128]{2,1,0:T(8,128)S(1)}, f32[16,32,128]{2,1,0:T(8,128)S(1)}, u32[]{:S(2)}, u32[]{:S(2)}) collective-permute-start(f32[16,32,128]{2,1,0:T(8,128)S(1)} %level_6_0.1._.c_ref), channel_id=1, source_target_pairs={{0,2},{1,3},{2,0},{3,1},{4,6},{5,7},{6,4},{7,5},{8,10},{9,11},{10,... | collective-permute-start | bytes 786440 | tf_op jit(solution)/shard_map/ppermute | solution.py:302
  59.4 0.5 collective-permute-done.16.p_ref
  60.2 2.6 %collective-permute-start.20 = (f32[16,32,128]{2,1,0:T(8,128)S(1)}, f32[16,32,128]{2,1,0:T(8,128)S(1)}, u32[]{:S(2)}, u32[]{:S(2)}) collective-permute-start(f32[16,32,128]{2,1,0:T(8,128)S(1)} %level_4_32.1._.c_ref), channel_id=1, source_target_pairs={{0,64},{8,72},{16,80},{24,88},{32,96},{40,104},{48,112},{56,120},{... | collective-permute-start | bytes 786440 | tf_op jit(solution)/shard_map/ppermute | solution.py:302
  63.1 3.1 %collective-permute-start.19 = (f32[16,32,128]{2,1,0:T(8,128)S(1)}, f32[16,32,128]{2,1,0:T(8,128)S(1)}, u32[]{:S(2)}, u32[]{:S(2)}) collective-permute-start(f32[16,32,128]{2,1,0:T(8,128)S(1)} %level_6_16.1._.c_ref), channel_id=1, source_target_pairs={{0,2},{1,3},{2,0},{3,1},{4,6},{5,7},{6,4},{7,5},{8,10},{9,11},{10,... | collective-permute-start | bytes 786440 | tf_op jit(solution)/shard_map/ppermute | solution.py:302
  66.5 1.1 %collective-permute-start.18 = (f32[16,32,128]{2,1,0:T(8,128)S(1)}, f32[16,32,128]{2,1,0:T(8,128)S(1)}, u32[]{:S(2)}, u32[]{:S(2)}) collective-permute-start(f32[16,32,128]{2,1,0:T(8,128)S(1)} %level_4_48.1._.c_ref), channel_id=1, source_target_pairs={{0,64},{8,72},{16,80},{24,88},{32,96},{40,104},{48,112},{56,120},{... | collective-permute-start | bytes 786440 | tf_op jit(solution)/shard_map/ppermute | solution.py:302
  67.6 0.6 collective-permute-done.13.p_ref
  68.2 0.3 level_7_0.1._.c_ref
  68.5 1.2 %collective-permute-start.17 = (f32[16,32,128]{2,1,0:T(8,128)S(1)}, f32[16,32,128]{2,1,0:T(8,128)S(1)}, u32[]{:S(2)}, u32[]{:S(2)}) collective-permute-start(f32[16,32,128]{2,1,0:T(8,128)S(1)} %level_7_0.1._.c_ref), channel_id=1, source_target_pairs={{0,4},{1,5},{2,6},{3,7},{4,0},{5,1},{6,2},{7,3},{8,12},{9,13},{10,... | collective-permute-start | bytes 786440 | tf_op jit(solution)/shard_map/ppermute | solution.py:302
  69.7 0.3 level_5_32.1._.c_ref
  70.0 1.0 collective-permute-start.22
  71.0 1.3 %collective-permute-done.19.p_ref = f32[16,32,128]{2,1,0:T(8,128)S(1)} collective-permute-done((f32[16,32,128]{2,1,0:T(8,128)S(1)}, f32[16,32,128]{2,1,0:T(8,128)S(1)}, u32[]{:S(2)}, u32[]{:S(2)}) %collective-permute-start.19) | collective-permute-done | bytes 262176 | tf_op jit(solution)/shard_map/ppermute | solution.py:302
  72.6 1.7 %collective-permute-start.21 = (f32[16,32,128]{2,1,0:T(8,128)S(1)}, f32[16,32,128]{2,1,0:T(8,128)S(1)}, u32[]{:S(2)}, u32[]{:S(2)}) collective-permute-start(f32[16,32,128]{2,1,0:T(8,128)S(1)} %level_7_16.1._.c_ref), channel_id=1, source_target_pairs={{0,4},{1,5},{2,6},{3,7},{4,0},{5,1},{6,2},{7,3},{8,12},{9,13},{10,... | collective-permute-start | bytes 786440 | tf_op jit(solution)/shard_map/ppermute | solution.py:302
  74.3 3.0 %collective-permute-done.18.p_ref = f32[16,32,128]{2,1,0:T(8,128)S(1)} collective-permute-done((f32[16,32,128]{2,1,0:T(8,128)S(1)}, f32[16,32,128]{2,1,0:T(8,128)S(1)}, u32[]{:S(2)}, u32[]{:S(2)}) %collective-permute-start.18) | collective-permute-done | bytes 262176 | tf_op jit(solution)/shard_map/ppermute | solution.py:302
  77.6 0.9 collective-permute-start.24
  78.5 3.3 %collective-permute-done.17.p_ref = f32[16,32,128]{2,1,0:T(8,128)S(1)} collective-permute-done((f32[16,32,128]{2,1,0:T(8,128)S(1)}, f32[16,32,128]{2,1,0:T(8,128)S(1)}, u32[]{:S(2)}, u32[]{:S(2)}) %collective-permute-start.17) | collective-permute-done | bytes 262176 | tf_op jit(solution)/shard_map/ppermute | solution.py:302
  81.8 0.7 last_0.1._.refs_0_
  82.6 0.3 level_6_32.1._.c_ref
  82.9 2.0 %collective-permute-start.23 = (f32[16,32,128]{2,1,0:T(8,128)S(1)}, f32[16,32,128]{2,1,0:T(8,128)S(1)}, u32[]{:S(2)}, u32[]{:S(2)}) collective-permute-start(f32[16,32,128]{2,1,0:T(8,128)S(1)} %level_6_32.1._.c_ref), channel_id=1, source_target_pairs={{0,2},{1,3},{2,0},{3,1},{4,6},{5,7},{6,4},{7,5},{8,10},{9,11},{10,... | collective-permute-start | bytes 786440 | tf_op jit(solution)/shard_map/ppermute | solution.py:302
  84.9 0.7 last_16.1._.refs_1_
  86.1 2.7 %collective-permute-start.26 = (f32[16,32,128]{2,1,0:T(8,128)S(1)}, f32[16,32,128]{2,1,0:T(8,128)S(1)}, u32[]{:S(2)}, u32[]{:S(2)}) collective-permute-start(f32[16,32,128]{2,1,0:T(8,128)S(1)} %level_6_48.1._.c_ref), channel_id=1, source_target_pairs={{0,2},{1,3},{2,0},{3,1},{4,6},{5,7},{6,4},{7,5},{8,10},{9,11},{10,... | collective-permute-start | bytes 786440 | tf_op jit(solution)/shard_map/ppermute | solution.py:302
  88.8 4.8 %collective-permute-done.23.p_ref = f32[16,32,128]{2,1,0:T(8,128)S(1)} collective-permute-done((f32[16,32,128]{2,1,0:T(8,128)S(1)}, f32[16,32,128]{2,1,0:T(8,128)S(1)}, u32[]{:S(2)}, u32[]{:S(2)}) %collective-permute-start.23) | collective-permute-done | bytes 262176 | tf_op jit(solution)/shard_map/ppermute | solution.py:302
  93.6 0.3 level_7_32.1._.c_ref
  93.9 1.4 %collective-permute-start.25 = (f32[16,32,128]{2,1,0:T(8,128)S(1)}, f32[16,32,128]{2,1,0:T(8,128)S(1)}, u32[]{:S(2)}, u32[]{:S(2)}) collective-permute-start(f32[16,32,128]{2,1,0:T(8,128)S(1)} %level_7_32.1._.c_ref), channel_id=1, source_target_pairs={{0,4},{1,5},{2,6},{3,7},{4,0},{5,1},{6,2},{7,3},{8,12},{9,13},{10,... | collective-permute-start | bytes 786440 | tf_op jit(solution)/shard_map/ppermute | solution.py:302
  95.4 1.1 %collective-permute-done.26.p_ref = f32[16,32,128]{2,1,0:T(8,128)S(1)} collective-permute-done((f32[16,32,128]{2,1,0:T(8,128)S(1)}, f32[16,32,128]{2,1,0:T(8,128)S(1)}, u32[]{:S(2)}, u32[]{:S(2)}) %collective-permute-start.26) | collective-permute-done | bytes 262176 | tf_op jit(solution)/shard_map/ppermute | solution.py:302
  96.8 1.5 %collective-permute-start.27 = (f32[16,32,128]{2,1,0:T(8,128)S(1)}, f32[16,32,128]{2,1,0:T(8,128)S(1)}, u32[]{:S(2)}, u32[]{:S(2)}) collective-permute-start(f32[16,32,128]{2,1,0:T(8,128)S(1)} %level_7_48.1._.c_ref), channel_id=1, source_target_pairs={{0,4},{1,5},{2,6},{3,7},{4,0},{5,1},{6,2},{7,3},{8,12},{9,13},{10,... | collective-permute-start | bytes 786440 | tf_op jit(solution)/shard_map/ppermute | solution.py:302
  98.2 4.1 %collective-permute-done.25.p_ref = f32[16,32,128]{2,1,0:T(8,128)S(1)} collective-permute-done((f32[16,32,128]{2,1,0:T(8,128)S(1)}, f32[16,32,128]{2,1,0:T(8,128)S(1)}, u32[]{:S(2)}, u32[]{:S(2)}) %collective-permute-start.25) | collective-permute-done | bytes 262176 | tf_op jit(solution)/shard_map/ppermute | solution.py:302
  102.4 0.7 last_32.1._.refs_2_
  103.1 2.1 %collective-permute-done.27.p_ref = f32[16,32,128]{2,1,0:T(8,128)S(1)} collective-permute-done((f32[16,32,128]{2,1,0:T(8,128)S(1)}, f32[16,32,128]{2,1,0:T(8,128)S(1)}, u32[]{:S(2)}, u32[]{:S(2)}) %collective-permute-start.27) | collective-permute-done | bytes 262176 | tf_op jit(solution)/shard_map/ppermute | solution.py:302
  105.2 0.7 last_48.1.refs_3_
  105.9 2.5 %output.1 = f32[64,128,128]{2,1,0:T(8,128)} custom-call(f32[64,2,16,128]{3,2,1,0:T(8,128)S(1)} %last_0.1._.refs_0_, f32[64,2,16,128]{3,2,1,0:T(8,128)S(1)} %last_16.1._.refs_1_, f32[64,2,16,128]{3,2,1,0:T(8,128)S(1)} %last_32.1._.refs_2_, f32[64,2,16,128]{3,2,1,0:T(8,128)S(1)} %last_48.1.refs_3_), custom_call_target="tpu_custom_call" | custom-call | tf_op jit(solution)/shard_map/output/pallas_call | solution.py:256
  (43 shorter events, 5.3 us)
Async XLA Ops:
  7.7 3.1 %slice-start = ((s8[9437184]{0:T(1024)(128)(4,1)}), s8[4194304]{0:T(1024)(128)(4,1)S(1)}, s32[]{:S(2)}) async-start(s8[9437184]{0:T(1024)(128)(4,1)} %bitcast), calls=%async_computation | async-start | bytes 8388608
  7.7 3.5 %slice-start.1 = ((s8[9437184]{0:T(1024)(128)(4,1)}), s8[4194304]{0:T(1024)(128)(4,1)S(1)}, s32[]{:S(2)}) async-start(s8[9437184]{0:T(1024)(128)(4,1)} %bitcast), calls=%async_computation.1 | async-start | bytes 8388608
  8.9 2.7 %slice-start.2 = ((s8[9437184]{0:T(1024)(128)(4,1)}), s8[1048576]{0:T(1024)(128)(4,1)S(1)}, s32[]{:S(2)}) async-start(s8[9437184]{0:T(1024)(128)(4,1)} %bitcast), calls=%async_computation.2 | async-start | bytes 2097152
  8.9 3.4 %collective-permute-start.1 = (f32[16,32,128]{2,1,0:T(8,128)S(1)}, f32[16,32,128]{2,1,0:T(8,128)S(1)}, u32[]{:S(2)}, u32[]{:S(2)}) collective-permute-start(f32[16,32,128]{2,1,0:T(8,128)S(1)} %source_0.1._.c_ref), channel_id=1, source_target_pairs={{0,8},{8,0},{16,24},{24,16},{32,40},{40,32},{48,56},{56,48},{64,72... | collective-permute-start | bytes 786440 | tf_op jit(solution)/shard_map/ppermute | solution.py:302
  10.3 4.5 %collective-permute-start = (f32[16,32,128]{2,1,0:T(8,128)S(1)}, f32[16,32,128]{2,1,0:T(8,128)S(1)}, u32[]{:S(2)}, u32[]{:S(2)}) collective-permute-start(f32[16,32,128]{2,1,0:T(8,128)S(1)} %source_16.1._.c_ref), channel_id=1, source_target_pairs={{0,8},{8,0},{16,24},{24,16},{32,40},{40,32},{48,56},{56,48},{64,72... | collective-permute-start | bytes 786440 | tf_op jit(solution)/shard_map/ppermute | solution.py:302
  12.7 9.2 %collective-permute-start.2 = (f32[16,32,128]{2,1,0:T(8,128)S(1)}, f32[16,32,128]{2,1,0:T(8,128)S(1)}, u32[]{:S(2)}, u32[]{:S(2)}) collective-permute-start(f32[16,32,128]{2,1,0:T(8,128)S(1)} %level_2_0.1._.c_ref), channel_id=1, source_target_pairs={{0,16},{8,24},{16,0},{24,8},{32,48},{40,56},{48,32},{56,40},{64,80... | collective-permute-start | bytes 786440 | tf_op jit(solution)/shard_map/ppermute | solution.py:302
  15.0 12.7 %collective-permute-start.4 = (f32[16,32,128]{2,1,0:T(8,128)S(1)}, f32[16,32,128]{2,1,0:T(8,128)S(1)}, u32[]{:S(2)}, u32[]{:S(2)}) collective-permute-start(f32[16,32,128]{2,1,0:T(8,128)S(1)} %level_2_16.1._.c_ref), channel_id=1, source_target_pairs={{0,16},{8,24},{16,0},{24,8},{32,48},{40,56},{48,32},{56,40},{64,80... | collective-permute-start | bytes 786440 | tf_op jit(solution)/shard_map/ppermute | solution.py:302
  18.8 1.6 %copy-start = (f32[128,32,128]{2,1,0:T(8,128)S(1)}, f32[128,32,128]{2,1,0:T(8,128)}, u32[]{:S(2)}) copy-start(f32[128,32,128]{2,1,0:T(8,128)} %ti_ref.1) | copy-start | bytes 6291460
  22.2 14.5 %collective-permute-start.3 = (f32[16,32,128]{2,1,0:T(8,128)S(1)}, f32[16,32,128]{2,1,0:T(8,128)S(1)}, u32[]{:S(2)}, u32[]{:S(2)}) collective-permute-start(f32[16,32,128]{2,1,0:T(8,128)S(1)} %level_3_0.1._.c_ref), channel_id=1, source_target_pairs={{0,32},{8,40},{16,48},{24,56},{32,0},{40,8},{48,16},{56,24},{64,96... | collective-permute-start | bytes 786440 | tf_op jit(solution)/shard_map/ppermute | solution.py:302
  27.7 12.6 %collective-permute-start.8 = (f32[16,32,128]{2,1,0:T(8,128)S(1)}, f32[16,32,128]{2,1,0:T(8,128)S(1)}, u32[]{:S(2)}, u32[]{:S(2)}) collective-permute-start(f32[16,32,128]{2,1,0:T(8,128)S(1)} %source_32.1._.c_ref), channel_id=1, source_target_pairs={{0,8},{8,0},{16,24},{24,16},{32,40},{40,32},{48,56},{56,48},{64,72... | collective-permute-start | bytes 786440 | tf_op jit(solution)/shard_map/ppermute | solution.py:302
  28.1 14.3 %collective-permute-start.7 = (f32[16,32,128]{2,1,0:T(8,128)S(1)}, f32[16,32,128]{2,1,0:T(8,128)S(1)}, u32[]{:S(2)}, u32[]{:S(2)}) collective-permute-start(f32[16,32,128]{2,1,0:T(8,128)S(1)} %level_3_16.1._.c_ref), channel_id=1, source_target_pairs={{0,32},{8,40},{16,48},{24,56},{32,0},{40,8},{48,16},{56,24},{64,96... | collective-permute-start | bytes 786440 | tf_op jit(solution)/shard_map/ppermute | solution.py:302
  33.1 12.8 %collective-permute-start.6 = (f32[16,32,128]{2,1,0:T(8,128)S(1)}, f32[16,32,128]{2,1,0:T(8,128)S(1)}, u32[]{:S(2)}, u32[]{:S(2)}) collective-permute-start(f32[16,32,128]{2,1,0:T(8,128)S(1)} %source_48.1._.c_ref), channel_id=1, source_target_pairs={{0,8},{8,0},{16,24},{24,16},{32,40},{40,32},{48,56},{56,48},{64,72... | collective-permute-start | bytes 786440 | tf_op jit(solution)/shard_map/ppermute | solution.py:302
  37.0 9.3 %collective-permute-start.5 = (f32[16,32,128]{2,1,0:T(8,128)S(1)}, f32[16,32,128]{2,1,0:T(8,128)S(1)}, u32[]{:S(2)}, u32[]{:S(2)}) collective-permute-start(f32[16,32,128]{2,1,0:T(8,128)S(1)} %level_4_0.1._.c_ref), channel_id=1, source_target_pairs={{0,64},{8,72},{16,80},{24,88},{32,96},{40,104},{48,112},{56,120},{... | collective-permute-start | bytes 786440 | tf_op jit(solution)/shard_map/ppermute | solution.py:302
  40.6 7.6 %collective-permute-start.12 = (f32[16,32,128]{2,1,0:T(8,128)S(1)}, f32[16,32,128]{2,1,0:T(8,128)S(1)}, u32[]{:S(2)}, u32[]{:S(2)}) collective-permute-start(f32[16,32,128]{2,1,0:T(8,128)S(1)} %level_2_32.1._.c_ref), channel_id=1, source_target_pairs={{0,16},{8,24},{16,0},{24,8},{32,48},{40,56},{48,32},{56,40},{64,80... | collective-permute-start | bytes 786440 | tf_op jit(solution)/shard_map/ppermute | solution.py:302
  42.6 8.0 %collective-permute-start.11 = (f32[16,32,128]{2,1,0:T(8,128)S(1)}, f32[16,32,128]{2,1,0:T(8,128)S(1)}, u32[]{:S(2)}, u32[]{:S(2)}) collective-permute-start(f32[16,32,128]{2,1,0:T(8,128)S(1)} %level_4_16.1._.c_ref), channel_id=1, source_target_pairs={{0,64},{8,72},{16,80},{24,88},{32,96},{40,104},{48,112},{56,120},{... | collective-permute-start | bytes 786440 | tf_op jit(solution)/shard_map/ppermute | solution.py:302
  46.2 9.3 %collective-permute-start.10 = (f32[16,32,128]{2,1,0:T(8,128)S(1)}, f32[16,32,128]{2,1,0:T(8,128)S(1)}, u32[]{:S(2)}, u32[]{:S(2)}) collective-permute-start(f32[16,32,128]{2,1,0:T(8,128)S(1)} %level_2_48.1._.c_ref), channel_id=1, source_target_pairs={{0,16},{8,24},{16,0},{24,8},{32,48},{40,56},{48,32},{56,40},{64,80... | collective-permute-start | bytes 786440 | tf_op jit(solution)/shard_map/ppermute | solution.py:302
  46.6 9.3 %collective-permute-start.9 = (f32[16,32,128]{2,1,0:T(8,128)S(1)}, f32[16,32,128]{2,1,0:T(8,128)S(1)}, u32[]{:S(2)}, u32[]{:S(2)}) collective-permute-start(f32[16,32,128]{2,1,0:T(8,128)S(1)} %level_5_0.1._.c_ref), channel_id=1, source_target_pairs={{0,1},{1,0},{2,3},{3,2},{4,5},{5,4},{6,7},{7,6},{8,9},{9,8},{10,11... | collective-permute-start | bytes 786440 | tf_op jit(solution)/shard_map/ppermute | solution.py:302
  48.5 11.4 %collective-permute-start.16 = (f32[16,32,128]{2,1,0:T(8,128)S(1)}, f32[16,32,128]{2,1,0:T(8,128)S(1)}, u32[]{:S(2)}, u32[]{:S(2)}) collective-permute-start(f32[16,32,128]{2,1,0:T(8,128)S(1)} %level_3_32.1._.c_ref), channel_id=1, source_target_pairs={{0,32},{8,40},{16,48},{24,56},{32,0},{40,8},{48,16},{56,24},{64,96... | collective-permute-start | bytes 786440 | tf_op jit(solution)/shard_map/ppermute | solution.py:302
  50.9 11.9 %collective-permute-start.15 = (f32[16,32,128]{2,1,0:T(8,128)S(1)}, f32[16,32,128]{2,1,0:T(8,128)S(1)}, u32[]{:S(2)}, u32[]{:S(2)}) collective-permute-start(f32[16,32,128]{2,1,0:T(8,128)S(1)} %level_5_16.1._.c_ref), channel_id=1, source_target_pairs={{0,1},{1,0},{2,3},{3,2},{4,5},{5,4},{6,7},{7,6},{8,9},{9,8},{10,11... | collective-permute-start | bytes 786440 | tf_op jit(solution)/shard_map/ppermute | solution.py:302
  55.9 10.3 %collective-permute-start.14 = (f32[16,32,128]{2,1,0:T(8,128)S(1)}, f32[16,32,128]{2,1,0:T(8,128)S(1)}, u32[]{:S(2)}, u32[]{:S(2)}) collective-permute-start(f32[16,32,128]{2,1,0:T(8,128)S(1)} %level_3_48.1._.c_ref), channel_id=1, source_target_pairs={{0,32},{8,40},{16,48},{24,56},{32,0},{40,8},{48,16},{56,24},{64,96... | collective-permute-start | bytes 786440 | tf_op jit(solution)/shard_map/ppermute | solution.py:302
  56.3 11.9 %collective-permute-start.13 = (f32[16,32,128]{2,1,0:T(8,128)S(1)}, f32[16,32,128]{2,1,0:T(8,128)S(1)}, u32[]{:S(2)}, u32[]{:S(2)}) collective-permute-start(f32[16,32,128]{2,1,0:T(8,128)S(1)} %level_6_0.1._.c_ref), channel_id=1, source_target_pairs={{0,2},{1,3},{2,0},{3,1},{4,6},{5,7},{6,4},{7,5},{8,10},{9,11},{10,... | collective-permute-start | bytes 786440 | tf_op jit(solution)/shard_map/ppermute | solution.py:302
  60.2 9.5 %collective-permute-start.20 = (f32[16,32,128]{2,1,0:T(8,128)S(1)}, f32[16,32,128]{2,1,0:T(8,128)S(1)}, u32[]{:S(2)}, u32[]{:S(2)}) collective-permute-start(f32[16,32,128]{2,1,0:T(8,128)S(1)} %level_4_32.1._.c_ref), channel_id=1, source_target_pairs={{0,64},{8,72},{16,80},{24,88},{32,96},{40,104},{48,112},{56,120},{... | collective-permute-start | bytes 786440 | tf_op jit(solution)/shard_map/ppermute | solution.py:302
  63.1 9.3 %collective-permute-start.19 = (f32[16,32,128]{2,1,0:T(8,128)S(1)}, f32[16,32,128]{2,1,0:T(8,128)S(1)}, u32[]{:S(2)}, u32[]{:S(2)}) collective-permute-start(f32[16,32,128]{2,1,0:T(8,128)S(1)} %level_6_16.1._.c_ref), channel_id=1, source_target_pairs={{0,2},{1,3},{2,0},{3,1},{4,6},{5,7},{6,4},{7,5},{8,10},{9,11},{10,... | collective-permute-start | bytes 786440 | tf_op jit(solution)/shard_map/ppermute | solution.py:302
  66.5 10.8 %collective-permute-start.18 = (f32[16,32,128]{2,1,0:T(8,128)S(1)}, f32[16,32,128]{2,1,0:T(8,128)S(1)}, u32[]{:S(2)}, u32[]{:S(2)}) collective-permute-start(f32[16,32,128]{2,1,0:T(8,128)S(1)} %level_4_48.1._.c_ref), channel_id=1, source_target_pairs={{0,64},{8,72},{16,80},{24,88},{32,96},{40,104},{48,112},{56,120},{... | collective-permute-start | bytes 786440 | tf_op jit(solution)/shard_map/ppermute | solution.py:302
  68.5 13.3 %collective-permute-start.17 = (f32[16,32,128]{2,1,0:T(8,128)S(1)}, f32[16,32,128]{2,1,0:T(8,128)S(1)}, u32[]{:S(2)}, u32[]{:S(2)}) collective-permute-start(f32[16,32,128]{2,1,0:T(8,128)S(1)} %level_7_0.1._.c_ref), channel_id=1, source_target_pairs={{0,4},{1,5},{2,6},{3,7},{4,0},{5,1},{6,2},{7,3},{8,12},{9,13},{10,... | collective-permute-start | bytes 786440 | tf_op jit(solution)/shard_map/ppermute | solution.py:302
  70.0 12.6 %collective-permute-start.22 = (f32[16,32,128]{2,1,0:T(8,128)S(1)}, f32[16,32,128]{2,1,0:T(8,128)S(1)}, u32[]{:S(2)}, u32[]{:S(2)}) collective-permute-start(f32[16,32,128]{2,1,0:T(8,128)S(1)} %level_5_32.1._.c_ref), channel_id=1, source_target_pairs={{0,1},{1,0},{2,3},{3,2},{4,5},{5,4},{6,7},{7,6},{8,9},{9,8},{10,11... | collective-permute-start | bytes 786440 | tf_op jit(solution)/shard_map/ppermute | solution.py:302
  72.6 12.3 %collective-permute-start.21 = (f32[16,32,128]{2,1,0:T(8,128)S(1)}, f32[16,32,128]{2,1,0:T(8,128)S(1)}, u32[]{:S(2)}, u32[]{:S(2)}) collective-permute-start(f32[16,32,128]{2,1,0:T(8,128)S(1)} %level_7_16.1._.c_ref), channel_id=1, source_target_pairs={{0,4},{1,5},{2,6},{3,7},{4,0},{5,1},{6,2},{7,3},{8,12},{9,13},{10,... | collective-permute-start | bytes 786440 | tf_op jit(solution)/shard_map/ppermute | solution.py:302
  77.6 8.2 %collective-permute-start.24 = (f32[16,32,128]{2,1,0:T(8,128)S(1)}, f32[16,32,128]{2,1,0:T(8,128)S(1)}, u32[]{:S(2)}, u32[]{:S(2)}) collective-permute-start(f32[16,32,128]{2,1,0:T(8,128)S(1)} %level_5_48.1._.c_ref), channel_id=1, source_target_pairs={{0,1},{1,0},{2,3},{3,2},{4,5},{5,4},{6,7},{7,6},{8,9},{9,8},{10,11... | collective-permute-start | bytes 786440 | tf_op jit(solution)/shard_map/ppermute | solution.py:302
  82.9 10.7 %collective-permute-start.23 = (f32[16,32,128]{2,1,0:T(8,128)S(1)}, f32[16,32,128]{2,1,0:T(8,128)S(1)}, u32[]{:S(2)}, u32[]{:S(2)}) collective-permute-start(f32[16,32,128]{2,1,0:T(8,128)S(1)} %level_6_32.1._.c_ref), channel_id=1, source_target_pairs={{0,2},{1,3},{2,0},{3,1},{4,6},{5,7},{6,4},{7,5},{8,10},{9,11},{10,... | collective-permute-start | bytes 786440 | tf_op jit(solution)/shard_map/ppermute | solution.py:302
  86.1 10.3 %collective-permute-start.26 = (f32[16,32,128]{2,1,0:T(8,128)S(1)}, f32[16,32,128]{2,1,0:T(8,128)S(1)}, u32[]{:S(2)}, u32[]{:S(2)}) collective-permute-start(f32[16,32,128]{2,1,0:T(8,128)S(1)} %level_6_48.1._.c_ref), channel_id=1, source_target_pairs={{0,2},{1,3},{2,0},{3,1},{4,6},{5,7},{6,4},{7,5},{8,10},{9,11},{10,... | collective-permute-start | bytes 786440 | tf_op jit(solution)/shard_map/ppermute | solution.py:302
  93.9 8.4 %collective-permute-start.25 = (f32[16,32,128]{2,1,0:T(8,128)S(1)}, f32[16,32,128]{2,1,0:T(8,128)S(1)}, u32[]{:S(2)}, u32[]{:S(2)}) collective-permute-start(f32[16,32,128]{2,1,0:T(8,128)S(1)} %level_7_32.1._.c_ref), channel_id=1, source_target_pairs={{0,4},{1,5},{2,6},{3,7},{4,0},{5,1},{6,2},{7,3},{8,12},{9,13},{10,... | collective-permute-start | bytes 786440 | tf_op jit(solution)/shard_map/ppermute | solution.py:302
  96.8 8.4 %collective-permute-start.27 = (f32[16,32,128]{2,1,0:T(8,128)S(1)}, f32[16,32,128]{2,1,0:T(8,128)S(1)}, u32[]{:S(2)}, u32[]{:S(2)}) collective-permute-start(f32[16,32,128]{2,1,0:T(8,128)S(1)} %level_7_48.1._.c_ref), channel_id=1, source_target_pairs={{0,4},{1,5},{2,6},{3,7},{4,0},{5,1},{6,2},{7,3},{8,12},{9,13},{10,... | collective-permute-start | bytes 786440 | tf_op jit(solution)/shard_map/ppermute | solution.py:302

commit v3 on v2

--- a/solution.py
+++ b/solution.py
@@ -13,7 +13,7 @@
 VMEM = pl.BlockSpec(memory_space=pltpu.VMEM)
 ANY = pl.BlockSpec(memory_space=pl.ANY)
 NEAR_ZERO = pl.CostEstimate(flops=1, bytes_accessed=1, transcendentals=0)
-STEP = (0, 1, -2, 0, 1, -3, -4, -5, -6, -7, -8, -9, 0, 2, 1, 3, 0, 2, 1, 3, 0, 2, 1, 3, 0, 2, 1, 3, 0, 2, 1, 3, 0, 2, 1, 3, 2, 3, 2, 3)
+STEP = (0, 1, 0, 1, -1, -3, -4, -5, -6, -7, 0, 2, 1, 3, -8, 0, 2, 1, 3, 0, 2, 1, -9, 3, 0, 2, 1, 3, 0, 2, 1, 3, 2, 3, 0, 2, 1, 3, 2, 3)
 ORDER = [("step", i) if i >= 0 else ("prepare", -i) for i in STEP]
 
 
@@ -34,19 +34,27 @@
     return lax.broadcasted_iota(jnp.int32, shape, len(shape) - 1) < HALF
 
 
+def turn_transfer(block):
+    return [jnp.concatenate([block[i], block[i + 8]], 0).T for i in range(8)]
+
+
+def place_transfer(turned, out_ref, gl, gh, k0):
+    mask = low_lanes((8, 8, NB))
+    v = jnp.swapaxes(jnp.stack(turned), 0, 1)
+    w = pltpu.roll(v, HALF, 2)
+    vh = v.astype(BF16).astype(F32)
+    wh = w.astype(BF16).astype(F32)
+    first = jnp.where(mask, vh, w - wh)
+    second = jnp.where(mask, wh, v - vh)
+    rows = jnp.concatenate([first, second], 1).astype(BF16)
+    out_ref[gl : gl + 8, gh * K + k0 : gh * K + k0 + 16, :] = rows
+
+
 def prepare_transfer(block, out_ref, k0):
-    turned = [jnp.concatenate([block[i], block[i + 8]], 0).T for i in range(8)]
-    mask = low_lanes((8, 8, NB))
+    turned = turn_transfer(block)
     for g0 in range(0, NB, 8):
-        v = jnp.swapaxes(jnp.stack([t[g0 : g0 + 8] for t in turned]), 0, 1)
-        w = pltpu.roll(v, HALF, 2)
-        vh = v.astype(BF16).astype(F32)
-        wh = w.astype(BF16).astype(F32)
-        first = jnp.where(mask, vh, w - wh)
-        second = jnp.where(mask, wh, v - vh)
         gh, gl = divmod(g0, HALF)
-        rows = jnp.concatenate([first, second], 1).astype(BF16)
-        out_ref[gl : gl + 8, gh * K + k0 : gh * K + k0 + 16, :] = rows
+        place_transfer([t[g0 : g0 + 8] for t in turned], out_ref, gl, gh, k0)
 
 
 def mix(weight, own, partner, mask):
@@ -56,10 +64,20 @@
     return jnp.where(mask, s[:K], s[K:])
 
 
+PART = HALF // 2
+EARLY = 3
+
+
+def part_shapes():
+    matrices = [pltpu.VMEM((PART, 2 * K, NB), BF16)] * EARLY
+    return [pltpu.VMEM((HALF, R, B), F32), pltpu.VMEM((HALF, K, B), F32)] + matrices
+
+
 def source_prepare(sources, source_interp, transfer):
-    def kernel(src_hbm, si_hbm, t_hbm, s_ref, m_ref, t0_ref, t1_ref, src, si, t, a_ref, src_sem, si_sem, t_sem):
+    def kernel(src_hbm, si_hbm, t_hbm, s_ref, m_ref, *refs):
+        t_refs, (us_ref, um_ref, ut_ref, src, si, t, a_ref, src_sem, si_sem, t_sem) = refs[:EARLY], refs[EARLY:]
         si_copy = [pltpu.make_async_copy(si_hbm.at[pl.ds(32 * i, 32)], si.at[pl.ds(32 * i, 32)], si_sem.at[i]) for i in range(4)]
-        t_copy = [pltpu.make_async_copy(t_hbm.at[i], t.at[i], t_sem.at[i]) for i in range(2)]
+        t_copy = [pltpu.make_async_copy(t_hbm.at[i], t.at[i], t_sem.at[i]) for i in range(EARLY)]
 
         def src_copy(i):
             rows = pl.ds(pl.multiple_of(8 * i, 8), 8)
@@ -72,45 +90,88 @@
             for b0 in range(32 * i, 32 * i + 32, 8):
                 a_ref[:, b0 : b0 + 8, :] = jnp.swapaxes(si[b0 : b0 + 8], 0, 1)
 
-        def turn(block, out_ref, first):
+        def turn(block, out_ref, rest_ref, first):
             turned = [block(j).T for j in range(8)]
-            for g0 in range(0, NB, 8):
-                out_ref[g0 : g0 + 8, pl.ds(first, 8), :] = jnp.swapaxes(jnp.stack([x[g0 : g0 + 8] for x in turned]), 0, 1)
-
-        @pl.loop(0, K // 8)
+            for gh in range(2):
+                for q in range(0, PART, 8):
+                    g0 = gh * HALF + q
+                    rows = jnp.swapaxes(jnp.stack([x[g0 : g0 + 8] for x in turned]), 0, 1)
+                    out_ref[gh * PART + q : gh * PART + q + 8, pl.ds(first, 8), :] = rows
+                g0 = gh * HALF + PART
+                for j in range(8):
+                    rest_ref[first + j, gh * PART : gh * PART + PART, :] = turned[j][g0 : g0 + PART]
+
+        @pl.loop(0, K // 8, unroll=True)
         def _(i):
             k0 = pl.multiple_of(i * 8, 8)
-            turn(lambda j: a_ref[k0 + j], m_ref, k0)
-
-        @pl.loop(0, 8)
+            turn(lambda j: a_ref[k0 + j], m_ref, um_ref, k0)
+
+        @pl.loop(0, 8, unroll=True)
         def _(i):
             src_copy(i).wait()
             r0 = pl.multiple_of(i * 8, 8)
-            turn(lambda j: src[r0 + j], s_ref, r0)
-
-        for i, out_ref in enumerate((t0_ref, t1_ref)):
+            turn(lambda j: src[r0 + j], s_ref, us_ref, r0)
+
+        for i, out_ref in enumerate(t_refs):
             t_copy[i].wait()
             for half in range(2):
-                prepare_transfer(t.at[i, pl.ds(16 * half, 16)], out_ref, 16 * half)
+                turned = turn_transfer(t.at[i, pl.ds(16 * half, 16)])
+                for gh in range(2):
+                    for q in range(0, PART, 8):
+                        g0 = gh * HALF + q
+                        place_transfer([x[g0 : g0 + 8] for x in turned], out_ref, q, gh, 16 * half)
+                    g0 = gh * HALF + PART
+                    for j in range(8):
+                        ut_ref[i, half, j, gh * PART : gh * PART + PART, :] = turned[j][g0 : g0 + PART]
 
     hbm = pl.BlockSpec(memory_space=pltpu.HBM)
+    rest = [pltpu.VMEM((R, HALF, B), F32), pltpu.VMEM((K, HALF, B), F32), pltpu.VMEM((EARLY, 2, 8, HALF, NB), F32)]
     return pl.pallas_call(
         kernel,
         name="source_prepare",
         in_specs=[hbm] * 3,
-        out_specs=[VMEM] * 4,
-        out_shape=[pltpu.VMEM((NB, R, B), F32), pltpu.VMEM((NB, K, B), F32)] + [pltpu.VMEM((HALF, 2 * K, NB), BF16)] * 2,
+        out_specs=[VMEM] * (5 + EARLY),
+        out_shape=part_shapes() + rest,
         scratch_shapes=[
             pltpu.VMEM((R, B, NB), F32),
             pltpu.VMEM((B, K, NB), F32),
-            pltpu.VMEM((2, K, 2 * K, NB), F32),
+            pltpu.VMEM((EARLY, K, 2 * K, NB), F32),
             pltpu.VMEM((K, B, NB), F32),
             pltpu.SemaphoreType.DMA((8,)),
             pltpu.SemaphoreType.DMA((4,)),
-            pltpu.SemaphoreType.DMA((2,)),
+            pltpu.SemaphoreType.DMA((EARLY,)),
         ],
-        compiler_params=pltpu.CompilerParams(vmem_limit_bytes=14 * MIB),
+        compiler_params=pltpu.CompilerParams(vmem_limit_bytes=15 * MIB),
     )(*in_hbm(sources, source_interp, transfer))
+
+
+def source_rest(rest, after):
+    def kernel(us_ref, um_ref, ut_ref, _, s_ref, m_ref, *t_refs):
+        def place(count, rest_ref, out_ref):
+            @pl.loop(0, count // 8)
+            def _(i):
+                first = pl.multiple_of(i * 8, 8)
+                for q in range(0, HALF, 8):
+                    out_ref[q : q + 8, pl.ds(first, 8), :] = jnp.swapaxes(rest_ref[pl.ds(first, 8), q : q + 8, :], 0, 1)
+
+        place(K, um_ref, m_ref)
+        place(R, us_ref, s_ref)
+        for i, out_ref in enumerate(t_refs):
+            for half in range(2):
+                for gh in range(2):
+                    for q in range(0, PART, 8):
+                        rows = [ut_ref[i, half, j, gh * PART + q : gh * PART + q + 8, :] for j in range(8)]
+                        place_transfer(rows, out_ref, q, gh, 16 * half)
+
+    return pl.pallas_call(
+        kernel,
+        name="source_rest",
+        in_specs=[VMEM] * 3 + [ANY],
+        out_specs=[VMEM] * (2 + EARLY),
+        out_shape=part_shapes(),
+        compiler_params=pltpu.CompilerParams(vmem_limit_bytes=2 * MIB),
+        cost_estimate=NEAR_ZERO,
+    )(*in_vmem(*rest, after))
 
 
 def source_stage(prepared, first, size, after):
@@ -118,16 +179,16 @@
         mask = low_lanes((K, NB))
         dims = (((1,), (1,)), ((), ()))
         for j in range(size):
-            gl = first + j
-            mh, ml = split(jnp.concatenate([m_ref[gl], m_ref[gl + HALF]], 0))
-            sh, sl = split(jnp.concatenate([s_ref[gl], s_ref[gl + HALF]], 0))
+            q = first % PART + j
+            mh, ml = split(jnp.concatenate([m_ref[q], m_ref[q + PART]], 0))
+            sh, sl = split(jnp.concatenate([s_ref[q], s_ref[q + PART]], 0))
             s = lax.dot_general(jnp.concatenate([mh, ml], 1), jnp.concatenate([sh, sh], 1), dims, preferred_element_type=F32)
             s = s + lax.dot_general(mh, sl, dims, preferred_element_type=F32)
             c_ref[j] = jnp.where(mask, s[:K], s[K:])
         for j in range(size):
-            d_ref[j] = mix(t0_ref[first + j], c_ref[j], c_ref[j ^ 1], mask)
-        for j in range(size):
-            o_ref[j] = mix(t1_ref[first + j], d_ref[j], d_ref[j ^ 2], mask)
+            d_ref[j] = mix(t0_ref[first % PART + j], c_ref[j], c_ref[j ^ 1], mask)
+        for j in range(size):
+            o_ref[j] = mix(t1_ref[first % PART + j], d_ref[j], d_ref[j ^ 2], mask)
 
     return pl.pallas_call(
         kernel,
@@ -161,7 +222,7 @@
     for b0 in range(0, B, 8):
         a_ref[:, b0 : b0 + 8, :] = jnp.swapaxes(ti_ref[b0 : b0 + 8], 0, 1)
 
-    @pl.loop(0, K // 8)
+    @pl.loop(0, K // 8, unroll=True)
     def _(i):
         k0 = pl.multiple_of(i * 8, 8)
         turned = [a_ref[k0 + j].T for j in range(8)]
@@ -185,11 +246,12 @@
 
 def level_stage(weights, own, partner, first, level, after):
     size = own.shape[0]
+    start = first % weights.shape[0]
 
     def kernel(t_ref, c_ref, p_ref, _, o_ref):
         mask = low_lanes((K, NB))
         for j in range(size):
-            o_ref[j] = mix(t_ref[first + j], c_ref[j], p_ref[j], mask)
+            o_ref[j] = mix(t_ref[start + j], c_ref[j], p_ref[j], mask)
 
     return pl.pallas_call(
         kernel,
@@ -242,14 +304,14 @@
             rows = pl.ds(pl.multiple_of(8 * i, 8), 8)
             return pltpu.make_async_copy(o_ref.at[rows], o_hbm.at[rows], sem.at[i])
 
-        @pl.loop(0, 8)
+        @pl.loop(0, 8, unroll=True)
         def _(i):
             for j in range(8):
                 r = i * 8 + j
                 o_ref[r] = jnp.concatenate([ref[r, gh] for gh in range(2) for ref in ins], 0).T
             copy(i).start()
 
-        @pl.loop(0, 8)
+        @pl.loop(0, 8, unroll=True)
         def _(i):
             copy(i).wait()
 
@@ -268,12 +330,16 @@
     prepared = source_prepare(sources, source_interp, transfer)
     count = len(CHUNKS)
     firsts = [sum(CHUNKS[:i]) for i in range(count)]
+    early = [prepared[: 2 + EARLY], None]
     weights, parts = {}, {}
     level, own, partner = [1] * count, [None] * count, [None] * count
     after = prepared[2]
     for kind, index in ORDER:
         if kind == "prepare":
-            if index == 9:
+            if index == 1:
+                early[1] = source_rest(prepared[2 + EARLY :], after)
+                after = early[1][2]
+            elif index == 9:
                 after = weights[9] = target_matrix_stage(target_interp, after)
             else:
                 after = weights[index] = transfer_stage(transfer, index, after)
@@ -283,7 +349,9 @@
             after = parts[index] = last_stage(weights[8], own[index], partner[index], weights[9], first, after)
             continue
         if n == 1:
-            after = source_stage(prepared, first, size, after)
+            after = source_stage(early[first // PART][:4], first, size, after)
+        elif n == 2:
+            after = level_stage(early[first // PART][4], own[index], partner[index], first, n, after)
         else:
             after = level_stage(weights[n], own[index], partner[index], first, n, after)
         own[index], level[index] = after, n + 1

time: 109 us -> 105 us (0.963)
  local copies, waits for them, and re-layouts: 1.65 us -> 0.02 us
  waiting for transfers between devices: 30.6 us -> 29.4 us
    unnamed x8, local copies, waits for them, and re-layouts: 1.65 us -> 0.02 us
    pallas_call x0 -> x1, Pallas kernels: none -> 1.42 us  [source_rest(): pl.pallas_call(kernel, name='source_rest', in_specs=[VMEM] * 3 + [ANY], o...]
    ppermute x28, waiting for transfers between devices: 30.6 us -> 29.4 us  [exchange(): return lax.ppermute(c, axis, [(i, i ^ 1 << bit) for i in range(size)])]
    pallas_call x7 -> x6, Pallas kernels: 5.08 us -> 4.36 us  [transfer_stage(): pl.pallas_call(kernel, name=f'transfer_{level}', in_specs=[VMEM, ANY], ou...]
  transfers between devices with their start and end apart: 28 -> 28, of which waited for: 14 -> 15; matrix products, arithmetic and copies ran while one was open for 0% -> 0% of each run, Pallas kernels for 18% -> 19%
where the time goes in v3:
time: 105 us
  starting transfers between devices  43.4 us (41%)
  Pallas kernels  31.4 us (30%)
  waiting for transfers between devices  29.4 us (28%)
    ppermute x28, starting transfers between devices, exchange(): return lax.ppermute(c, axis, [(i, i ^ 1 << bit) for i in range(size)])  43.4 us
    ppermute x28, waiting for transfers between devices, exchange(): return lax.ppermute(c, axis, [(i, i ^ 1 << bit) for i in range(size)])  29.4 us
    pallas_call x1, Pallas kernels, source_prepare(): pl.pallas_call(kernel, name='source_prepare', in_specs=[hbm] * 3, out_spe...  7.49 us
    pallas_call x24, Pallas kernels, level_stage(): pl.pallas_call(kernel, name=f'level_{level}_{first}', in_specs=[VMEM] * 3...  7.09 us
    pallas_call x4, Pallas kernels, source_stage(): pl.pallas_call(kernel, name=f'source_{first}', in_specs=[VMEM] * 4 + [ANY...  4.81 us
    pallas_call x6, Pallas kernels, transfer_stage(): pl.pallas_call(kernel, name=f'transfer_{level}', in_specs=[VMEM, ANY], ou...  4.36 us
    pallas_call x4, Pallas kernels, last_stage(): pl.pallas_call(kernel, name=f'last_{first}', in_specs=[VMEM] * 4 + [ANY],...  2.86 us
    pallas_call x1, Pallas kernels, output_stage(): pl.pallas_call(kernel, name='output', in_specs=[VMEM] * len(parts), out_s...  2.27 us
  transfers between devices with their start and end apart: 28, of which 15 were waited for; matrix products, arithmetic and copies ran while one was open for 0% of the time, Pallas kernels for 19%

profile of v3, /device:TPU:0, one launch (start us, length us, event | category | flops | bytes accessed | tf_op | source)
XLA Modules:
  0.0 104.8 jit_solution(9397860557909098892)
XLA Ops:
  0.0 7.5 %source_prepare.1 = (f32[64,64,128]{2,1,0:T(8,128)S(1)}, f32[64,32,128]{2,1,0:T(8,128)S(1)}, bf16[32,64,128]{2,1,0:T(8,128)(2,1)S(1)}, bf16[32,64,128]{2,1,0:T(8...) custom-call(f32[64,128,128]{2,1,0:T(8,128)} %src_hbm.1, ...), custom_call_target="tpu_custom_call" | custom-call | tf_op jit(solution)/shard_map/source_prepare/pallas_call | solution.py:129
  7.5 1.2 %source_0.1._.c_ref = f32[16,32,128]{2,1,0:T(8,128)S(1)} custom-call(f32[64,64,128]{2,1,0:T(8,128)S(1)} %get-tuple-element.22.s_ref, f32[64,32,128]{2,1,0:T(8,128)S(1)} %get-tuple-element.23.m_ref, bf16[32,64,128]{2,1,0:T(8,128)(2,1)S(1)} %get-tuple-element.24.t0_ref._, bf16[32,64,128]{2,1,0:T(8,128)(2,1)S(1)} %get-tuple-element.25.t1_ref, ...), custom_call_target="tpu_custom_call" | custom-call | flops 1 | bytes 1 | tf_op jit(solution)/shard_map/source_0/pallas_call | solution.py:193
  8.8 1.2 %source_16.1._.c_ref = f32[16,32,128]{2,1,0:T(8,128)S(1)} custom-call(f32[64,64,128]{2,1,0:T(8,128)S(1)} %get-tuple-element.22.s_ref, f32[64,32,128]{2,1,0:T(8,128)S(1)} %get-tuple-element.23.m_ref, bf16[32,64,128]{2,1,0:T(8,128)(2,1)S(1)} %get-tuple-element.24.t0_ref._, bf16[32,64,128]{2,1,0:T(8,128)(2,1)S(1)} %get-tuple-element.25.t1_ref, ...), custom_call_target="tpu_custom_call" | custom-call | flops 1 | bytes 1 | tf_op jit(solution)/shard_map/source_16/pallas_call | solution.py:193
  10.0 0.6 collective-permute-start
  10.9 2.1 %collective-permute-start.3 = (f32[16,32,128]{2,1,0:T(8,128)S(1)}, f32[16,32,128]{2,1,0:T(8,128)S(1)}, u32[]{:S(2)}, u32[]{:S(2)}) collective-permute-start(f32[16,32,128]{2,1,0:T(8,128)S(1)} %level_2_0.1._.c_ref), channel_id=1, source_target_pairs={{0,16},{8,24},{16,0},{24,8},{32,48},{40,56},{48,32},{56,40},{64,80... | collective-permute-start | bytes 786440 | tf_op jit(solution)/shard_map/ppermute | solution.py:370
  13.3 1.0 collective-permute-start.2
  14.3 1.4 %source_rest.1 = (f32[64,64,128]{2,1,0:T(8,128)S(1)}, f32[64,32,128]{2,1,0:T(8,128)S(1)}, bf16[32,64,128]{2,1,0:T(8,128)(2,1)S(1)}, bf16[32,64,128]{2,1,0:T(8,128)(2,1)S(1)}, bf16[32,64,128]{2,1,0:T(8,128)(2,1)S(1)}) custom-call(f32[64,64,128]{2,1,0:T(8,128)S(1)} %get-tuple-element.18.us_ref, f32[32,64,128]{2,1,0:T(8,128)S(1)} %get-tuple-element.19.um_ref, ...), custom_call_target="tpu_custom_call" | custom-call | flops 1 | bytes 1 | tf_op jit(solution)/shard_map/source_rest/pallas_call | solution.py:166
  15.8 0.7 transfer_3.1._.t_ref
  16.6 0.7 transfer_4.1._.t_ref
  17.3 0.7 transfer_5.1._.t_ref
  18.0 0.7 transfer_6.1._.t_ref
  18.8 0.7 transfer_7.1._.t_ref
  19.5 0.6 collective-permute-done.3.p_ref
  20.4 4.1 %collective-permute-start.4 = (f32[16,32,128]{2,1,0:T(8,128)S(1)}, f32[16,32,128]{2,1,0:T(8,128)S(1)}, u32[]{:S(2)}, u32[]{:S(2)}) collective-permute-start(f32[16,32,128]{2,1,0:T(8,128)S(1)} %level_3_0.1._.c_ref), channel_id=1, source_target_pairs={{0,32},{8,40},{16,48},{24,56},{32,0},{40,8},{48,16},{56,24},{64,96... | collective-permute-start | bytes 786440 | tf_op jit(solution)/shard_map/ppermute | solution.py:370
  24.5 1.2 %source_32.1._.c_ref = f32[16,32,128]{2,1,0:T(8,128)S(1)} custom-call(f32[64,64,128]{2,1,0:T(8,128)S(1)} %get-tuple-element.26.s_ref, f32[64,32,128]{2,1,0:T(8,128)S(1)} %get-tuple-element.27.m_ref, bf16[32,64,128]{2,1,0:T(8,128)(2,1)S(1)} %get-tuple-element.28._.t0_ref, bf16[32,64,128]{2,1,0:T(8,128)(2,1)S(1)} %get-tuple-element.29.t1_ref, ...), custom_call_target="tpu_custom_call" | custom-call | flops 1 | bytes 1 | tf_op jit(solution)/shard_map/source_32/pallas_call | solution.py:193
  26.1 4.0 %collective-permute-start.7 = (f32[16,32,128]{2,1,0:T(8,128)S(1)}, f32[16,32,128]{2,1,0:T(8,128)S(1)}, u32[]{:S(2)}, u32[]{:S(2)}) collective-permute-start(f32[16,32,128]{2,1,0:T(8,128)S(1)} %level_3_16.1._.c_ref), channel_id=1, source_target_pairs={{0,32},{8,40},{16,48},{24,56},{32,0},{40,8},{48,16},{56,24},{64,96... | collective-permute-start | bytes 786440 | tf_op jit(solution)/shard_map/ppermute | solution.py:370
  30.1 1.2 %source_48.1._.c_ref = f32[16,32,128]{2,1,0:T(8,128)S(1)} custom-call(f32[64,64,128]{2,1,0:T(8,128)S(1)} %get-tuple-element.26.s_ref, f32[64,32,128]{2,1,0:T(8,128)S(1)} %get-tuple-element.27.m_ref, bf16[32,64,128]{2,1,0:T(8,128)(2,1)S(1)} %get-tuple-element.28._.t0_ref, bf16[32,64,128]{2,1,0:T(8,128)(2,1)S(1)} %get-tuple-element.29.t1_ref, ...), custom_call_target="tpu_custom_call" | custom-call | flops 1 | bytes 1 | tf_op jit(solution)/shard_map/source_48/pallas_call | solution.py:193
  31.4 0.7 transfer_8.1._.t_ref
  32.2 2.8 %collective-permute-done.4.p_ref = f32[16,32,128]{2,1,0:T(8,128)S(1)} collective-permute-done((f32[16,32,128]{2,1,0:T(8,128)S(1)}, f32[16,32,128]{2,1,0:T(8,128)S(1)}, u32[]{:S(2)}, u32[]{:S(2)}) %collective-permute-start.4) | collective-permute-done | bytes 262176 | tf_op jit(solution)/shard_map/ppermute | solution.py:370
  35.3 3.3 %collective-permute-start.5 = (f32[16,32,128]{2,1,0:T(8,128)S(1)}, f32[16,32,128]{2,1,0:T(8,128)S(1)}, u32[]{:S(2)}, u32[]{:S(2)}) collective-permute-start(f32[16,32,128]{2,1,0:T(8,128)S(1)} %level_4_0.1._.c_ref), channel_id=1, source_target_pairs={{0,64},{8,72},{16,80},{24,88},{32,96},{40,104},{48,112},{56,120},{... | collective-permute-start | bytes 786440 | tf_op jit(solution)/shard_map/ppermute | solution.py:370
  38.9 1.5 %collective-permute-done.7.p_ref = f32[16,32,128]{2,1,0:T(8,128)S(1)} collective-permute-done((f32[16,32,128]{2,1,0:T(8,128)S(1)}, f32[16,32,128]{2,1,0:T(8,128)S(1)}, u32[]{:S(2)}, u32[]{:S(2)}) %collective-permute-start.7) | collective-permute-done | bytes 262176 | tf_op jit(solution)/shard_map/ppermute | solution.py:370
  40.4 0.3 level_4_16.1._.c_ref
  40.7 3.4 %collective-permute-start.11 = (f32[16,32,128]{2,1,0:T(8,128)S(1)}, f32[16,32,128]{2,1,0:T(8,128)S(1)}, u32[]{:S(2)}, u32[]{:S(2)}) collective-permute-start(f32[16,32,128]{2,1,0:T(8,128)S(1)} %level_4_16.1._.c_ref), channel_id=1, source_target_pairs={{0,64},{8,72},{16,80},{24,88},{32,96},{40,104},{48,112},{56,120},{... | collective-permute-start | bytes 786440 | tf_op jit(solution)/shard_map/ppermute | solution.py:370
  44.6 0.3 level_5_0.1._.c_ref
  44.9 1.6 %collective-permute-start.9 = (f32[16,32,128]{2,1,0:T(8,128)S(1)}, f32[16,32,128]{2,1,0:T(8,128)S(1)}, u32[]{:S(2)}, u32[]{:S(2)}) collective-permute-start(f32[16,32,128]{2,1,0:T(8,128)S(1)} %level_5_0.1._.c_ref), channel_id=1, source_target_pairs={{0,1},{1,0},{2,3},{3,2},{4,5},{5,4},{6,7},{7,6},{8,9},{9,8},{10,11... | collective-permute-start | bytes 786440 | tf_op jit(solution)/shard_map/ppermute | solution.py:370
  46.4 0.3 level_3_32.1._.c_ref
  46.8 0.4 collective-permute-start.16
  47.2 1.7 %collective-permute-done.11.p_ref = f32[16,32,128]{2,1,0:T(8,128)S(1)} collective-permute-done((f32[16,32,128]{2,1,0:T(8,128)S(1)}, f32[16,32,128]{2,1,0:T(8,128)S(1)}, u32[]{:S(2)}, u32[]{:S(2)}) %collective-permute-start.11) | collective-permute-done | bytes 262176 | tf_op jit(solution)/shard_map/ppermute | solution.py:370
  49.2 1.6 %collective-permute-start.15 = (f32[16,32,128]{2,1,0:T(8,128)S(1)}, f32[16,32,128]{2,1,0:T(8,128)S(1)}, u32[]{:S(2)}, u32[]{:S(2)}) collective-permute-start(f32[16,32,128]{2,1,0:T(8,128)S(1)} %level_5_16.1._.c_ref), channel_id=1, source_target_pairs={{0,1},{1,0},{2,3},{3,2},{4,5},{5,4},{6,7},{7,6},{8,9},{9,8},{10,11... | collective-permute-start | bytes 786440 | tf_op jit(solution)/shard_map/ppermute | solution.py:370
  50.8 1.1 %target_matrix.1._.m_ref = f32[128,32,128]{2,1,0:T(8,128)S(1)} custom-call(f32[128,32,128]{2,1,0:T(8,128)S(1)} %copy-done, f32[16,32,128]{2,1,0:T(8,128)S(1)} %level_5_16.1._.c_ref), custom_call_target="tpu_custom_call" | custom-call | flops 1 | bytes 1 | tf_op jit(solution)/shard_map/target_matrix/pallas_call | solution.py:235
  51.9 1.9 %collective-permute-done.10.p_ref = f32[16,32,128]{2,1,0:T(8,128)S(1)} collective-permute-done((f32[16,32,128]{2,1,0:T(8,128)S(1)}, f32[16,32,128]{2,1,0:T(8,128)S(1)}, u32[]{:S(2)}, u32[]{:S(2)}) %collective-permute-start.10) | collective-permute-done | bytes 262176 | tf_op jit(solution)/shard_map/ppermute | solution.py:370
  53.8 0.3 level_3_48.1._.c_ref
  54.2 0.3 level_6_0.1._.c_ref
  54.5 3.1 %collective-permute-start.13 = (f32[16,32,128]{2,1,0:T(8,128)S(1)}, f32[16,32,128]{2,1,0:T(8,128)S(1)}, u32[]{:S(2)}, u32[]{:S(2)}) collective-permute-start(f32[16,32,128]{2,1,0:T(8,128)S(1)} %level_6_0.1._.c_ref), channel_id=1, source_target_pairs={{0,2},{1,3},{2,0},{3,1},{4,6},{5,7},{6,4},{7,5},{8,10},{9,11},{10,... | collective-permute-start | bytes 786440 | tf_op jit(solution)/shard_map/ppermute | solution.py:370
  57.6 0.4 collective-permute-done.16.p_ref
  58.0 0.3 level_4_32.1._.c_ref
  58.3 2.7 %collective-permute-start.20 = (f32[16,32,128]{2,1,0:T(8,128)S(1)}, f32[16,32,128]{2,1,0:T(8,128)S(1)}, u32[]{:S(2)}, u32[]{:S(2)}) collective-permute-start(f32[16,32,128]{2,1,0:T(8,128)S(1)} %level_4_32.1._.c_ref), channel_id=1, source_target_pairs={{0,64},{8,72},{16,80},{24,88},{32,96},{40,104},{48,112},{56,120},{... | collective-permute-start | bytes 786440 | tf_op jit(solution)/shard_map/ppermute | solution.py:370
  61.3 3.1 %collective-permute-start.19 = (f32[16,32,128]{2,1,0:T(8,128)S(1)}, f32[16,32,128]{2,1,0:T(8,128)S(1)}, u32[]{:S(2)}, u32[]{:S(2)}) collective-permute-start(f32[16,32,128]{2,1,0:T(8,128)S(1)} %level_6_16.1._.c_ref), channel_id=1, source_target_pairs={{0,2},{1,3},{2,0},{3,1},{4,6},{5,7},{6,4},{7,5},{8,10},{9,11},{10,... | collective-permute-start | bytes 786440 | tf_op jit(solution)/shard_map/ppermute | solution.py:370
  64.7 1.0 collective-permute-start.18
  65.7 0.3 collective-permute-done.13.p_ref
  66.6 2.0 %collective-permute-start.22 = (f32[16,32,128]{2,1,0:T(8,128)S(1)}, f32[16,32,128]{2,1,0:T(8,128)S(1)}, u32[]{:S(2)}, u32[]{:S(2)}) collective-permute-start(f32[16,32,128]{2,1,0:T(8,128)S(1)} %level_5_32.1._.c_ref), channel_id=1, source_target_pairs={{0,1},{1,0},{2,3},{3,2},{4,5},{5,4},{6,7},{7,6},{8,9},{9,8},{10,11... | collective-permute-start | bytes 786440 | tf_op jit(solution)/shard_map/ppermute | solution.py:370
  68.6 2.0 %collective-permute-done.19.p_ref = f32[16,32,128]{2,1,0:T(8,128)S(1)} collective-permute-done((f32[16,32,128]{2,1,0:T(8,128)S(1)}, f32[16,32,128]{2,1,0:T(8,128)S(1)}, u32[]{:S(2)}, u32[]{:S(2)}) %collective-permute-start.19) | collective-permute-done | bytes 262176 | tf_op jit(solution)/shard_map/ppermute | solution.py:370
  70.9 1.8 %collective-permute-done.18.p_ref = f32[16,32,128]{2,1,0:T(8,128)S(1)} collective-permute-done((f32[16,32,128]{2,1,0:T(8,128)S(1)}, f32[16,32,128]{2,1,0:T(8,128)S(1)}, u32[]{:S(2)}, u32[]{:S(2)}) %collective-permute-start.18) | collective-permute-done | bytes 262176 | tf_op jit(solution)/shard_map/ppermute | solution.py:370
  73.0 0.8 collective-permute-start.21
  73.7 1.1 %collective-permute-start.17 = (f32[16,32,128]{2,1,0:T(8,128)S(1)}, f32[16,32,128]{2,1,0:T(8,128)S(1)}, u32[]{:S(2)}, u32[]{:S(2)}) collective-permute-start(f32[16,32,128]{2,1,0:T(8,128)S(1)} %level_7_0.1._.c_ref), channel_id=1, source_target_pairs={{0,4},{1,5},{2,6},{3,7},{4,0},{5,1},{6,2},{7,3},{8,12},{9,13},{10,... | collective-permute-start | bytes 786440 | tf_op jit(solution)/shard_map/ppermute | solution.py:370
  74.8 1.6 %collective-permute-done.22.p_ref = f32[16,32,128]{2,1,0:T(8,128)S(1)} collective-permute-done((f32[16,32,128]{2,1,0:T(8,128)S(1)}, f32[16,32,128]{2,1,0:T(8,128)S(1)}, u32[]{:S(2)}, u32[]{:S(2)}) %collective-permute-start.22) | collective-permute-done | bytes 262176 | tf_op jit(solution)/shard_map/ppermute | solution.py:370
  76.7 1.3 %collective-permute-start.24 = (f32[16,32,128]{2,1,0:T(8,128)S(1)}, f32[16,32,128]{2,1,0:T(8,128)S(1)}, u32[]{:S(2)}, u32[]{:S(2)}) collective-permute-start(f32[16,32,128]{2,1,0:T(8,128)S(1)} %level_6_32.1._.c_ref), channel_id=1, source_target_pairs={{0,2},{1,3},{2,0},{3,1},{4,6},{5,7},{6,4},{7,5},{8,10},{9,11},{10,... | collective-permute-start | bytes 786440 | tf_op jit(solution)/shard_map/ppermute | solution.py:370
  77.9 1.2 %collective-permute-start.23 = (f32[16,32,128]{2,1,0:T(8,128)S(1)}, f32[16,32,128]{2,1,0:T(8,128)S(1)}, u32[]{:S(2)}, u32[]{:S(2)}) collective-permute-start(f32[16,32,128]{2,1,0:T(8,128)S(1)} %level_7_16.1._.c_ref), channel_id=1, source_target_pairs={{0,4},{1,5},{2,6},{3,7},{4,0},{5,1},{6,2},{7,3},{8,12},{9,13},{10,... | collective-permute-start | bytes 786440 | tf_op jit(solution)/shard_map/ppermute | solution.py:370
  79.1 3.2 %collective-permute-done.21.p_ref = f32[16,32,128]{2,1,0:T(8,128)S(1)} collective-permute-done((f32[16,32,128]{2,1,0:T(8,128)S(1)}, f32[16,32,128]{2,1,0:T(8,128)S(1)}, u32[]{:S(2)}, u32[]{:S(2)}) %collective-permute-start.21) | collective-permute-done | bytes 262176 | tf_op jit(solution)/shard_map/ppermute | solution.py:370
  82.3 0.3 level_6_48.1._.c_ref
  82.6 2.3 %collective-permute-start.26 = (f32[16,32,128]{2,1,0:T(8,128)S(1)}, f32[16,32,128]{2,1,0:T(8,128)S(1)}, u32[]{:S(2)}, u32[]{:S(2)}) collective-permute-start(f32[16,32,128]{2,1,0:T(8,128)S(1)} %level_6_48.1._.c_ref), channel_id=1, source_target_pairs={{0,2},{1,3},{2,0},{3,1},{4,6},{5,7},{6,4},{7,5},{8,10},{9,11},{10,... | collective-permute-start | bytes 786440 | tf_op jit(solution)/shard_map/ppermute | solution.py:370
  84.9 0.7 last_0.1._.refs_0_
  85.6 3.7 %collective-permute-done.24.p_ref = f32[16,32,128]{2,1,0:T(8,128)S(1)} collective-permute-done((f32[16,32,128]{2,1,0:T(8,128)S(1)}, f32[16,32,128]{2,1,0:T(8,128)S(1)}, u32[]{:S(2)}, u32[]{:S(2)}) %collective-permute-start.24) | collective-permute-done | bytes 262176 | tf_op jit(solution)/shard_map/ppermute | solution.py:370
  89.3 0.3 level_7_32.1._.c_ref
  89.6 1.2 %collective-permute-start.25 = (f32[16,32,128]{2,1,0:T(8,128)S(1)}, f32[16,32,128]{2,1,0:T(8,128)S(1)}, u32[]{:S(2)}, u32[]{:S(2)}) collective-permute-start(f32[16,32,128]{2,1,0:T(8,128)S(1)} %level_7_32.1._.c_ref), channel_id=1, source_target_pairs={{0,4},{1,5},{2,6},{3,7},{4,0},{5,1},{6,2},{7,3},{8,12},{9,13},{10,... | collective-permute-start | bytes 786440 | tf_op jit(solution)/shard_map/ppermute | solution.py:370
  90.8 0.7 last_16.1._.refs_1_
  91.5 1.3 %collective-permute-done.26.p_ref = f32[16,32,128]{2,1,0:T(8,128)S(1)} collective-permute-done((f32[16,32,128]{2,1,0:T(8,128)S(1)}, f32[16,32,128]{2,1,0:T(8,128)S(1)}, u32[]{:S(2)}, u32[]{:S(2)}) %collective-permute-start.26) | collective-permute-done | bytes 262176 | tf_op jit(solution)/shard_map/ppermute | solution.py:370
  92.8 0.3 level_7_48.1._.c_ref
  93.1 1.3 %collective-permute-start.27 = (f32[16,32,128]{2,1,0:T(8,128)S(1)}, f32[16,32,128]{2,1,0:T(8,128)S(1)}, u32[]{:S(2)}, u32[]{:S(2)}) collective-permute-start(f32[16,32,128]{2,1,0:T(8,128)S(1)} %level_7_48.1._.c_ref), channel_id=1, source_target_pairs={{0,4},{1,5},{2,6},{3,7},{4,0},{5,1},{6,2},{7,3},{8,12},{9,13},{10,... | collective-permute-start | bytes 786440 | tf_op jit(solution)/shard_map/ppermute | solution.py:370
  94.4 3.9 %collective-permute-done.25.p_ref = f32[16,32,128]{2,1,0:T(8,128)S(1)} collective-permute-done((f32[16,32,128]{2,1,0:T(8,128)S(1)}, f32[16,32,128]{2,1,0:T(8,128)S(1)}, u32[]{:S(2)}, u32[]{:S(2)}) %collective-permute-start.25) | collective-permute-done | bytes 262176 | tf_op jit(solution)/shard_map/ppermute | solution.py:370
  98.3 0.7 last_32.1._.refs_2_
  99.0 2.7 %collective-permute-done.27.p_ref = f32[16,32,128]{2,1,0:T(8,128)S(1)} collective-permute-done((f32[16,32,128]{2,1,0:T(8,128)S(1)}, f32[16,32,128]{2,1,0:T(8,128)S(1)}, u32[]{:S(2)}, u32[]{:S(2)}) %collective-permute-start.27) | collective-permute-done | bytes 262176 | tf_op jit(solution)/shard_map/ppermute | solution.py:370
  101.7 0.7 last_48.1.refs_3_
  102.4 2.3 %output.1 = f32[64,128,128]{2,1,0:T(8,128)} custom-call(f32[64,2,16,128]{3,2,1,0:T(8,128)S(1)} %last_0.1._.refs_0_, f32[64,2,16,128]{3,2,1,0:T(8,128)S(1)} %last_16.1._.refs_1_, f32[64,2,16,128]{3,2,1,0:T(8,128)S(1)} %last_32.1._.refs_2_, f32[64,2,16,128]{3,2,1,0:T(8,128)S(1)} %last_48.1.refs_3_), custom_call_target="tpu_custom_call" | custom-call | tf_op jit(solution)/shard_map/output/pallas_call | solution.py:318
  (43 shorter events, 5.0 us)
Async XLA Ops:
  0.0 15.8 %slice-start = ((s8[9437184]{0:T(1024)(128)(4,1)}), s8[1048576]{0:T(1024)(128)(4,1)S(1)}, s32[]{:S(2)}) async-start(s8[9437184]{0:T(1024)(128)(4,1)} %bitcast), calls=%async_computation | async-start | bytes 2097152
  0.0 15.8 %slice-start.1 = ((s8[9437184]{0:T(1024)(128)(4,1)}), s8[4194304]{0:T(1024)(128)(4,1)S(1)}, s32[]{:S(2)}) async-start(s8[9437184]{0:T(1024)(128)(4,1)} %bitcast), calls=%async_computation.1 | async-start | bytes 8388608
  8.7 7.1 %slice-start.2 = ((s8[9437184]{0:T(1024)(128)(4,1)}), s8[4194304]{0:T(1024)(128)(4,1)S(1)}, s32[]{:S(2)}) async-start(s8[9437184]{0:T(1024)(128)(4,1)} %bitcast), calls=%async_computation.2 | async-start | bytes 8388608
  8.7 1.9 %collective-permute-start.1 = (f32[16,32,128]{2,1,0:T(8,128)S(1)}, f32[16,32,128]{2,1,0:T(8,128)S(1)}, u32[]{:S(2)}, u32[]{:S(2)}) collective-permute-start(f32[16,32,128]{2,1,0:T(8,128)S(1)} %source_0.1._.c_ref), channel_id=1, source_target_pairs={{0,8},{8,0},{16,24},{24,16},{32,40},{40,32},{48,56},{56,48},{64,72... | collective-permute-start | bytes 786440 | tf_op jit(solution)/shard_map/ppermute | solution.py:370
  10.0 3.0 %collective-permute-start = (f32[16,32,128]{2,1,0:T(8,128)S(1)}, f32[16,32,128]{2,1,0:T(8,128)S(1)}, u32[]{:S(2)}, u32[]{:S(2)}) collective-permute-start(f32[16,32,128]{2,1,0:T(8,128)S(1)} %source_16.1._.c_ref), channel_id=1, source_target_pairs={{0,8},{8,0},{16,24},{24,16},{32,40},{40,32},{48,56},{56,48},{64,72... | collective-permute-start | bytes 786440 | tf_op jit(solution)/shard_map/ppermute | solution.py:370
  10.9 9.2 %collective-permute-start.3 = (f32[16,32,128]{2,1,0:T(8,128)S(1)}, f32[16,32,128]{2,1,0:T(8,128)S(1)}, u32[]{:S(2)}, u32[]{:S(2)}) collective-permute-start(f32[16,32,128]{2,1,0:T(8,128)S(1)} %level_2_0.1._.c_ref), channel_id=1, source_target_pairs={{0,16},{8,24},{16,0},{24,8},{32,48},{40,56},{48,32},{56,40},{64,80... | collective-permute-start | bytes 786440 | tf_op jit(solution)/shard_map/ppermute | solution.py:370
  13.3 12.5 %collective-permute-start.2 = (f32[16,32,128]{2,1,0:T(8,128)S(1)}, f32[16,32,128]{2,1,0:T(8,128)S(1)}, u32[]{:S(2)}, u32[]{:S(2)}) collective-permute-start(f32[16,32,128]{2,1,0:T(8,128)S(1)} %level_2_16.1._.c_ref), channel_id=1, source_target_pairs={{0,16},{8,24},{16,0},{24,8},{32,48},{40,56},{48,32},{56,40},{64,80... | collective-permute-start | bytes 786440 | tf_op jit(solution)/shard_map/ppermute | solution.py:370
  20.4 14.5 %collective-permute-start.4 = (f32[16,32,128]{2,1,0:T(8,128)S(1)}, f32[16,32,128]{2,1,0:T(8,128)S(1)}, u32[]{:S(2)}, u32[]{:S(2)}) collective-permute-start(f32[16,32,128]{2,1,0:T(8,128)S(1)} %level_3_0.1._.c_ref), channel_id=1, source_target_pairs={{0,32},{8,40},{16,48},{24,56},{32,0},{40,8},{48,16},{56,24},{64,96... | collective-permute-start | bytes 786440 | tf_op jit(solution)/shard_map/ppermute | solution.py:370
  25.7 12.8 %collective-permute-start.8 = (f32[16,32,128]{2,1,0:T(8,128)S(1)}, f32[16,32,128]{2,1,0:T(8,128)S(1)}, u32[]{:S(2)}, u32[]{:S(2)}) collective-permute-start(f32[16,32,128]{2,1,0:T(8,128)S(1)} %source_32.1._.c_ref), channel_id=1, source_target_pairs={{0,8},{8,0},{16,24},{24,16},{32,40},{40,32},{48,56},{56,48},{64,72... | collective-permute-start | bytes 786440 | tf_op jit(solution)/shard_map/ppermute | solution.py:370
  26.1 14.3 %collective-permute-start.7 = (f32[16,32,128]{2,1,0:T(8,128)S(1)}, f32[16,32,128]{2,1,0:T(8,128)S(1)}, u32[]{:S(2)}, u32[]{:S(2)}) collective-permute-start(f32[16,32,128]{2,1,0:T(8,128)S(1)} %level_3_16.1._.c_ref), channel_id=1, source_target_pairs={{0,32},{8,40},{16,48},{24,56},{32,0},{40,8},{48,16},{56,24},{64,96... | collective-permute-start | bytes 786440 | tf_op jit(solution)/shard_map/ppermute | solution.py:370
  31.3 12.8 %collective-permute-start.6 = (f32[16,32,128]{2,1,0:T(8,128)S(1)}, f32[16,32,128]{2,1,0:T(8,128)S(1)}, u32[]{:S(2)}, u32[]{:S(2)}) collective-permute-start(f32[16,32,128]{2,1,0:T(8,128)S(1)} %source_48.1._.c_ref), channel_id=1, source_target_pairs={{0,8},{8,0},{16,24},{24,16},{32,40},{40,32},{48,56},{56,48},{64,72... | collective-permute-start | bytes 786440 | tf_op jit(solution)/shard_map/ppermute | solution.py:370
  35.3 9.3 %collective-permute-start.5 = (f32[16,32,128]{2,1,0:T(8,128)S(1)}, f32[16,32,128]{2,1,0:T(8,128)S(1)}, u32[]{:S(2)}, u32[]{:S(2)}) collective-permute-start(f32[16,32,128]{2,1,0:T(8,128)S(1)} %level_4_0.1._.c_ref), channel_id=1, source_target_pairs={{0,64},{8,72},{16,80},{24,88},{32,96},{40,104},{48,112},{56,120},{... | collective-permute-start | bytes 786440 | tf_op jit(solution)/shard_map/ppermute | solution.py:370
  38.8 7.6 %collective-permute-start.12 = (f32[16,32,128]{2,1,0:T(8,128)S(1)}, f32[16,32,128]{2,1,0:T(8,128)S(1)}, u32[]{:S(2)}, u32[]{:S(2)}) collective-permute-start(f32[16,32,128]{2,1,0:T(8,128)S(1)} %level_2_32.1._.c_ref), channel_id=1, source_target_pairs={{0,16},{8,24},{16,0},{24,8},{32,48},{40,56},{48,32},{56,40},{64,80... | collective-permute-start | bytes 786440 | tf_op jit(solution)/shard_map/ppermute | solution.py:370
  40.7 8.2 %collective-permute-start.11 = (f32[16,32,128]{2,1,0:T(8,128)S(1)}, f32[16,32,128]{2,1,0:T(8,128)S(1)}, u32[]{:S(2)}, u32[]{:S(2)}) collective-permute-start(f32[16,32,128]{2,1,0:T(8,128)S(1)} %level_4_16.1._.c_ref), channel_id=1, source_target_pairs={{0,64},{8,72},{16,80},{24,88},{32,96},{40,104},{48,112},{56,120},{... | collective-permute-start | bytes 786440 | tf_op jit(solution)/shard_map/ppermute | solution.py:370
  44.4 9.3 %collective-permute-start.10 = (f32[16,32,128]{2,1,0:T(8,128)S(1)}, f32[16,32,128]{2,1,0:T(8,128)S(1)}, u32[]{:S(2)}, u32[]{:S(2)}) collective-permute-start(f32[16,32,128]{2,1,0:T(8,128)S(1)} %level_2_48.1._.c_ref), channel_id=1, source_target_pairs={{0,16},{8,24},{16,0},{24,8},{32,48},{40,56},{48,32},{56,40},{64,80... | collective-permute-start | bytes 786440 | tf_op jit(solution)/shard_map/ppermute | solution.py:370
  44.9 5.9 %copy-start = (f32[128,32,128]{2,1,0:T(8,128)S(1)}, f32[128,32,128]{2,1,0:T(8,128)}, u32[]{:S(2)}) copy-start(f32[128,32,128]{2,1,0:T(8,128)} %ti_ref.1) | copy-start | bytes 6291460
  44.9 9.3 %collective-permute-start.9 = (f32[16,32,128]{2,1,0:T(8,128)S(1)}, f32[16,32,128]{2,1,0:T(8,128)S(1)}, u32[]{:S(2)}, u32[]{:S(2)}) collective-permute-start(f32[16,32,128]{2,1,0:T(8,128)S(1)} %level_5_0.1._.c_ref), channel_id=1, source_target_pairs={{0,1},{1,0},{2,3},{3,2},{4,5},{5,4},{6,7},{7,6},{8,9},{9,8},{10,11... | collective-permute-start | bytes 786440 | tf_op jit(solution)/shard_map/ppermute | solution.py:370
  46.8 11.2 %collective-permute-start.16 = (f32[16,32,128]{2,1,0:T(8,128)S(1)}, f32[16,32,128]{2,1,0:T(8,128)S(1)}, u32[]{:S(2)}, u32[]{:S(2)}) collective-permute-start(f32[16,32,128]{2,1,0:T(8,128)S(1)} %level_3_32.1._.c_ref), channel_id=1, source_target_pairs={{0,32},{8,40},{16,48},{24,56},{32,0},{40,8},{48,16},{56,24},{64,96... | collective-permute-start | bytes 786440 | tf_op jit(solution)/shard_map/ppermute | solution.py:370
  49.2 11.8 %collective-permute-start.15 = (f32[16,32,128]{2,1,0:T(8,128)S(1)}, f32[16,32,128]{2,1,0:T(8,128)S(1)}, u32[]{:S(2)}, u32[]{:S(2)}) collective-permute-start(f32[16,32,128]{2,1,0:T(8,128)S(1)} %level_5_16.1._.c_ref), channel_id=1, source_target_pairs={{0,1},{1,0},{2,3},{3,2},{4,5},{5,4},{6,7},{7,6},{8,9},{9,8},{10,11... | collective-permute-start | bytes 786440 | tf_op jit(solution)/shard_map/ppermute | solution.py:370
  54.1 10.3 %collective-permute-start.14 = (f32[16,32,128]{2,1,0:T(8,128)S(1)}, f32[16,32,128]{2,1,0:T(8,128)S(1)}, u32[]{:S(2)}, u32[]{:S(2)}) collective-permute-start(f32[16,32,128]{2,1,0:T(8,128)S(1)} %level_3_48.1._.c_ref), channel_id=1, source_target_pairs={{0,32},{8,40},{16,48},{24,56},{32,0},{40,8},{48,16},{56,24},{64,96... | collective-permute-start | bytes 786440 | tf_op jit(solution)/shard_map/ppermute | solution.py:370
  54.5 11.5 %collective-permute-start.13 = (f32[16,32,128]{2,1,0:T(8,128)S(1)}, f32[16,32,128]{2,1,0:T(8,128)S(1)}, u32[]{:S(2)}, u32[]{:S(2)}) collective-permute-start(f32[16,32,128]{2,1,0:T(8,128)S(1)} %level_6_0.1._.c_ref), channel_id=1, source_target_pairs={{0,2},{1,3},{2,0},{3,1},{4,6},{5,7},{6,4},{7,5},{8,10},{9,11},{10,... | collective-permute-start | bytes 786440 | tf_op jit(solution)/shard_map/ppermute | solution.py:370
  58.3 8.0 %collective-permute-start.20 = (f32[16,32,128]{2,1,0:T(8,128)S(1)}, f32[16,32,128]{2,1,0:T(8,128)S(1)}, u32[]{:S(2)}, u32[]{:S(2)}) collective-permute-start(f32[16,32,128]{2,1,0:T(8,128)S(1)} %level_4_32.1._.c_ref), channel_id=1, source_target_pairs={{0,64},{8,72},{16,80},{24,88},{32,96},{40,104},{48,112},{56,120},{... | collective-permute-start | bytes 786440 | tf_op jit(solution)/shard_map/ppermute | solution.py:370
  61.3 9.3 %collective-permute-start.19 = (f32[16,32,128]{2,1,0:T(8,128)S(1)}, f32[16,32,128]{2,1,0:T(8,128)S(1)}, u32[]{:S(2)}, u32[]{:S(2)}) collective-permute-start(f32[16,32,128]{2,1,0:T(8,128)S(1)} %level_6_16.1._.c_ref), channel_id=1, source_target_pairs={{0,2},{1,3},{2,0},{3,1},{4,6},{5,7},{6,4},{7,5},{8,10},{9,11},{10,... | collective-permute-start | bytes 786440 | tf_op jit(solution)/shard_map/ppermute | solution.py:370
  64.7 8.0 %collective-permute-start.18 = (f32[16,32,128]{2,1,0:T(8,128)S(1)}, f32[16,32,128]{2,1,0:T(8,128)S(1)}, u32[]{:S(2)}, u32[]{:S(2)}) collective-permute-start(f32[16,32,128]{2,1,0:T(8,128)S(1)} %level_4_48.1._.c_ref), channel_id=1, source_target_pairs={{0,64},{8,72},{16,80},{24,88},{32,96},{40,104},{48,112},{56,120},{... | collective-permute-start | bytes 786440 | tf_op jit(solution)/shard_map/ppermute | solution.py:370
  66.6 9.8 %collective-permute-start.22 = (f32[16,32,128]{2,1,0:T(8,128)S(1)}, f32[16,32,128]{2,1,0:T(8,128)S(1)}, u32[]{:S(2)}, u32[]{:S(2)}) collective-permute-start(f32[16,32,128]{2,1,0:T(8,128)S(1)} %level_5_32.1._.c_ref), channel_id=1, source_target_pairs={{0,1},{1,0},{2,3},{3,2},{4,5},{5,4},{6,7},{7,6},{8,9},{9,8},{10,11... | collective-permute-start | bytes 786440 | tf_op jit(solution)/shard_map/ppermute | solution.py:370
  73.0 9.3 %collective-permute-start.21 = (f32[16,32,128]{2,1,0:T(8,128)S(1)}, f32[16,32,128]{2,1,0:T(8,128)S(1)}, u32[]{:S(2)}, u32[]{:S(2)}) collective-permute-start(f32[16,32,128]{2,1,0:T(8,128)S(1)} %level_5_48.1._.c_ref), channel_id=1, source_target_pairs={{0,1},{1,0},{2,3},{3,2},{4,5},{5,4},{6,7},{7,6},{8,9},{9,8},{10,11... | collective-permute-start | bytes 786440 | tf_op jit(solution)/shard_map/ppermute | solution.py:370
  73.7 11.2 %collective-permute-start.17 = (f32[16,32,128]{2,1,0:T(8,128)S(1)}, f32[16,32,128]{2,1,0:T(8,128)S(1)}, u32[]{:S(2)}, u32[]{:S(2)}) collective-permute-start(f32[16,32,128]{2,1,0:T(8,128)S(1)} %level_7_0.1._.c_ref), channel_id=1, source_target_pairs={{0,4},{1,5},{2,6},{3,7},{4,0},{5,1},{6,2},{7,3},{8,12},{9,13},{10,... | collective-permute-start | bytes 786440 | tf_op jit(solution)/shard_map/ppermute | solution.py:370
  76.7 12.6 %collective-permute-start.24 = (f32[16,32,128]{2,1,0:T(8,128)S(1)}, f32[16,32,128]{2,1,0:T(8,128)S(1)}, u32[]{:S(2)}, u32[]{:S(2)}) collective-permute-start(f32[16,32,128]{2,1,0:T(8,128)S(1)} %level_6_32.1._.c_ref), channel_id=1, source_target_pairs={{0,2},{1,3},{2,0},{3,1},{4,6},{5,7},{6,4},{7,5},{8,10},{9,11},{10,... | collective-permute-start | bytes 786440 | tf_op jit(solution)/shard_map/ppermute | solution.py:370
  77.9 12.8 %collective-permute-start.23 = (f32[16,32,128]{2,1,0:T(8,128)S(1)}, f32[16,32,128]{2,1,0:T(8,128)S(1)}, u32[]{:S(2)}, u32[]{:S(2)}) collective-permute-start(f32[16,32,128]{2,1,0:T(8,128)S(1)} %level_7_16.1._.c_ref), channel_id=1, source_target_pairs={{0,4},{1,5},{2,6},{3,7},{4,0},{5,1},{6,2},{7,3},{8,12},{9,13},{10,... | collective-permute-start | bytes 786440 | tf_op jit(solution)/shard_map/ppermute | solution.py:370
  82.6 10.2 %collective-permute-start.26 = (f32[16,32,128]{2,1,0:T(8,128)S(1)}, f32[16,32,128]{2,1,0:T(8,128)S(1)}, u32[]{:S(2)}, u32[]{:S(2)}) collective-permute-start(f32[16,32,128]{2,1,0:T(8,128)S(1)} %level_6_48.1._.c_ref), channel_id=1, source_target_pairs={{0,2},{1,3},{2,0},{3,1},{4,6},{5,7},{6,4},{7,5},{8,10},{9,11},{10,... | collective-permute-start | bytes 786440 | tf_op jit(solution)/shard_map/ppermute | solution.py:370
  89.6 8.7 %collective-permute-start.25 = (f32[16,32,128]{2,1,0:T(8,128)S(1)}, f32[16,32,128]{2,1,0:T(8,128)S(1)}, u32[]{:S(2)}, u32[]{:S(2)}) collective-permute-start(f32[16,32,128]{2,1,0:T(8,128)S(1)} %level_7_32.1._.c_ref), channel_id=1, source_target_pairs={{0,4},{1,5},{2,6},{3,7},{4,0},{5,1},{6,2},{7,3},{8,12},{9,13},{10,... | collective-permute-start | bytes 786440 | tf_op jit(solution)/shard_map/ppermute | solution.py:370
  93.1 8.5 %collective-permute-start.27 = (f32[16,32,128]{2,1,0:T(8,128)S(1)}, f32[16,32,128]{2,1,0:T(8,128)S(1)}, u32[]{:S(2)}, u32[]{:S(2)}) collective-permute-start(f32[16,32,128]{2,1,0:T(8,128)S(1)} %level_7_48.1._.c_ref), channel_id=1, source_target_pairs={{0,4},{1,5},{2,6},{3,7},{4,0},{5,1},{6,2},{7,3},{8,12},{9,13},{10,... | collective-permute-start | bytes 786440 | tf_op jit(solution)/shard_map/ppermute | solution.py:370

commit v4 on v3

--- a/solution.py
+++ b/solution.py
@@ -13,7 +13,7 @@
 VMEM = pl.BlockSpec(memory_space=pltpu.VMEM)
 ANY = pl.BlockSpec(memory_space=pl.ANY)
 NEAR_ZERO = pl.CostEstimate(flops=1, bytes_accessed=1, transcendentals=0)
-STEP = (0, 1, 0, 1, -1, -3, -4, -5, -6, -7, 0, 2, 1, 3, -8, 0, 2, 1, 3, 0, 2, 1, -9, 3, 0, 2, 1, 3, 0, 2, 1, 3, 2, 3, 0, 2, 1, 3, 2, 3)
+STEP = (0, 1, 0, 1, -1, -3, -4, -5, -6, -7, 0, 2, 1, 3, -8, 0, 2, 1, 3, 0, 2, 1, -9, 3, 0, 1, 2, 3, 0, 2, 1, 3, 2, 3, 0, 2, 1, 3, 2, 3)
 ORDER = [("step", i) if i >= 0 else ("prepare", -i) for i in STEP]
 
 

time: 105 us -> 105 us (level)
  no operation moved by 1% of the time
where the time goes in v4:
time: 105 us
  starting transfers between devices  42.9 us (41%)
  Pallas kernels  31.4 us (30%)
  waiting for transfers between devices  29.6 us (28%)
    ppermute x28, starting transfers between devices, exchange(): return lax.ppermute(c, axis, [(i, i ^ 1 << bit) for i in range(size)])  42.9 us
    ppermute x28, waiting for transfers between devices, exchange(): return lax.ppermute(c, axis, [(i, i ^ 1 << bit) for i in range(size)])  29.6 us
    pallas_call x1, Pallas kernels, source_prepare(): pl.pallas_call(kernel, name='source_prepare', in_specs=[hbm] * 3, out_spe...  7.49 us
    pallas_call x24, Pallas kernels, level_stage(): pl.pallas_call(kernel, name=f'level_{level}_{first}', in_specs=[VMEM] * 3...  7.08 us
    pallas_call x4, Pallas kernels, source_stage(): pl.pallas_call(kernel, name=f'source_{first}', in_specs=[VMEM] * 4 + [ANY...  4.81 us
    pallas_call x6, Pallas kernels, transfer_stage(): pl.pallas_call(kernel, name=f'transfer_{level}', in_specs=[VMEM, ANY], ou...  4.36 us
    pallas_call x4, Pallas kernels, last_stage(): pl.pallas_call(kernel, name=f'last_{first}', in_specs=[VMEM] * 4 + [ANY],...  2.86 us
    pallas_call x1, Pallas kernels, output_stage(): pl.pallas_call(kernel, name='output', in_specs=[VMEM] * len(parts), out_s...  2.27 us
  transfers between devices with their start and end apart: 28, of which 15 were waited for; matrix products, arithmetic and copies ran while one was open for 0% of the time, Pallas kernels for 19%

profile of v4, /device:TPU:0, one launch (start us, length us, event | category | flops | bytes accessed | tf_op | source)
XLA Modules:
  0.0 104.5 jit_solution(2756745828949734778)
XLA Ops:
  0.0 7.5 %source_prepare.1 = (f32[64,64,128]{2,1,0:T(8,128)S(1)}, f32[64,32,128]{2,1,0:T(8,128)S(1)}, bf16[32,64,128]{2,1,0:T(8,128)(2,1)S(1)}, bf16[32,64,128]{2,1,0:T(8...) custom-call(f32[64,128,128]{2,1,0:T(8,128)} %src_hbm.1, ...), custom_call_target="tpu_custom_call" | custom-call | tf_op jit(solution)/shard_map/source_prepare/pallas_call | solution.py:129
  7.5 1.2 %source_0.1._.c_ref = f32[16,32,128]{2,1,0:T(8,128)S(1)} custom-call(f32[64,64,128]{2,1,0:T(8,128)S(1)} %get-tuple-element.22.s_ref, f32[64,32,128]{2,1,0:T(8,128)S(1)} %get-tuple-element.23.m_ref, bf16[32,64,128]{2,1,0:T(8,128)(2,1)S(1)} %get-tuple-element.24.t0_ref._, bf16[32,64,128]{2,1,0:T(8,128)(2,1)S(1)} %get-tuple-element.25.t1_ref, ...), custom_call_target="tpu_custom_call" | custom-call | flops 1 | bytes 1 | tf_op jit(solution)/shard_map/source_0/pallas_call | solution.py:193
  8.8 1.2 %source_16.1._.c_ref = f32[16,32,128]{2,1,0:T(8,128)S(1)} custom-call(f32[64,64,128]{2,1,0:T(8,128)S(1)} %get-tuple-element.22.s_ref, f32[64,32,128]{2,1,0:T(8,128)S(1)} %get-tuple-element.23.m_ref, bf16[32,64,128]{2,1,0:T(8,128)(2,1)S(1)} %get-tuple-element.24.t0_ref._, bf16[32,64,128]{2,1,0:T(8,128)(2,1)S(1)} %get-tuple-element.25.t1_ref, ...), custom_call_target="tpu_custom_call" | custom-call | flops 1 | bytes 1 | tf_op jit(solution)/shard_map/source_16/pallas_call | solution.py:193
  10.0 0.6 collective-permute-start
  10.9 2.1 %collective-permute-start.3 = (f32[16,32,128]{2,1,0:T(8,128)S(1)}, f32[16,32,128]{2,1,0:T(8,128)S(1)}, u32[]{:S(2)}, u32[]{:S(2)}) collective-permute-start(f32[16,32,128]{2,1,0:T(8,128)S(1)} %level_2_0.1._.c_ref), channel_id=1, source_target_pairs={{0,16},{8,24},{16,0},{24,8},{32,48},{40,56},{48,32},{56,40},{64,80... | collective-permute-start | bytes 786440 | tf_op jit(solution)/shard_map/ppermute | solution.py:370
  13.3 1.0 collective-permute-start.2
  14.3 1.4 %source_rest.1 = (f32[64,64,128]{2,1,0:T(8,128)S(1)}, f32[64,32,128]{2,1,0:T(8,128)S(1)}, bf16[32,64,128]{2,1,0:T(8,128)(2,1)S(1)}, bf16[32,64,128]{2,1,0:T(8,128)(2,1)S(1)}, bf16[32,64,128]{2,1,0:T(8,128)(2,1)S(1)}) custom-call(f32[64,64,128]{2,1,0:T(8,128)S(1)} %get-tuple-element.18.us_ref, f32[32,64,128]{2,1,0:T(8,128)S(1)} %get-tuple-element.19.um_ref, ...), custom_call_target="tpu_custom_call" | custom-call | flops 1 | bytes 1 | tf_op jit(solution)/shard_map/source_rest/pallas_call | solution.py:166
  15.8 0.7 transfer_3.1._.t_ref
  16.6 0.7 transfer_4.1._.t_ref
  17.3 0.7 transfer_5.1._.t_ref
  18.0 0.7 transfer_6.1._.t_ref
  18.8 0.7 transfer_7.1._.t_ref
  19.5 0.6 collective-permute-done.3.p_ref
  20.1 0.3 level_3_0.1._.c_ref
  20.4 4.1 %collective-permute-start.4 = (f32[16,32,128]{2,1,0:T(8,128)S(1)}, f32[16,32,128]{2,1,0:T(8,128)S(1)}, u32[]{:S(2)}, u32[]{:S(2)}) collective-permute-start(f32[16,32,128]{2,1,0:T(8,128)S(1)} %level_3_0.1._.c_ref), channel_id=1, source_target_pairs={{0,32},{8,40},{16,48},{24,56},{32,0},{40,8},{48,16},{56,24},{64,96... | collective-permute-start | bytes 786440 | tf_op jit(solution)/shard_map/ppermute | solution.py:370
  24.5 1.2 %source_32.1._.c_ref = f32[16,32,128]{2,1,0:T(8,128)S(1)} custom-call(f32[64,64,128]{2,1,0:T(8,128)S(1)} %get-tuple-element.26.s_ref, f32[64,32,128]{2,1,0:T(8,128)S(1)} %get-tuple-element.27.m_ref, bf16[32,64,128]{2,1,0:T(8,128)(2,1)S(1)} %get-tuple-element.28._.t0_ref, bf16[32,64,128]{2,1,0:T(8,128)(2,1)S(1)} %get-tuple-element.29.t1_ref, ...), custom_call_target="tpu_custom_call" | custom-call | flops 1 | bytes 1 | tf_op jit(solution)/shard_map/source_32/pallas_call | solution.py:193
  25.8 0.3 level_3_16.1._.c_ref
  26.1 4.0 %collective-permute-start.7 = (f32[16,32,128]{2,1,0:T(8,128)S(1)}, f32[16,32,128]{2,1,0:T(8,128)S(1)}, u32[]{:S(2)}, u32[]{:S(2)}) collective-permute-start(f32[16,32,128]{2,1,0:T(8,128)S(1)} %level_3_16.1._.c_ref), channel_id=1, source_target_pairs={{0,32},{8,40},{16,48},{24,56},{32,0},{40,8},{48,16},{56,24},{64,96... | collective-permute-start | bytes 786440 | tf_op jit(solution)/shard_map/ppermute | solution.py:370
  30.1 1.2 %source_48.1._.c_ref = f32[16,32,128]{2,1,0:T(8,128)S(1)} custom-call(f32[64,64,128]{2,1,0:T(8,128)S(1)} %get-tuple-element.26.s_ref, f32[64,32,128]{2,1,0:T(8,128)S(1)} %get-tuple-element.27.m_ref, bf16[32,64,128]{2,1,0:T(8,128)(2,1)S(1)} %get-tuple-element.28._.t0_ref, bf16[32,64,128]{2,1,0:T(8,128)(2,1)S(1)} %get-tuple-element.29.t1_ref, ...), custom_call_target="tpu_custom_call" | custom-call | flops 1 | bytes 1 | tf_op jit(solution)/shard_map/source_48/pallas_call | solution.py:193
  31.4 0.7 transfer_8.1._.t_ref
  32.2 2.8 %collective-permute-done.4.p_ref = f32[16,32,128]{2,1,0:T(8,128)S(1)} collective-permute-done((f32[16,32,128]{2,1,0:T(8,128)S(1)}, f32[16,32,128]{2,1,0:T(8,128)S(1)}, u32[]{:S(2)}, u32[]{:S(2)}) %collective-permute-start.4) | collective-permute-done | bytes 262176 | tf_op jit(solution)/shard_map/ppermute | solution.py:370
  35.3 3.3 %collective-permute-start.5 = (f32[16,32,128]{2,1,0:T(8,128)S(1)}, f32[16,32,128]{2,1,0:T(8,128)S(1)}, u32[]{:S(2)}, u32[]{:S(2)}) collective-permute-start(f32[16,32,128]{2,1,0:T(8,128)S(1)} %level_4_0.1._.c_ref), channel_id=1, source_target_pairs={{0,64},{8,72},{16,80},{24,88},{32,96},{40,104},{48,112},{56,120},{... | collective-permute-start | bytes 786440 | tf_op jit(solution)/shard_map/ppermute | solution.py:370
  38.9 1.5 %collective-permute-done.7.p_ref = f32[16,32,128]{2,1,0:T(8,128)S(1)} collective-permute-done((f32[16,32,128]{2,1,0:T(8,128)S(1)}, f32[16,32,128]{2,1,0:T(8,128)S(1)}, u32[]{:S(2)}, u32[]{:S(2)}) %collective-permute-start.7) | collective-permute-done | bytes 262176 | tf_op jit(solution)/shard_map/ppermute | solution.py:370
  40.4 0.3 level_4_16.1._.c_ref
  40.7 3.4 %collective-permute-start.11 = (f32[16,32,128]{2,1,0:T(8,128)S(1)}, f32[16,32,128]{2,1,0:T(8,128)S(1)}, u32[]{:S(2)}, u32[]{:S(2)}) collective-permute-start(f32[16,32,128]{2,1,0:T(8,128)S(1)} %level_4_16.1._.c_ref), channel_id=1, source_target_pairs={{0,64},{8,72},{16,80},{24,88},{32,96},{40,104},{48,112},{56,120},{... | collective-permute-start | bytes 786440 | tf_op jit(solution)/shard_map/ppermute | solution.py:370
  44.1 0.3 level_2_48.1._.c_ref
  44.6 0.3 level_5_0.1._.c_ref
  44.9 1.8 %collective-permute-start.9 = (f32[16,32,128]{2,1,0:T(8,128)S(1)}, f32[16,32,128]{2,1,0:T(8,128)S(1)}, u32[]{:S(2)}, u32[]{:S(2)}) collective-permute-start(f32[16,32,128]{2,1,0:T(8,128)S(1)} %level_5_0.1._.c_ref), channel_id=1, source_target_pairs={{0,1},{1,0},{2,3},{3,2},{4,5},{5,4},{6,7},{7,6},{8,9},{9,8},{10,11... | collective-permute-start | bytes 786440 | tf_op jit(solution)/shard_map/ppermute | solution.py:370
  47.0 1.9 %collective-permute-done.11.p_ref = f32[16,32,128]{2,1,0:T(8,128)S(1)} collective-permute-done((f32[16,32,128]{2,1,0:T(8,128)S(1)}, f32[16,32,128]{2,1,0:T(8,128)S(1)}, u32[]{:S(2)}, u32[]{:S(2)}) %collective-permute-start.11) | collective-permute-done | bytes 262176 | tf_op jit(solution)/shard_map/ppermute | solution.py:370
  49.2 1.6 %collective-permute-start.16 = (f32[16,32,128]{2,1,0:T(8,128)S(1)}, f32[16,32,128]{2,1,0:T(8,128)S(1)}, u32[]{:S(2)}, u32[]{:S(2)}) collective-permute-start(f32[16,32,128]{2,1,0:T(8,128)S(1)} %level_5_16.1._.c_ref), channel_id=1, source_target_pairs={{0,1},{1,0},{2,3},{3,2},{4,5},{5,4},{6,7},{7,6},{8,9},{9,8},{10,11... | collective-permute-start | bytes 786440 | tf_op jit(solution)/shard_map/ppermute | solution.py:370
  51.0 1.1 %target_matrix.1._.m_ref = f32[128,32,128]{2,1,0:T(8,128)S(1)} custom-call(f32[128,32,128]{2,1,0:T(8,128)S(1)} %copy-done, f32[16,32,128]{2,1,0:T(8,128)S(1)} %level_5_16.1._.c_ref), custom_call_target="tpu_custom_call" | custom-call | flops 1 | bytes 1 | tf_op jit(solution)/shard_map/target_matrix/pallas_call | solution.py:235
  52.1 0.3 level_3_48.1._.c_ref
  52.4 3.4 %collective-permute-start.14 = (f32[16,32,128]{2,1,0:T(8,128)S(1)}, f32[16,32,128]{2,1,0:T(8,128)S(1)}, u32[]{:S(2)}, u32[]{:S(2)}) collective-permute-start(f32[16,32,128]{2,1,0:T(8,128)S(1)} %level_3_48.1._.c_ref), channel_id=1, source_target_pairs={{0,32},{8,40},{16,48},{24,56},{32,0},{40,8},{48,16},{56,24},{64,96... | collective-permute-start | bytes 786440 | tf_op jit(solution)/shard_map/ppermute | solution.py:370
  56.1 2.8 %collective-permute-start.13 = (f32[16,32,128]{2,1,0:T(8,128)S(1)}, f32[16,32,128]{2,1,0:T(8,128)S(1)}, u32[]{:S(2)}, u32[]{:S(2)}) collective-permute-start(f32[16,32,128]{2,1,0:T(8,128)S(1)} %level_6_0.1._.c_ref), channel_id=1, source_target_pairs={{0,2},{1,3},{2,0},{3,1},{4,6},{5,7},{6,4},{7,5},{8,10},{9,11},{10,... | collective-permute-start | bytes 786440 | tf_op jit(solution)/shard_map/ppermute | solution.py:370
  59.2 1.3 %collective-permute-done.15.p_ref = f32[16,32,128]{2,1,0:T(8,128)S(1)} collective-permute-done((f32[16,32,128]{2,1,0:T(8,128)S(1)}, f32[16,32,128]{2,1,0:T(8,128)S(1)}, u32[]{:S(2)}, u32[]{:S(2)}) %collective-permute-start.15) | collective-permute-done | bytes 262176 | tf_op jit(solution)/shard_map/ppermute | solution.py:370
  60.5 0.3 level_4_32.1._.c_ref
  60.8 3.1 %collective-permute-start.20 = (f32[16,32,128]{2,1,0:T(8,128)S(1)}, f32[16,32,128]{2,1,0:T(8,128)S(1)}, u32[]{:S(2)}, u32[]{:S(2)}) collective-permute-start(f32[16,32,128]{2,1,0:T(8,128)S(1)} %level_4_32.1._.c_ref), channel_id=1, source_target_pairs={{0,64},{8,72},{16,80},{24,88},{32,96},{40,104},{48,112},{56,120},{... | collective-permute-start | bytes 786440 | tf_op jit(solution)/shard_map/ppermute | solution.py:370
  63.9 2.7 %collective-permute-start.19 = (f32[16,32,128]{2,1,0:T(8,128)S(1)}, f32[16,32,128]{2,1,0:T(8,128)S(1)}, u32[]{:S(2)}, u32[]{:S(2)}) collective-permute-start(f32[16,32,128]{2,1,0:T(8,128)S(1)} %level_6_16.1._.c_ref), channel_id=1, source_target_pairs={{0,2},{1,3},{2,0},{3,1},{4,6},{5,7},{6,4},{7,5},{8,10},{9,11},{10,... | collective-permute-start | bytes 786440 | tf_op jit(solution)/shard_map/ppermute | solution.py:370
  66.7 0.3 level_4_48.1._.c_ref
  67.0 0.6 collective-permute-start.18
  67.8 2.6 %collective-permute-done.20.p_ref = f32[16,32,128]{2,1,0:T(8,128)S(1)} collective-permute-done((f32[16,32,128]{2,1,0:T(8,128)S(1)}, f32[16,32,128]{2,1,0:T(8,128)S(1)}, u32[]{:S(2)}, u32[]{:S(2)}) %collective-permute-start.20) | collective-permute-done | bytes 262176 | tf_op jit(solution)/shard_map/ppermute | solution.py:370
  70.4 0.3 level_5_32.1._.c_ref
  70.7 0.3 collective-permute-start.22
  71.0 3.6 %collective-permute-done.19.p_ref = f32[16,32,128]{2,1,0:T(8,128)S(1)} collective-permute-done((f32[16,32,128]{2,1,0:T(8,128)S(1)}, f32[16,32,128]{2,1,0:T(8,128)S(1)}, u32[]{:S(2)}, u32[]{:S(2)}) %collective-permute-start.19) | collective-permute-done | bytes 262176 | tf_op jit(solution)/shard_map/ppermute | solution.py:370
  74.6 0.3 level_7_16.1._.c_ref
  74.9 1.9 %collective-permute-done.18.p_ref = f32[16,32,128]{2,1,0:T(8,128)S(1)} collective-permute-done((f32[16,32,128]{2,1,0:T(8,128)S(1)}, f32[16,32,128]{2,1,0:T(8,128)S(1)}, u32[]{:S(2)}, u32[]{:S(2)}) %collective-permute-start.18) | collective-permute-done | bytes 262176 | tf_op jit(solution)/shard_map/ppermute | solution.py:370
  76.8 0.3 level_5_48.1._.c_ref
  77.2 1.4 %collective-permute-start.17 = (f32[16,32,128]{2,1,0:T(8,128)S(1)}, f32[16,32,128]{2,1,0:T(8,128)S(1)}, u32[]{:S(2)}, u32[]{:S(2)}) collective-permute-start(f32[16,32,128]{2,1,0:T(8,128)S(1)} %level_7_0.1._.c_ref), channel_id=1, source_target_pairs={{0,4},{1,5},{2,6},{3,7},{4,0},{5,1},{6,2},{7,3},{8,12},{9,13},{10,... | collective-permute-start | bytes 786440 | tf_op jit(solution)/shard_map/ppermute | solution.py:370
  78.5 1.5 %collective-permute-done.22.p_ref = f32[16,32,128]{2,1,0:T(8,128)S(1)} collective-permute-done((f32[16,32,128]{2,1,0:T(8,128)S(1)}, f32[16,32,128]{2,1,0:T(8,128)S(1)}, u32[]{:S(2)}, u32[]{:S(2)}) %collective-permute-start.22) | collective-permute-done | bytes 262176 | tf_op jit(solution)/shard_map/ppermute | solution.py:370
  80.3 2.1 %collective-permute-start.24 = (f32[16,32,128]{2,1,0:T(8,128)S(1)}, f32[16,32,128]{2,1,0:T(8,128)S(1)}, u32[]{:S(2)}, u32[]{:S(2)}) collective-permute-start(f32[16,32,128]{2,1,0:T(8,128)S(1)} %level_6_32.1._.c_ref), channel_id=1, source_target_pairs={{0,2},{1,3},{2,0},{3,1},{4,6},{5,7},{6,4},{7,5},{8,10},{9,11},{10,... | collective-permute-start | bytes 786440 | tf_op jit(solution)/shard_map/ppermute | solution.py:370
  82.4 0.8 collective-permute-start.23
  83.2 3.1 %collective-permute-done.21.p_ref = f32[16,32,128]{2,1,0:T(8,128)S(1)} collective-permute-done((f32[16,32,128]{2,1,0:T(8,128)S(1)}, f32[16,32,128]{2,1,0:T(8,128)S(1)}, u32[]{:S(2)}, u32[]{:S(2)}) %collective-permute-start.21) | collective-permute-done | bytes 262176 | tf_op jit(solution)/shard_map/ppermute | solution.py:370
  86.6 1.4 %collective-permute-start.26 = (f32[16,32,128]{2,1,0:T(8,128)S(1)}, f32[16,32,128]{2,1,0:T(8,128)S(1)}, u32[]{:S(2)}, u32[]{:S(2)}) collective-permute-start(f32[16,32,128]{2,1,0:T(8,128)S(1)} %level_6_48.1._.c_ref), channel_id=1, source_target_pairs={{0,2},{1,3},{2,0},{3,1},{4,6},{5,7},{6,4},{7,5},{8,10},{9,11},{10,... | collective-permute-start | bytes 786440 | tf_op jit(solution)/shard_map/ppermute | solution.py:370
  88.0 0.7 last_0.1._.refs_0_
  88.8 1.6 %collective-permute-done.24.p_ref = f32[16,32,128]{2,1,0:T(8,128)S(1)} collective-permute-done((f32[16,32,128]{2,1,0:T(8,128)S(1)}, f32[16,32,128]{2,1,0:T(8,128)S(1)}, u32[]{:S(2)}, u32[]{:S(2)}) %collective-permute-start.24) | collective-permute-done | bytes 262176 | tf_op jit(solution)/shard_map/ppermute | solution.py:370
  90.7 0.7 collective-permute-start.25
  91.5 0.7 last_16.1._.refs_1_
  92.2 2.4 %collective-permute-done.26.p_ref = f32[16,32,128]{2,1,0:T(8,128)S(1)} collective-permute-done((f32[16,32,128]{2,1,0:T(8,128)S(1)}, f32[16,32,128]{2,1,0:T(8,128)S(1)}, u32[]{:S(2)}, u32[]{:S(2)}) %collective-permute-start.26) | collective-permute-done | bytes 262176 | tf_op jit(solution)/shard_map/ppermute | solution.py:370
  94.9 1.1 %collective-permute-start.27 = (f32[16,32,128]{2,1,0:T(8,128)S(1)}, f32[16,32,128]{2,1,0:T(8,128)S(1)}, u32[]{:S(2)}, u32[]{:S(2)}) collective-permute-start(f32[16,32,128]{2,1,0:T(8,128)S(1)} %level_7_48.1._.c_ref), channel_id=1, source_target_pairs={{0,4},{1,5},{2,6},{3,7},{4,0},{5,1},{6,2},{7,3},{8,12},{9,13},{10,... | collective-permute-start | bytes 786440 | tf_op jit(solution)/shard_map/ppermute | solution.py:370
  96.0 1.4 %collective-permute-done.25.p_ref = f32[16,32,128]{2,1,0:T(8,128)S(1)} collective-permute-done((f32[16,32,128]{2,1,0:T(8,128)S(1)}, f32[16,32,128]{2,1,0:T(8,128)S(1)}, u32[]{:S(2)}, u32[]{:S(2)}) %collective-permute-start.25) | collective-permute-done | bytes 262176 | tf_op jit(solution)/shard_map/ppermute | solution.py:370
  97.4 0.7 last_32.1._.refs_2_
  98.1 3.2 %collective-permute-done.27.p_ref = f32[16,32,128]{2,1,0:T(8,128)S(1)} collective-permute-done((f32[16,32,128]{2,1,0:T(8,128)S(1)}, f32[16,32,128]{2,1,0:T(8,128)S(1)}, u32[]{:S(2)}, u32[]{:S(2)}) %collective-permute-start.27) | collective-permute-done | bytes 262176 | tf_op jit(solution)/shard_map/ppermute | solution.py:370
  101.3 0.7 last_48.1.refs_3_
  102.1 2.3 %output.1 = f32[64,128,128]{2,1,0:T(8,128)} custom-call(f32[64,2,16,128]{3,2,1,0:T(8,128)S(1)} %last_0.1._.refs_0_, f32[64,2,16,128]{3,2,1,0:T(8,128)S(1)} %last_16.1._.refs_1_, f32[64,2,16,128]{3,2,1,0:T(8,128)S(1)} %last_32.1._.refs_2_, f32[64,2,16,128]{3,2,1,0:T(8,128)S(1)} %last_48.1.refs_3_), custom_call_target="tpu_custom_call" | custom-call | tf_op jit(solution)/shard_map/output/pallas_call | solution.py:318
  (43 shorter events, 4.7 us)
Async XLA Ops:
  0.0 15.8 %slice-start = ((s8[9437184]{0:T(1024)(128)(4,1)}), s8[1048576]{0:T(1024)(128)(4,1)S(1)}, s32[]{:S(2)}) async-start(s8[9437184]{0:T(1024)(128)(4,1)} %bitcast), calls=%async_computation | async-start | bytes 2097152
  0.0 15.8 %slice-start.1 = ((s8[9437184]{0:T(1024)(128)(4,1)}), s8[4194304]{0:T(1024)(128)(4,1)S(1)}, s32[]{:S(2)}) async-start(s8[9437184]{0:T(1024)(128)(4,1)} %bitcast), calls=%async_computation.1 | async-start | bytes 8388608
  8.7 7.1 %slice-start.2 = ((s8[9437184]{0:T(1024)(128)(4,1)}), s8[4194304]{0:T(1024)(128)(4,1)S(1)}, s32[]{:S(2)}) async-start(s8[9437184]{0:T(1024)(128)(4,1)} %bitcast), calls=%async_computation.2 | async-start | bytes 8388608
  8.7 1.9 %collective-permute-start.1 = (f32[16,32,128]{2,1,0:T(8,128)S(1)}, f32[16,32,128]{2,1,0:T(8,128)S(1)}, u32[]{:S(2)}, u32[]{:S(2)}) collective-permute-start(f32[16,32,128]{2,1,0:T(8,128)S(1)} %source_0.1._.c_ref), channel_id=1, source_target_pairs={{0,8},{8,0},{16,24},{24,16},{32,40},{40,32},{48,56},{56,48},{64,72... | collective-permute-start | bytes 786440 | tf_op jit(solution)/shard_map/ppermute | solution.py:370
  10.0 3.0 %collective-permute-start = (f32[16,32,128]{2,1,0:T(8,128)S(1)}, f32[16,32,128]{2,1,0:T(8,128)S(1)}, u32[]{:S(2)}, u32[]{:S(2)}) collective-permute-start(f32[16,32,128]{2,1,0:T(8,128)S(1)} %source_16.1._.c_ref), channel_id=1, source_target_pairs={{0,8},{8,0},{16,24},{24,16},{32,40},{40,32},{48,56},{56,48},{64,72... | collective-permute-start | bytes 786440 | tf_op jit(solution)/shard_map/ppermute | solution.py:370
  10.9 9.2 %collective-permute-start.3 = (f32[16,32,128]{2,1,0:T(8,128)S(1)}, f32[16,32,128]{2,1,0:T(8,128)S(1)}, u32[]{:S(2)}, u32[]{:S(2)}) collective-permute-start(f32[16,32,128]{2,1,0:T(8,128)S(1)} %level_2_0.1._.c_ref), channel_id=1, source_target_pairs={{0,16},{8,24},{16,0},{24,8},{32,48},{40,56},{48,32},{56,40},{64,80... | collective-permute-start | bytes 786440 | tf_op jit(solution)/shard_map/ppermute | solution.py:370
  13.3 12.5 %collective-permute-start.2 = (f32[16,32,128]{2,1,0:T(8,128)S(1)}, f32[16,32,128]{2,1,0:T(8,128)S(1)}, u32[]{:S(2)}, u32[]{:S(2)}) collective-permute-start(f32[16,32,128]{2,1,0:T(8,128)S(1)} %level_2_16.1._.c_ref), channel_id=1, source_target_pairs={{0,16},{8,24},{16,0},{24,8},{32,48},{40,56},{48,32},{56,40},{64,80... | collective-permute-start | bytes 786440 | tf_op jit(solution)/shard_map/ppermute | solution.py:370
  20.4 14.5 %collective-permute-start.4 = (f32[16,32,128]{2,1,0:T(8,128)S(1)}, f32[16,32,128]{2,1,0:T(8,128)S(1)}, u32[]{:S(2)}, u32[]{:S(2)}) collective-permute-start(f32[16,32,128]{2,1,0:T(8,128)S(1)} %level_3_0.1._.c_ref), channel_id=1, source_target_pairs={{0,32},{8,40},{16,48},{24,56},{32,0},{40,8},{48,16},{56,24},{64,96... | collective-permute-start | bytes 786440 | tf_op jit(solution)/shard_map/ppermute | solution.py:370
  25.7 12.8 %collective-permute-start.8 = (f32[16,32,128]{2,1,0:T(8,128)S(1)}, f32[16,32,128]{2,1,0:T(8,128)S(1)}, u32[]{:S(2)}, u32[]{:S(2)}) collective-permute-start(f32[16,32,128]{2,1,0:T(8,128)S(1)} %source_32.1._.c_ref), channel_id=1, source_target_pairs={{0,8},{8,0},{16,24},{24,16},{32,40},{40,32},{48,56},{56,48},{64,72... | collective-permute-start | bytes 786440 | tf_op jit(solution)/shard_map/ppermute | solution.py:370
  26.1 14.3 %collective-permute-start.7 = (f32[16,32,128]{2,1,0:T(8,128)S(1)}, f32[16,32,128]{2,1,0:T(8,128)S(1)}, u32[]{:S(2)}, u32[]{:S(2)}) collective-permute-start(f32[16,32,128]{2,1,0:T(8,128)S(1)} %level_3_16.1._.c_ref), channel_id=1, source_target_pairs={{0,32},{8,40},{16,48},{24,56},{32,0},{40,8},{48,16},{56,24},{64,96... | collective-permute-start | bytes 786440 | tf_op jit(solution)/shard_map/ppermute | solution.py:370
  31.3 12.8 %collective-permute-start.6 = (f32[16,32,128]{2,1,0:T(8,128)S(1)}, f32[16,32,128]{2,1,0:T(8,128)S(1)}, u32[]{:S(2)}, u32[]{:S(2)}) collective-permute-start(f32[16,32,128]{2,1,0:T(8,128)S(1)} %source_48.1._.c_ref), channel_id=1, source_target_pairs={{0,8},{8,0},{16,24},{24,16},{32,40},{40,32},{48,56},{56,48},{64,72... | collective-permute-start | bytes 786440 | tf_op jit(solution)/shard_map/ppermute | solution.py:370
  35.3 9.3 %collective-permute-start.5 = (f32[16,32,128]{2,1,0:T(8,128)S(1)}, f32[16,32,128]{2,1,0:T(8,128)S(1)}, u32[]{:S(2)}, u32[]{:S(2)}) collective-permute-start(f32[16,32,128]{2,1,0:T(8,128)S(1)} %level_4_0.1._.c_ref), channel_id=1, source_target_pairs={{0,64},{8,72},{16,80},{24,88},{32,96},{40,104},{48,112},{56,120},{... | collective-permute-start | bytes 786440 | tf_op jit(solution)/shard_map/ppermute | solution.py:370
  38.8 7.8 %collective-permute-start.12 = (f32[16,32,128]{2,1,0:T(8,128)S(1)}, f32[16,32,128]{2,1,0:T(8,128)S(1)}, u32[]{:S(2)}, u32[]{:S(2)}) collective-permute-start(f32[16,32,128]{2,1,0:T(8,128)S(1)} %level_2_32.1._.c_ref), channel_id=1, source_target_pairs={{0,16},{8,24},{16,0},{24,8},{32,48},{40,56},{48,32},{56,40},{64,80... | collective-permute-start | bytes 786440 | tf_op jit(solution)/shard_map/ppermute | solution.py:370
  40.7 8.2 %collective-permute-start.11 = (f32[16,32,128]{2,1,0:T(8,128)S(1)}, f32[16,32,128]{2,1,0:T(8,128)S(1)}, u32[]{:S(2)}, u32[]{:S(2)}) collective-permute-start(f32[16,32,128]{2,1,0:T(8,128)S(1)} %level_4_16.1._.c_ref), channel_id=1, source_target_pairs={{0,64},{8,72},{16,80},{24,88},{32,96},{40,104},{48,112},{56,120},{... | collective-permute-start | bytes 786440 | tf_op jit(solution)/shard_map/ppermute | solution.py:370
  44.4 7.6 %collective-permute-start.10 = (f32[16,32,128]{2,1,0:T(8,128)S(1)}, f32[16,32,128]{2,1,0:T(8,128)S(1)}, u32[]{:S(2)}, u32[]{:S(2)}) collective-permute-start(f32[16,32,128]{2,1,0:T(8,128)S(1)} %level_2_48.1._.c_ref), channel_id=1, source_target_pairs={{0,16},{8,24},{16,0},{24,8},{32,48},{40,56},{48,32},{56,40},{64,80... | collective-permute-start | bytes 786440 | tf_op jit(solution)/shard_map/ppermute | solution.py:370
  44.9 6.1 %copy-start = (f32[128,32,128]{2,1,0:T(8,128)S(1)}, f32[128,32,128]{2,1,0:T(8,128)}, u32[]{:S(2)}) copy-start(f32[128,32,128]{2,1,0:T(8,128)} %ti_ref.1) | copy-start | bytes 6291460
  44.9 10.9 %collective-permute-start.9 = (f32[16,32,128]{2,1,0:T(8,128)S(1)}, f32[16,32,128]{2,1,0:T(8,128)S(1)}, u32[]{:S(2)}, u32[]{:S(2)}) collective-permute-start(f32[16,32,128]{2,1,0:T(8,128)S(1)} %level_5_0.1._.c_ref), channel_id=1, source_target_pairs={{0,1},{1,0},{2,3},{3,2},{4,5},{5,4},{6,7},{7,6},{8,9},{9,8},{10,11... | collective-permute-start | bytes 786440 | tf_op jit(solution)/shard_map/ppermute | solution.py:370
  49.2 9.7 %collective-permute-start.16 = (f32[16,32,128]{2,1,0:T(8,128)S(1)}, f32[16,32,128]{2,1,0:T(8,128)S(1)}, u32[]{:S(2)}, u32[]{:S(2)}) collective-permute-start(f32[16,32,128]{2,1,0:T(8,128)S(1)} %level_5_16.1._.c_ref), channel_id=1, source_target_pairs={{0,1},{1,0},{2,3},{3,2},{4,5},{5,4},{6,7},{7,6},{8,9},{9,8},{10,11... | collective-permute-start | bytes 786440 | tf_op jit(solution)/shard_map/ppermute | solution.py:370
  50.8 9.7 %collective-permute-start.15 = (f32[16,32,128]{2,1,0:T(8,128)S(1)}, f32[16,32,128]{2,1,0:T(8,128)S(1)}, u32[]{:S(2)}, u32[]{:S(2)}) collective-permute-start(f32[16,32,128]{2,1,0:T(8,128)S(1)} %level_3_32.1._.c_ref), channel_id=1, source_target_pairs={{0,32},{8,40},{16,48},{24,56},{32,0},{40,8},{48,16},{56,24},{64,96... | collective-permute-start | bytes 786440 | tf_op jit(solution)/shard_map/ppermute | solution.py:370
  52.4 14.3 %collective-permute-start.14 = (f32[16,32,128]{2,1,0:T(8,128)S(1)}, f32[16,32,128]{2,1,0:T(8,128)S(1)}, u32[]{:S(2)}, u32[]{:S(2)}) collective-permute-start(f32[16,32,128]{2,1,0:T(8,128)S(1)} %level_3_48.1._.c_ref), channel_id=1, source_target_pairs={{0,32},{8,40},{16,48},{24,56},{32,0},{40,8},{48,16},{56,24},{64,96... | collective-permute-start | bytes 786440 | tf_op jit(solution)/shard_map/ppermute | solution.py:370
  56.1 11.4 %collective-permute-start.13 = (f32[16,32,128]{2,1,0:T(8,128)S(1)}, f32[16,32,128]{2,1,0:T(8,128)S(1)}, u32[]{:S(2)}, u32[]{:S(2)}) collective-permute-start(f32[16,32,128]{2,1,0:T(8,128)S(1)} %level_6_0.1._.c_ref), channel_id=1, source_target_pairs={{0,2},{1,3},{2,0},{3,1},{4,6},{5,7},{6,4},{7,5},{8,10},{9,11},{10,... | collective-permute-start | bytes 786440 | tf_op jit(solution)/shard_map/ppermute | solution.py:370
  60.8 9.6 %collective-permute-start.20 = (f32[16,32,128]{2,1,0:T(8,128)S(1)}, f32[16,32,128]{2,1,0:T(8,128)S(1)}, u32[]{:S(2)}, u32[]{:S(2)}) collective-permute-start(f32[16,32,128]{2,1,0:T(8,128)S(1)} %level_4_32.1._.c_ref), channel_id=1, source_target_pairs={{0,64},{8,72},{16,80},{24,88},{32,96},{40,104},{48,112},{56,120},{... | collective-permute-start | bytes 786440 | tf_op jit(solution)/shard_map/ppermute | solution.py:370
  63.9 10.7 %collective-permute-start.19 = (f32[16,32,128]{2,1,0:T(8,128)S(1)}, f32[16,32,128]{2,1,0:T(8,128)S(1)}, u32[]{:S(2)}, u32[]{:S(2)}) collective-permute-start(f32[16,32,128]{2,1,0:T(8,128)S(1)} %level_6_16.1._.c_ref), channel_id=1, source_target_pairs={{0,2},{1,3},{2,0},{3,1},{4,6},{5,7},{6,4},{7,5},{8,10},{9,11},{10,... | collective-permute-start | bytes 786440 | tf_op jit(solution)/shard_map/ppermute | solution.py:370
  67.0 9.8 %collective-permute-start.18 = (f32[16,32,128]{2,1,0:T(8,128)S(1)}, f32[16,32,128]{2,1,0:T(8,128)S(1)}, u32[]{:S(2)}, u32[]{:S(2)}) collective-permute-start(f32[16,32,128]{2,1,0:T(8,128)S(1)} %level_4_48.1._.c_ref), channel_id=1, source_target_pairs={{0,64},{8,72},{16,80},{24,88},{32,96},{40,104},{48,112},{56,120},{... | collective-permute-start | bytes 786440 | tf_op jit(solution)/shard_map/ppermute | solution.py:370
  70.7 9.3 %collective-permute-start.22 = (f32[16,32,128]{2,1,0:T(8,128)S(1)}, f32[16,32,128]{2,1,0:T(8,128)S(1)}, u32[]{:S(2)}, u32[]{:S(2)}) collective-permute-start(f32[16,32,128]{2,1,0:T(8,128)S(1)} %level_5_32.1._.c_ref), channel_id=1, source_target_pairs={{0,1},{1,0},{2,3},{3,2},{4,5},{5,4},{6,7},{7,6},{8,9},{9,8},{10,11... | collective-permute-start | bytes 786440 | tf_op jit(solution)/shard_map/ppermute | solution.py:370
  77.1 9.3 %collective-permute-start.21 = (f32[16,32,128]{2,1,0:T(8,128)S(1)}, f32[16,32,128]{2,1,0:T(8,128)S(1)}, u32[]{:S(2)}, u32[]{:S(2)}) collective-permute-start(f32[16,32,128]{2,1,0:T(8,128)S(1)} %level_5_48.1._.c_ref), channel_id=1, source_target_pairs={{0,1},{1,0},{2,3},{3,2},{4,5},{5,4},{6,7},{7,6},{8,9},{9,8},{10,11... | collective-permute-start | bytes 786440 | tf_op jit(solution)/shard_map/ppermute | solution.py:370
  77.2 10.9 %collective-permute-start.17 = (f32[16,32,128]{2,1,0:T(8,128)S(1)}, f32[16,32,128]{2,1,0:T(8,128)S(1)}, u32[]{:S(2)}, u32[]{:S(2)}) collective-permute-start(f32[16,32,128]{2,1,0:T(8,128)S(1)} %level_7_0.1._.c_ref), channel_id=1, source_target_pairs={{0,4},{1,5},{2,6},{3,7},{4,0},{5,1},{6,2},{7,3},{8,12},{9,13},{10,... | collective-permute-start | bytes 786440 | tf_op jit(solution)/shard_map/ppermute | solution.py:370
  80.3 10.1 %collective-permute-start.24 = (f32[16,32,128]{2,1,0:T(8,128)S(1)}, f32[16,32,128]{2,1,0:T(8,128)S(1)}, u32[]{:S(2)}, u32[]{:S(2)}) collective-permute-start(f32[16,32,128]{2,1,0:T(8,128)S(1)} %level_6_32.1._.c_ref), channel_id=1, source_target_pairs={{0,2},{1,3},{2,0},{3,1},{4,6},{5,7},{6,4},{7,5},{8,10},{9,11},{10,... | collective-permute-start | bytes 786440 | tf_op jit(solution)/shard_map/ppermute | solution.py:370
  82.4 9.1 %collective-permute-start.23 = (f32[16,32,128]{2,1,0:T(8,128)S(1)}, f32[16,32,128]{2,1,0:T(8,128)S(1)}, u32[]{:S(2)}, u32[]{:S(2)}) collective-permute-start(f32[16,32,128]{2,1,0:T(8,128)S(1)} %level_7_16.1._.c_ref), channel_id=1, source_target_pairs={{0,4},{1,5},{2,6},{3,7},{4,0},{5,1},{6,2},{7,3},{8,12},{9,13},{10,... | collective-permute-start | bytes 786440 | tf_op jit(solution)/shard_map/ppermute | solution.py:370
  86.6 8.0 %collective-permute-start.26 = (f32[16,32,128]{2,1,0:T(8,128)S(1)}, f32[16,32,128]{2,1,0:T(8,128)S(1)}, u32[]{:S(2)}, u32[]{:S(2)}) collective-permute-start(f32[16,32,128]{2,1,0:T(8,128)S(1)} %level_6_48.1._.c_ref), channel_id=1, source_target_pairs={{0,2},{1,3},{2,0},{3,1},{4,6},{5,7},{6,4},{7,5},{8,10},{9,11},{10,... | collective-permute-start | bytes 786440 | tf_op jit(solution)/shard_map/ppermute | solution.py:370
  90.7 6.7 %collective-permute-start.25 = (f32[16,32,128]{2,1,0:T(8,128)S(1)}, f32[16,32,128]{2,1,0:T(8,128)S(1)}, u32[]{:S(2)}, u32[]{:S(2)}) collective-permute-start(f32[16,32,128]{2,1,0:T(8,128)S(1)} %level_7_32.1._.c_ref), channel_id=1, source_target_pairs={{0,4},{1,5},{2,6},{3,7},{4,0},{5,1},{6,2},{7,3},{8,12},{9,13},{10,... | collective-permute-start | bytes 786440 | tf_op jit(solution)/shard_map/ppermute | solution.py:370
  94.9 6.5 %collective-permute-start.27 = (f32[16,32,128]{2,1,0:T(8,128)S(1)}, f32[16,32,128]{2,1,0:T(8,128)S(1)}, u32[]{:S(2)}, u32[]{:S(2)}) collective-permute-start(f32[16,32,128]{2,1,0:T(8,128)S(1)} %level_7_48.1._.c_ref), channel_id=1, source_target_pairs={{0,4},{1,5},{2,6},{3,7},{4,0},{5,1},{6,2},{7,3},{8,12},{9,13},{10,... | collective-permute-start | bytes 786440 | tf_op jit(solution)/shard_map/ppermute | solution.py:370
